TPU v7x, 256 devices: a whole 4x4x8 slice. The times are simulated.
256 devices in a mesh: snap: 4 (over x_hi, core), param: 64 (over x_lo, z, y).
Axes of the slice: x: 4 (x_hi: 2, x_lo: 2; x = x_hi * 2 + x_lo), y: 4, z: 8, core: 2. Of those that a mesh axis runs over, the one named last changes fastest.
Arguments:
- snap_in: float32 [32, 64, 1344], P('snap', None, 'param'), may hold values from -6 to 6
- snap_qkv: float32 [32, 1344, 4032], P('snap', 'param'), may hold values from -16 to 16
- snap_proj: float32 [32, 1344, 1344], P('snap', 'param'), may hold values from -16 to 16
- snap_out: float32 [32, 1344, 64], P('snap', 'param'), may hold values from -48 to 48
- coeffs: float32 [32, 8], P('snap'), may hold values from -3 to 3
- latent: float32 [64, 64, 256], P('param'), may hold values from -6 to 6
- levels: int32 [64], P('param'), may hold values from 0 to 15
Outputs:
- denoised: float32 [8, 64, 64, 256], P('snap', 'param')
All inputs are finite; a program needn't handle non-finite values.
Results may differ from a plain program's by a relative error of at most 0.012.
Values may be sent and summed in bfloat16 or wider, within the bound.
No kernel may reach another device: no remote copies, remote signals or barrier semaphores. Data moves between devices by JAX's collectives and lax.ppermute only.
A program may use at most 192 MiB of HBM per device.

v0:
```python
import jax
import jax.numpy as jnp
from jax import lax
from jax.sharding import PartitionSpec as P

HEAD_DIM = 64
PROF = 8
NLEV = 16


EPS = 0.0001


def noise_scales(levels):
    step = levels.astype(jnp.float32) / (NLEV - 1)
    sigma = jnp.exp(jnp.log(0.2) + step * (jnp.log(5.0) - jnp.log(0.2)))
    square = sigma * sigma + 0.25
    return (1.0 / jnp.sqrt(square), 0.25 / square, 0.5 * sigma / jnp.sqrt(square))


def to_tokens(image):
    count = image.shape[0]
    parts = image.reshape(count, 16, 4, 16, 4, 4).transpose(0, 1, 3, 2, 4, 5)
    return parts.reshape(count, 256, 64)


def from_tokens(feature):
    count = feature.shape[0]
    parts = feature.reshape(count, 16, 16, 4, 4, 4).transpose(0, 1, 3, 2, 4, 5)
    return parts.reshape(count, 64, 256)


def head_unit(values):
    scale = jnp.sqrt(jnp.mean(values * values, axis=-1, keepdims=True))
    return (values / (EPS + scale)).astype(jnp.bfloat16)


def contract(coeffs, snaps):
    return jnp.einsum("sp,sij->pij", coeffs, snaps, precision=lax.Precision.HIGHEST)


def squares(weights):
    return jnp.sum(weights * weights, axis=1)


def scaled(weights, sums):
    return (weights / (EPS + jnp.sqrt(sums))[:, None, :]).astype(jnp.bfloat16)


def denoise(tokens, w_in, qkv_product, proj_product, w_out):
    rows = tokens.shape[0]
    count = rows // 256
    width = w_in.shape[1]
    heads = width // HEAD_DIM
    hidden = jnp.dot(tokens, w_in, preferred_element_type=jnp.float32).astype(jnp.bfloat16)
    qkv = qkv_product(hidden)
    qkv = head_unit(qkv.reshape(count, 256, 3, heads, HEAD_DIM))
    query = qkv[:, :, 0]
    keys = qkv[:, :, 1]
    values = qkv[:, :, 2]
    scores = jnp.einsum("bqhd,bkhd->bhqk", query, keys, preferred_element_type=jnp.float32)
    scores = scores * (1.0 / jnp.sqrt(float(HEAD_DIM)))
    expo = jnp.exp(scores)
    weights = (expo / jnp.sum(expo, axis=-1, keepdims=True)).astype(jnp.bfloat16)
    attended = jnp.einsum("bhqk,bkhd->bqhd", weights, values, preferred_element_type=jnp.float32)
    attended = attended.astype(jnp.bfloat16).reshape(rows, width)
    projected = proj_product(attended)
    mixed = ((0.7 * hidden.astype(jnp.float32) + 0.3 * projected) / jnp.sqrt(0.58)).astype(
        jnp.bfloat16
    )
    return jnp.dot(mixed, w_out, preferred_element_type=jnp.float32)


def prepare(latent, levels):
    c_in, c_skip, c_out = noise_scales(levels)
    count = latent.shape[0]
    tokens = to_tokens(c_in[:, None, None] * latent).reshape(count * 256, 64).astype(jnp.bfloat16)
    return (tokens, c_skip, c_out)


def finish(feature, latent, c_skip, c_out):
    count = latent.shape[0]
    image = from_tokens(feature.reshape(count, 256, 64))
    return c_skip[:, None, None] * latent + c_out[:, None, None] * image


def plain_products(full_qkv, full_proj):

    def qkv_product(hidden):
        return jnp.dot(hidden, full_qkv, preferred_element_type=jnp.float32)

    def proj_product(attended):
        return jnp.dot(attended, full_proj, preferred_element_type=jnp.float32)

    return (qkv_product, proj_product)


def one_group_profile(unit_in, unit_qkv, unit_proj, unit_out, tokens, latent, c_skip, c_out):
    full_in, full_qkv, full_proj, full_out = (
        lax.all_gather(unit_in, "param", axis=1, tiled=True),
        lax.all_gather(unit_qkv, "param", axis=0, tiled=True),
        lax.all_gather(unit_proj, "param", axis=0, tiled=True),
        lax.all_gather(unit_out, "param", axis=0, tiled=True),
    )
    qkv_product, proj_product = plain_products(full_qkv, full_proj)
    feature = denoise(tokens, full_in, qkv_product, proj_product, full_out)
    return finish(feature, latent, c_skip, c_out)


def shards(snap_in, snap_qkv, snap_proj, snap_out, coeffs, latent, levels):
    owned = PROF // lax.axis_size("snap")
    part_in = contract(coeffs, snap_in)
    part_qkv = contract(coeffs, snap_qkv)
    part_proj = contract(coeffs, snap_proj)
    part_out = contract(coeffs, snap_out)
    summed = (
        lax.psum(part_in.astype(jnp.bfloat16), "snap").astype(jnp.float32),
        lax.psum(part_qkv.astype(jnp.bfloat16), "snap").astype(jnp.float32),
        lax.psum(part_proj.astype(jnp.bfloat16), "snap").astype(jnp.float32),
        lax.psum(part_out.astype(jnp.bfloat16), "snap").astype(jnp.float32),
    )
    first = lax.axis_index("snap") * owned
    prof_in, prof_qkv, prof_proj, prof_out = [
        lax.dynamic_slice_in_dim(item, first, owned, 0) for item in summed
    ]
    sums_qkv, sums_proj, sums_out = lax.psum(
        (squares(prof_qkv), squares(prof_proj), squares(prof_out)), "param"
    )
    unit_in = scaled(prof_in, squares(prof_in))
    unit_qkv = scaled(prof_qkv, sums_qkv)
    unit_proj = scaled(prof_proj, sums_proj)
    unit_out = scaled(prof_out, sums_out)
    tokens, c_skip, c_out = prepare(latent, levels)
    results = []
    for profile in range(owned):
        results.append(
            one_group_profile(
                unit_in[profile],
                unit_qkv[profile],
                unit_proj[profile],
                unit_out[profile],
                tokens,
                latent,
                c_skip,
                c_out,
            )
        )
    return jnp.stack(results)


def solution(mesh):
    in_specs = (
        P("snap", None, "param"),
        P("snap", "param", None),
        P("snap", "param", None),
        P("snap", "param", None),
        P("snap", None),
        P("param", None, None),
        P("param"),
    )
    out_specs = P("snap", "param", None, None)
    return jax.shard_map(shards, mesh=mesh, in_specs=in_specs, out_specs=out_specs, check_vma=False)
```

profile of v0, /device:TPU:8, one launch (start us, length us, event | category | flops | bytes accessed | tf_op | source)
XLA Modules:
  0.0 1694.0 jit_solution(575024128490017414)
XLA Ops:
  6.6 1.7 copy-done
  8.3 4.3 convolution_convert_fusion
  12.6 1.8 convolution_convert_fusion.3
  15.0 17.0 %all-reduce.1 = (bf16[8,64,21]{1,0,2:T(8,128)(2,1)S(1)}, bf16[8,21,64]{2,0,1:T(8,128)(2,1)S(1)}) all-reduce(bf16[8,64,21]{1,0,2:T(8,128)(2,1)S(1)} %convolution_convert_fusion.5, bf16[8,21,64]{2,0,1:T(8,128)(2,1)S(1)} %convolution_convert_fusion.4), channel_id=1, replica_groups=mesh['snap'=4,'param'=64] {'snap'}, use_global_device_ids=true, to_apply=%region_0.0 | all-reduce | flops 21504 | bytes 86016 | tf_op jit(solution)/shard_map/psum | solution.py:117
  32.1 45.6 %all-reduce.5.cloned.1.call-done = (bf16[8,21,4032]{2,0,1:T(8,128)(2,1)}, bf16[8,21,1344]{2,0,1:T(8,128)(2,1)}) async-done(((bf16[8,21,4032]{2,0,1:T(8,128)(2,1)}, bf16[8,21,1344]{2,0,1:T(8,128)(2,1)}), (bf16[8,21,4032]{2,0,1:T(8,128)(2,1)}, bf16[8,21,1344]{2,0,1:T(8,128)(2,1)})) %all-reduce.5.cloned.1.call-update) | async-done | bytes 1806352 | tf_op jit(solution)/shard_map/psum | solution.py:118
  77.7 1.9 fusion.55
  79.6 1.2 fusion.65
  80.9 302.3 %all-reduce = (f32[2,4032]{1,0:T(2,128)S(1)}, f32[2,1344]{1,0:T(2,128)S(1)}, f32[2,64]{1,0:T(2,128)S(1)}) all-reduce(f32[2,4032]{1,0:T(2,128)S(1)} %fusion.55, f32[2,1344]{1,0:T(2,128)S(1)} %fusion.65, f32[2,64]{1,0:T(2,128)S(1)} %fusion.73), channel_id=1, replica_groups=mesh['snap'=4,'param'=64] {'param'}, use_global_device_ids=true, to_apply=%region_4.0 | all-reduce | flops 10880 | bytes 87040 | tf_op jit(solution)/shard_map/psum | solution.py:126
  383.2 1.9 fusion.54
  385.1 1.6 fusion.86
  386.8 1.2 fusion.64
  390.6 162.2 %all-gather.4 = bf16[1,64,1344]{1,0,2:T(2,128)(2,1)S(1)} all-gather(bf16[1,64,21]{1,0,2:T(2,128)(2,1)S(1)} %get-tuple-element.21), channel_id=6, replica_groups=mesh['snap'=4,'param'=64] {'param'}, dimensions={2}, use_global_device_ids=true | all-gather | bytes 174720 | tf_op jit(solution)/shard_map/all_gather | solution.py:100
  554.5 1.2 convert_element_type.119
  555.7 2.0 copy.34
  558.0 154.6 %all-gather = bf16[1,64,1344]{1,0,2:T(2,128)(2,1)S(1)} all-gather(bf16[1,64,21]{1,0,2:T(2,128)(2,1)S(1)} %get-tuple-element.20), channel_id=2, replica_groups=mesh['snap'=4,'param'=64] {'param'}, dimensions={2}, use_global_device_ids=true | all-gather | bytes 174720 | tf_op jit(solution)/shard_map/all_gather | solution.py:100
  714.3 157.2 %all-gather.7 = bf16[1,1344,64]{2,0,1:T(2,128)(2,1)S(1)} all-gather(bf16[1,21,64]{2,0,1:T(2,128)(2,1)S(1)} %get-tuple-element.19), channel_id=9, replica_groups=mesh['snap'=4,'param'=64] {'param'}, dimensions={1}, use_global_device_ids=true | all-gather | bytes 174720 | tf_op jit(solution)/shard_map/all_gather | solution.py:103
  871.5 1.6 copy.45
  873.0 154.7 %all-gather.3 = bf16[1,1344,64]{2,0,1:T(2,128)(2,1)S(1)} all-gather(bf16[1,21,64]{2,0,1:T(2,128)(2,1)S(1)} %get-tuple-element.18), channel_id=5, replica_groups=mesh['snap'=4,'param'=64] {'param'}, dimensions={1}, use_global_device_ids=true | all-gather | bytes 174720 | tf_op jit(solution)/shard_map/all_gather | solution.py:103
  1027.8 1.6 copy.41
  1029.4 17.3 %fusion = f32[256,4032]{0,1:T(8,128)S(1)} fusion(bf16[256,1344]{0,1:T(8,128)(2,1)S(1)} %convolution_convert_fusion.1, bf16[1,1344,4032]{2,0,1:T(2,128)(2,1)} %all-gather.17.cloned.1.call-done), kind=kOutput, calls=%fused_computation | convolution fusion | flops 2774532096 | bytes 15654912 | tf_op jit(solution)/shard_map/dot_general | solution.py:90
  1049.2 2.0 fusion.40
  1051.2 5.2 fusion.48
  1056.7 2.0 copy.46
  1058.7 1.6 mul.171
  1060.3 304.9 %all-gather.13.cloned.1.call-done = bf16[1,1344,4032]{2,0,1:T(2,128)(2,1)} async-done(((bf16[1,21,4032]{2,0,1:T(2,128)(2,1)}), bf16[1,1344,4032]{2,0,1:T(2,128)(2,1)}) %all-gather.13.cloned.1.call-update) | async-done | bytes 10838032 | tf_op jit(solution)/shard_map/all_gather | solution.py:101
  1365.2 17.5 %fusion.3 = f32[256,4032]{0,1:T(8,128)S(1)} fusion(bf16[256,1344]{0,1:T(8,128)(2,1)S(1)} %convolution_convert_fusion.2, bf16[1,1344,4032]{2,0,1:T(2,128)(2,1)} %all-gather.13.cloned.1.call-done), kind=kOutput, calls=%fused_computation.3 | convolution fusion | flops 2774532096 | bytes 15654912 | tf_op jit(solution)/shard_map/dot_general | solution.py:90
  1384.1 1.2 fusion.6
  1385.3 1.9 fusion.41
  1387.2 286.3 %all-gather.15.cloned.1.call-done = bf16[1,1344,1344]{2,0,1:T(2,128)(2,1)} async-done(((bf16[1,21,1344]{2,0,1:T(2,128)(2,1)}), bf16[1,1344,1344]{2,0,1:T(2,128)(2,1)}) %all-gather.15.cloned.1.call-update) | async-done | bytes 3612688 | tf_op jit(solution)/shard_map/all_gather | solution.py:102
  1673.5 6.0 fusion.51
  1680.5 3.1 copy.42
  1683.7 2.6 mul.163
  (62 shorter events, 12.1 us)
Async XLA Ops:
  6.5 1.8 copy-start
  6.5 6.0 copy-start.8
  6.5 7.9 copy-start.6
  6.5 8.2 copy-start.7
  6.5 71.2 %all-reduce.5.cloned.1.call-start = ((), (), s32[]{:S(2)}) async-start(), calls=%async_computation.4 | async-start | bytes 3698688 | tf_op jit(solution)/shard_map/psum | solution.py:118
  8.3 4.3 copy-start.2
  14.3 539.2 %copy-start.5 = (f32[1,64,256]{2,1,0:T(8,128)S(1)}, f32[1,64,256]{2,1,0:T(8,128)}, u32[]{:S(2)}) copy-start(f32[1,64,256]{2,1,0:T(8,128)} %param.12) | copy-start | bytes 196612
  14.4 1015.0 %all-gather.17.cloned.1.call-start = ((), (), s32[]{:S(2)}) async-start(), calls=%async_computation.2 | async-start | bytes 22364160 | tf_op jit(solution)/shard_map/all_gather | solution.py:101
  386.7 664.5 %all-gather.19.cloned.1.call-start = ((), (), s32[]{:S(2)}) async-start(), calls=%async_computation.3 | async-start | bytes 7687680 | tf_op jit(solution)/shard_map/all_gather | solution.py:102
  388.9 976.3 %all-gather.13.cloned.1.call-start = ((), (), s32[]{:S(2)}) async-start(), calls=%async_computation | async-start | bytes 22364160 | tf_op jit(solution)/shard_map/all_gather | solution.py:101
  389.5 1284.0 %all-gather.15.cloned.1.call-start = ((), (), s32[]{:S(2)}) async-start(), calls=%async_computation.1 | async-start | bytes 7687680 | tf_op jit(solution)/shard_map/all_gather | solution.py:102
  1673.5 13.7 copy-start.1
  1679.4 6.9 copy-start.3
  1679.4 6.9 copy-start.4
Sparse Core Ops, SparseCore 0:
  14.5 63.2 all-reduce.4
  386.8 336.5 all-gather.16
  725.2 306.8 all-gather.18
  1033.7 331.4 all-gather.12
  1366.9 306.5 all-gather.14
where the time goes:
time: 1700 us; the launch traced here: 1690 us
  blocking collectives  948 us (56%)
  waiting for transfers between devices  637 us (37%)
  matrix products  59.7 us (4%)
  local copies, waits for them, and re-layouts  24.8 us (1%)
    all_gather x2, blocking collectives, one_group_profile(): lax.all_gather(unit_in, 'param', axis=1, tiled=True)  317 us
    all_gather x2, blocking collectives, one_group_profile(): lax.all_gather(unit_out, 'param', axis=0, tiled=True)  312 us
    all_gather x2, waiting for transfers between devices, one_group_profile(): lax.all_gather(unit_qkv, 'param', axis=0, tiled=True)  305 us
    psum x1, blocking collectives, shards(): lax.psum((squares(prof_qkv), squares(prof_proj), squares(prof_out)), 'par...  302 us
    all_gather x2, waiting for transfers between devices, one_group_profile(): lax.all_gather(unit_proj, 'param', axis=0, tiled=True)  286 us
    psum x1, waiting for transfers between devices, shards(): lax.psum(part_qkv.astype(jnp.bfloat16), 'snap').astype(jnp.float32)  45.6 us
    dot_general x2, matrix products, qkv_product(): return jnp.dot(hidden, full_qkv, preferred_element_type=jnp.float32)  34.8 us
  transfers between devices with their start and end apart: 5, of which 3 were waited for; matrix products, arithmetic and copies ran while one was open for 4% of the time, Pallas kernels for 0%

commit v1 on v0

v1 whole, which is shorter than its diff:
```python
import jax
import jax.numpy as jnp
from jax import lax
from jax.sharding import Mesh, PartitionSpec as P

HEAD_DIM = 64
PROF = 8
NLEV = 16
EPS = 0.0001

SNAP = ("xh", "core")
PARAM = ("xl", "z", "y")
ZY = ("z", "y")
X = ("xh", "xl")


def noise_scales(levels):
    step = levels.astype(jnp.float32) / (NLEV - 1)
    sigma = jnp.exp(jnp.log(0.2) + step * (jnp.log(5.0) - jnp.log(0.2)))
    square = sigma * sigma + 0.25
    return (1.0 / jnp.sqrt(square), 0.25 / square, 0.5 * sigma / jnp.sqrt(square))


def to_tokens(image):
    return image.reshape(16, 4, 16, 4, 4).transpose(0, 2, 1, 3, 4).reshape(256, 64)


def from_tokens(feature):
    count = feature.shape[0]
    parts = feature.reshape(count, 16, 16, 4, 4, 4).transpose(0, 1, 3, 2, 4, 5)
    return parts.reshape(count, 64, 256)


def a2a(x, axis):
    return lax.all_to_all(x, axis, 0, 0, tiled=True)


def natural(rows):
    rows = rows.reshape(32, 2, 24, 64)[:, :, :21]
    return rows.transpose(1, 0, 2, 3).reshape(1344, 64)


def shards(snap_in, snap_qkv, snap_proj, snap_out, coeffs, latent, levels):
    f32, bf16 = jnp.float32, jnp.bfloat16
    mix = coeffs.reshape(8, 2, 2, 2).transpose(2, 1, 3, 0).reshape(8, 8)
    eye = jnp.eye(24, 21, dtype=f32)
    mix = (mix[:, None, None, :] * eye[None, :, :, None]).reshape(192, 168)

    def contract(x):
        return jnp.dot(mix, x, precision=lax.Precision.HIGHEST).astype(bf16)

    w_q = contract(snap_qkv.transpose(1, 0, 2).reshape(168, 4032))
    w_p = contract(snap_proj.transpose(1, 0, 2).reshape(168, 1344))
    w_o = contract(snap_out.transpose(1, 0, 2).reshape(168, 64))
    w_i = contract(snap_in.transpose(2, 0, 1).reshape(168, 64))
    pad = jnp.zeros((192, 64), bf16)
    part = jnp.concatenate([w_q, pad, w_p, pad, w_i, w_o], axis=1)

    part = a2a(part.reshape(2, 96, 5632), "core").astype(f32)
    part = (part[0] + part[1]).astype(bf16)
    part = a2a(part.reshape(4, 24, 5632), X).astype(f32)
    part = part.reshape(2, 48, 5632)
    total = part[0] + part[1]
    q, p, wi, wo = total[:, :4096], total[:, 4096:5440], total[:, 5504:5568], total[:, 5568:]
    wi = wi / (EPS + jnp.sqrt(jnp.sum(wi * wi, axis=1, keepdims=True)))
    ww = jnp.concatenate([wi, wo], axis=1).astype(bf16)
    squares = jnp.pad(jnp.sum(p * p, axis=0), (0, 64)).reshape(11, 128)
    squares = jnp.pad(squares, ((0, 5), (0, 0))).astype(bf16)
    q = q.astype(bf16).reshape(48, 32, 128).transpose(1, 0, 2)
    same = jnp.concatenate([ww, squares], axis=0)
    send = jnp.concatenate([q, jnp.broadcast_to(same[None], (32, 64, 128))], axis=1)
    got = a2a(send, ZY)

    q = got[:, :48].reshape(1536, 128)
    wi = got[:, 48:96, :64].reshape(1536, 64)
    wo = natural(got[:, 48:96, 64:])
    qf = q.astype(f32)
    qn = 1.0 / (EPS + jnp.sqrt(jnp.sum(qf * qf, axis=0)))
    m = lax.dot_general(wi, q, (((0,), (0,)), ((), ())), preferred_element_type=f32) * qn
    of = wo.astype(f32)
    on = 1.0 / (EPS + jnp.sqrt(jnp.sum(of * of, axis=0)))
    squares = jnp.sum(got[:, 96:107].astype(f32), axis=0).reshape(1408)[:1344]
    p = (p / (EPS + jnp.sqrt(squares))).astype(bf16)
    r = jnp.dot(p, wo, preferred_element_type=f32) * on
    n = lax.dot_general(natural(got[:, 48:96, :64]), wo, (((0,), (0,)), ((), ())), preferred_element_type=f32) * on
    r = r.reshape(2, 24, 64).transpose(1, 0, 2).reshape(24, 128)
    send = jnp.concatenate([m, r], axis=0).astype(bf16)
    got = a2a(jnp.broadcast_to(send[None], (32, 88, 128)), ZY)
    m = got[:, :64].transpose(1, 0, 2).reshape(64, 4096)[:, :4032]
    r = natural(got[:, 64:].reshape(32, 24, 2, 64).transpose(0, 2, 1, 3))

    c_in, c_skip, c_out = noise_scales(levels)
    tokens = to_tokens(c_in[:, None, None] * latent).astype(bf16)
    tokens = lax.all_gather(tokens, "xl", axis=0, tiled=True)
    qkv = jnp.dot(tokens, m, preferred_element_type=f32).reshape(2, 256, 3, 21, 64)
    scale = jnp.sqrt(jnp.mean(qkv * qkv, axis=-1, keepdims=True))
    qkv = (qkv / (EPS + scale)).astype(bf16)
    query, keys, values = qkv[:, :, 0], qkv[:, :, 1], qkv[:, :, 2]
    scores = jnp.einsum("bqhd,bkhd->bhqk", query, keys, preferred_element_type=f32)
    expo = jnp.exp(scores * (1.0 / jnp.sqrt(float(HEAD_DIM))))
    weights = (expo / jnp.sum(expo, axis=-1, keepdims=True)).astype(bf16)
    attended = jnp.einsum("bhqk,bkhd->bqhd", weights, values, preferred_element_type=f32)
    attended = attended.astype(bf16).reshape(512, 1344)
    feature = 0.3 * jnp.dot(attended, r, preferred_element_type=f32)
    feature = feature + 0.7 * jnp.dot(tokens, n.astype(bf16), preferred_element_type=f32)
    feature = feature * (1.0 / jnp.sqrt(0.58))

    feature = a2a(feature.reshape(2, 256, 64), "xl")
    image = from_tokens(feature)
    out = c_skip[:, None, None] * latent + c_out[:, None, None] * image
    return out[:, None]


def solution(mesh):
    fine = Mesh(mesh.devices.reshape(2, 2, 2, 8, 4), ("xh", "core", "xl", "z", "y"))
    in_specs = (
        P(SNAP, None, PARAM),
        P(SNAP, PARAM, None),
        P(SNAP, PARAM, None),
        P(SNAP, PARAM, None),
        P(SNAP, None),
        P(PARAM, None, None),
        P(PARAM),
    )
    out_specs = P(SNAP, PARAM, None, None)
    return jax.shard_map(shards, mesh=fine, in_specs=in_specs, out_specs=out_specs, check_vma=False)
```

time: 1700 us -> 166 us (0.10)
  blocking collectives: 948 us -> 67 us
  waiting for transfers between devices: 637 us -> 14.7 us
  matrix products: 59.7 us -> 19.9 us
    all_gather x4 -> x1, blocking collectives: 629 us -> 4.58 us  [shards(): tokens = lax.all_gather(tokens, 'xl', axis=0, tiled=True)]
    all_gather x4 -> x0, waiting for transfers between devices: 591 us -> none  [the longest x2 305 us: one_group_profile(): lax.all_gather(unit_qkv, 'param', axis=0, tiled=True)]
    psum x2 -> x0, blocking collectives: 319 us -> none  [the longest x1 302 us: shards(): lax.psum((squares(prof_qkv), squares(prof_proj), squares(prof_out)), 'par...]
    all_to_all x0 -> x3, blocking collectives: none -> 62.4 us  [a2a(): return lax.all_to_all(x, axis, 0, 0, tiled=True)]
    psum x1 -> x0, waiting for transfers between devices: 45.6 us -> none  [shards(): lax.psum(part_qkv.astype(jnp.bfloat16), 'snap').astype(jnp.float32)]
    dot_general x14 -> x11, matrix products: 59.7 us -> 19.9 us  [the longest x4 8.75 us: contract(): return jnp.dot(mix, x, precision=lax.Precision.HIGHEST).astype(bf16)]
  transfers between devices with their start and end apart: 5 -> 2, of which waited for: 3 -> 2; matrix products, arithmetic and copies ran while one was open for 4% -> 2% of each run, Pallas kernels for 0% -> 0%
where the time goes in v1:
time: 166 us; the launch traced here: 165 us
  blocking collectives  67 us (40%)
  local copies, waits for them, and re-layouts  38 us (23%)
  matrix products  19.9 us (12%)
  other arithmetic  15.3 us (9%)
  waiting for transfers between devices  14.7 us (9%)
  starting transfers between devices  8.94 us (5%)
    all_to_all x3, blocking collectives, a2a(): return lax.all_to_all(x, axis, 0, 0, tiled=True)  62.4 us
    all_to_all x2, waiting for transfers between devices, a2a(): return lax.all_to_all(x, axis, 0, 0, tiled=True)  14.7 us
    mul x3, local copies, waits for them, and re-layouts, shards(): out = c_skip[:, None, None] * latent + c_out[:, None, None] * image  11 us
    reshape x1, local copies, waits for them, and re-layouts, shards(): jnp.dot(tokens, m, preferred_element_type=f32).reshape(2, 256, 3, 21, 64)  10.4 us
    all_to_all x2, starting transfers between devices, a2a(): return lax.all_to_all(x, axis, 0, 0, tiled=True)  8.94 us
    dot_general x4, matrix products, contract(): return jnp.dot(mix, x, precision=lax.Precision.HIGHEST).astype(bf16)  8.75 us
    reduce_sum x1, other arithmetic, shards(): scale = jnp.sqrt(jnp.mean(qkv * qkv, axis=-1, keepdims=True))  7.56 us
    convert_element_type x1, other arithmetic, shards(): qkv = (qkv / (EPS + scale)).astype(bf16)  4.64 us
  transfers between devices with their start and end apart: 2, of which 2 were waited for; matrix products, arithmetic and copies ran while one was open for 2% of the time, Pallas kernels for 0%

profile of v1, /device:TPU:8, one launch (start us, length us, event | category | flops | bytes accessed | tf_op | source)
XLA Modules:
  0.0 165.2 jit_solution(15831513101341045576)
XLA Ops:
  0.0 0.9 copy.75
  1.0 1.0 broadcast_multiply_fusion
  2.0 1.3 mul.172
  3.3 1.2 convolution_convert_fusion.2
  4.7 1.3 convolution_convert_fusion.3
  5.9 0.7 copy.78
  6.7 2.3 %convolution_convert_fusion.1 = bf16[192,1344]{1,0:T(8,128)(2,1)S(1)} fusion(f32[192,168]{0,1:T(8,128)S(1)} %mul.172, f32[8,21,1344]{2,0,1:T(8,128)} %param.9), kind=kOutput, calls=%fused_computation.9 | convolution fusion | flops 520482816 | bytes 1548288 | tf_op jit(solution)/shard_map/dot_general | solution.py:50
  9.0 3.9 %convolution_convert_fusion = bf16[192,4032]{1,0:T(8,128)(2,1)} fusion(f32[192,168]{0,1:T(8,128)S(1)} %mul.172, f32[8,21,4032]{2,0,1:T(8,128)S(1)} %copy-done), kind=kOutput, calls=%fused_computation.7 | convolution fusion | flops 1561448448 | bytes 4386816 | tf_op jit(solution)/shard_map/dot_general | solution.py:50
  12.9 4.4 %concatenate.23 = bf16[192,5632]{1,0:T(8,128)(2,1)} concatenate(bf16[192,4032]{1,0:T(8,128)(2,1)} %convolution_convert_fusion, bf16[192,64]{1,0:T(8,128)(2,1)S(1)} %broadcast_in_dim.6, bf16[192,1344]{1,0:T(8,128)(2,1)S(1)} %convolution_convert_fusion.1, bf16[192,64]{1,0:T(8,128)(2,1)S(1)} %broadcast_in_dim.6, bf16[192,64]{1,0:T(8,128)(2,1)} %copy.78, bf16[192,64]{1,0:T(8,128)(2,1)S(1)} %copy.79), dimensions={1} | concatenate | bytes 4325376 | tf_op jit(solution)/shard_map/concatenate | solution.py:57
  17.3 6.7 %all_to_all.25 = bf16[2,96,5632]{2,1,0:T(8,128)(2,1)S(1)} all-to-all(bf16[2,96,5632]{2,1,0:T(8,128)(2,1)} %bitcast.137), channel_id=1, replica_groups=mesh['xh'=2,'core'=2,'xl'=2,'z'=8,'y'=4] {'core'}, dimensions={0} | all-to-all | bytes 4325376 | tf_op jit(solution)/shard_map/all_to_all | solution.py:35
  24.7 19.8 %all_to_all.26 = bf16[4,24,5632]{2,1,0:T(8,128)(2,1)S(1)} all-to-all(bf16[4,24,5632]{2,1,0:T(8,128)(2,1)S(1)} %bitcast.144), channel_id=1, replica_groups=mesh['xh'=2,'core'=2,'xl'=2,'z'=8,'y'=4] {'xh','xl'}, dimensions={0} | all-to-all | bytes 2162688 | tf_op jit(solution)/shard_map/all_to_all | solution.py:35
  45.6 35.9 %all_to_all.27 = bf16[32,112,128]{2,1,0:T(8,128)(2,1)S(1)} all-to-all(bf16[32,112,128]{2,1,0:T(8,128)(2,1)S(1)} %pad_maximum_fusion), channel_id=1, replica_groups=mesh['xh'=2,'core'=2,'xl'=2,'z'=8,'y'=4] {'z','y'}, dimensions={0} | all-to-all | bytes 1835008 | tf_op jit(solution)/shard_map/all_to_all | solution.py:35
  82.4 1.1 fusion.14
  83.9 0.9 broadcast_in_dim.8
  84.9 5.6 %all-to-all-start.3 = ((bf16[32,88,128]{2,1,0:T(8,128)(2,1)}), bf16[32,88,128]{2,1,0:T(8,128)(2,1)S(1)}, u32[]{:S(2)}, u32[]{:S(2)}) async-start(bf16[32,88,128]{2,1,0:T(8,128)(2,1)} %broadcast_in_dim.8), calls=%async_computation.3 | async-start | bytes 1441792 | tf_op jit(solution)/shard_map/all_to_all | solution.py:35
  91.4 1.2 convert_element_type.90
  92.6 2.0 %copy.74 = bf16[16,16,4,4,4]{1,0,4,3,2:T(8,128)(2,1)S(1)} copy(bf16[16,16,4,4,4]{2,0,4,3,1:T(8,128)(2,1)S(1)} %bitcast.146) | data formatting | bytes 65536 | tf_op jit(solution)/shard_map/convert_element_type | solution.py:93
  94.9 4.6 %all_gather.3 = bf16[512,64]{0,1:T(8,128)(2,1)S(1)} all-gather(bf16[256,64]{0,1:T(8,128)(2,1)S(1)} %convert_element_type.92), channel_id=1, replica_groups=mesh['xh'=2,'core'=2,'xl'=2,'z'=8,'y'=4] {'xl'}, dimensions={0}, use_global_device_ids=true | all-gather | bytes 98304 | tf_op jit(solution)/shard_map/all_gather | solution.py:94
  99.9 10.4 %all-to-all-done.3 = bf16[32,88,128]{2,1,0:T(8,128)(2,1)S(1)} async-done(((bf16[32,88,128]{2,1,0:T(8,128)(2,1)}), bf16[32,88,128]{2,1,0:T(8,128)(2,1)S(1)}, u32[]{:S(2)}, u32[]{:S(2)}) %all-to-all-start.3) | async-done | bytes 720928 | tf_op jit(solution)/shard_map/all_to_all | solution.py:35
  111.0 4.4 %fusion.16 = f32[512,4032]{0,1:T(8,128)} fusion(bf16[512,64]{0,1:T(8,128)(2,1)S(1)} %all_gather.3, bf16[64,4096]{1,0:T(8,128)(2,1)S(1)} %copy_bitcast_fusion), kind=kOutput, calls=%fused_computation.38 | convolution fusion | flops 264241152 | bytes 8847360 | tf_op jit(solution)/shard_map/dot_general | solution.py:95
  115.4 10.4 %reshape.195 = f32[2,256,3,21,64]{1,0,4,3,2:T(2,128)} reshape(f32[512,4032]{0,1:T(8,128)} %fusion.16) | data formatting | bytes 16515072 | tf_op jit(solution)/shard_map/reshape | solution.py:95
  125.8 7.6 %multiply_reduce_fusion = f32[2,256,3,21]{1,0,3,2:T(2,128)S(1)} fusion(f32[2,256,3,21,64]{1,0,4,3,2:T(2,128)} %reshape.195), kind=kLoop, calls=%fused_computation.5 | loop fusion | flops 4096512 | bytes 8386560 | tf_op jit(solution)/shard_map/reduce_sum | solution.py:96
  133.6 4.6 %fusion.1 = bf16[2,256,3,21,64]{1,4,3,0,2:T(8,128)(2,1)S(1)} fusion(f32[2,256,3,21,64]{1,0,4,3,2:T(2,128)} %reshape.195, f32[2,256,3,21]{1,3,0,2:T(8,128)S(1)} %copy.84), kind=kLoop, calls=%fused_computation.4 | loop fusion | flops 4128768 | bytes 12515328 | tf_op jit(solution)/shard_map/convert_element_type | solution.py:97
  138.2 2.3 %fusion = (f32[2,21,256]{2,1,0:T(8,128)S(1)}, f32[2,21,256,256]{2,3,1,0:T(8,128)S(1)}) fusion(bf16[2,256,3,21,64]{1,4,3,0,2:T(8,128)(2,1)S(1)} %fusion.1), kind=kOutput, calls=%fused_computation.2 | convolution fusion | flops 357815808 | bytes 13805568 | tf_op jit(solution)/shard_map/bqhd,bkhd->bhqk/dot_general | solution.py:99
  140.5 2.2 %fusion.6 = bf16[2,256,21,64]{1,3,2,0:T(8,128)(2,1)S(1)} fusion(f32[2,21,256,256]{2,3,1,0:T(8,128)S(1)} %get-tuple-element.10, f32[2,21,256]{2,1,0:T(8,128)S(1)} %get-tuple-element.9, bf16[2,256,3,21,64]{1,4,3,0,2:T(8,128)(2,1)S(1)} %fusion.1), kind=kOutput, calls=%fused_computation.13 | convolution fusion | flops 361267200 | bytes 13811712 | tf_op jit(solution)/shard_map/bhqk,bkhd->bqhd/dot_general | solution.py:102
  142.7 1.4 copy.87
  145.5 3.4 %all-to-all-start.4 = ((f32[2,256,64]{1,2,0:T(8,128)}), f32[2,256,64]{1,2,0:T(8,128)S(1)}, u32[]{:S(2)}, u32[]{:S(2)}) async-start(f32[2,256,64]{1,2,0:T(8,128)} %bitcast.135), calls=%async_computation.4 | async-start | bytes 262144 | tf_op jit(solution)/shard_map/all_to_all | solution.py:35
  149.0 4.3 %all-to-all-done.4 = f32[2,256,64]{1,2,0:T(8,128)S(1)} async-done(((f32[2,256,64]{1,2,0:T(8,128)}), f32[2,256,64]{1,2,0:T(8,128)S(1)}, u32[]{:S(2)}, u32[]{:S(2)}) %all-to-all-start.4) | async-done | bytes 131104 | tf_op jit(solution)/shard_map/all_to_all | solution.py:35
  153.4 1.3 mul.193
  154.7 6.0 %copy.91 = f32[2,16,4,16,4,4]{2,1,5,4,3,0:T(8,128)} copy(f32[2,16,4,16,4,4]{3,1,5,4,2,0:T(8,128)} %bitcast.145) | data formatting | bytes 262144 | tf_op jit(solution)/shard_map/mul | solution.py:110
  160.7 3.6 %mul.195 = f32[2,1,64,256]{2,3,0,1:T(8,128)S(1)} reshape(f32[2,16,4,16,4,4]{2,1,5,4,3,0:T(8,128)} %copy.91) | data formatting | bytes 262144 | tf_op jit(solution)/shard_map/mul | solution.py:110
  164.4 0.8 copy.92
  (59 shorter events, 6.3 us)
Async XLA Ops:
  0.0 9.0 %copy-start = (f32[8,21,4032]{2,0,1:T(8,128)S(1)}, f32[8,21,4032]{2,0,1:T(8,128)}, u32[]{:S(2)}) copy-start(f32[8,21,4032]{2,0,1:T(8,128)} %param.8) | copy-start | bytes 8128516
  44.8 36.7 %copy-start.2 = (f32[2,24,5632]{2,1,0:T(8,128)}, f32[2,24,5632]{2,1,0:T(8,128)S(1)}, u32[]{:S(2)}) copy-start(f32[2,24,5632]{2,1,0:T(8,128)S(1)} %slice_add_fusion.1) | copy-start | bytes 3244036
  82.2 9.1 %copy-start.3 = (f32[1,64,256]{2,1,0:T(8,128)S(1)}, f32[1,64,256]{2,1,0:T(8,128)}, u32[]{:S(2)}) copy-start(f32[1,64,256]{2,1,0:T(8,128)} %param.12) | copy-start | bytes 196612
  84.9 25.4 %all-to-all-start.3 = ((bf16[32,88,128]{2,1,0:T(8,128)(2,1)}), bf16[32,88,128]{2,1,0:T(8,128)(2,1)S(1)}, u32[]{:S(2)}, u32[]{:S(2)}) async-start(bf16[32,88,128]{2,1,0:T(8,128)(2,1)} %broadcast_in_dim.8), calls=%async_computation.3 | async-start | bytes 1441792 | tf_op jit(solution)/shard_map/all_to_all | solution.py:35
  145.5 7.8 %all-to-all-start.4 = ((f32[2,256,64]{1,2,0:T(8,128)}), f32[2,256,64]{1,2,0:T(8,128)S(1)}, u32[]{:S(2)}, u32[]{:S(2)}) async-start(f32[2,256,64]{1,2,0:T(8,128)} %bitcast.135), calls=%async_computation.4 | async-start | bytes 262144 | tf_op jit(solution)/shard_map/all_to_all | solution.py:35
  154.7 10.5 %copy-start.1 = (f32[8,21,4032]{2,0,1:T(8,128)S(1)}, f32[8,21,4032]{2,0,1:T(8,128)}, u32[]{:S(2)}) copy-start(f32[8,21,4032]{2,0,1:T(8,128)} %param.8) | copy-start | bytes 8128516

commit v2 on v1

v2 whole, which is shorter than its diff:
```python
import jax
import jax.numpy as jnp
from jax import lax
from jax.experimental import pallas as pl
from jax.experimental.pallas import tpu as pltpu
from jax.sharding import Mesh, PartitionSpec as P

HEAD_DIM = 64
PROF = 8
NLEV = 16
EPS = 0.0001
LOG2E = 1.4426950408889634

SNAP = ("xh", "core")
PARAM = ("xl", "z", "y")
ZY = ("z", "y")
X = ("xh", "xl")
F32 = jnp.float32
BF16 = jnp.bfloat16
TN = (((0,), (0,)), ((), ()))


def noise_scales(levels):
    step = levels.astype(jnp.float32) / (NLEV - 1)
    sigma = jnp.exp(jnp.log(0.2) + step * (jnp.log(5.0) - jnp.log(0.2)))
    square = sigma * sigma + 0.25
    return (1.0 / jnp.sqrt(square), 0.25 / square, 0.5 * sigma / jnp.sqrt(square))


def a2a(x, axis):
    return lax.all_to_all(x, axis, 0, 0, tiled=True)


def contract_kernel(c_ref, q_ref, p_ref, i_ref, o_ref, out_ref):
    snap = lax.broadcasted_iota(jnp.int32, (8, 168), 0)
    col = lax.broadcasted_iota(jnp.int32, (8, 168), 1)
    pick = jnp.where(lax.rem(col, 8) == snap, 1.0, 0.0)
    rows = lax.dot_general(c_ref[...], pick, TN, precision=lax.Precision.HIGHEST,
                           preferred_element_type=F32)
    r = lax.broadcasted_iota(jnp.int32, (24, 168), 0)
    col = lax.broadcasted_iota(jnp.int32, (24, 168), 1)
    same = jnp.where(col // 8 == r, 1.0, 0.0)
    mix = jnp.concatenate([rows[p:p + 1] * same for p in range(8)], axis=0)
    mix_hi = mix.astype(BF16)
    mix_lo = (mix - mix_hi.astype(F32)).astype(BF16)

    def piece(ref, start, width, at):
        x = ref[:, start:start + width]
        hi = x.astype(BF16)
        lo = (x - hi.astype(F32)).astype(BF16)
        y = jnp.dot(mix_hi, hi, preferred_element_type=F32)
        y = y + jnp.dot(mix_hi, lo, preferred_element_type=F32)
        y = y + jnp.dot(mix_lo, hi, preferred_element_type=F32)
        y = y.astype(BF16)
        for p in range(8):
            core, slot = (p // 2) % 2, (p // 4) * 2 + p % 2
            out_ref[core, slot * 24:slot * 24 + 24, at:at + width] = y[p * 24:p * 24 + 24]

    for k in range(7):
        piece(q_ref, 512 * k, 512, 512 * k)
    piece(q_ref, 3584, 448, 3584)
    for k in range(2):
        piece(p_ref, 512 * k, 512, 4096 + 512 * k)
    piece(p_ref, 1024, 320, 5120)
    piece(i_ref, 0, 64, 5504)
    piece(o_ref, 0, 64, 5568)
    out_ref[:, :, 4032:4096] = jnp.zeros((2, 96, 64), BF16)
    out_ref[:, :, 5440:5504] = jnp.zeros((2, 96, 64), BF16)


def contract(coeffs, q, p, w_in, w_out):
    return pl.pallas_call(
        contract_kernel,
        out_shape=jax.ShapeDtypeStruct((2, 96, 5632), BF16),
        name="contract",
        cost_estimate=pl.CostEstimate(flops=3 * 2 * 192 * 168 * 5504, bytes_accessed=6000000,
                                      transcendentals=0),
    )(coeffs, q, p, w_in, w_out)


def attend_kernel(t_ref, b_ref, r_ref, n_ref, o_ref, s_ref, a_ref, z_ref):
    tokens = jnp.concatenate([t_ref[0], t_ref[1]], axis=1)

    def project(c, carry):
        x = lax.dot_general(b_ref[c, 0:64, :], tokens, TN, preferred_element_type=F32)
        x = x.reshape(2, 64, 512)
        scale = jnp.sqrt(jnp.sum(x * x, axis=1, keepdims=True) * (1.0 / 64))
        s_ref[pl.ds(2 * c, 2)] = (x * (1.0 / (EPS + scale))).astype(BF16)
        return carry

    lax.fori_loop(0, 32, project, 0, unroll=4)

    def head(h, carry):
        for b in range(2):
            at = slice(256 * b, 256 * b + 256)
            query, keys, values = s_ref[h, :, at], s_ref[21 + h, :, at], s_ref[42 + h, :, at]
            scores = lax.dot_general(keys, query, TN, preferred_element_type=F32)
            expo = jnp.exp2(scores * (0.125 * LOG2E))
            total = jnp.sum(expo, axis=0, keepdims=True)
            out = jnp.dot(values, expo.astype(BF16), preferred_element_type=F32)
            a_ref[pl.ds(pl.multiple_of(h * 64, 64), 64), at] = (out * (1.0 / total)).astype(BF16)
        return carry

    lax.fori_loop(0, 21, head, 0, unroll=3)

    feature = 0.3 * lax.dot_general(r_ref[...], a_ref[...], TN, preferred_element_type=F32)
    feature = feature + 0.7 * lax.dot_general(n_ref[...], tokens, TN, preferred_element_type=F32)
    feature = feature * (1.0 / (0.58 ** 0.5))
    token = lax.broadcasted_iota(jnp.int32, (256, 256), 0)
    lane = lax.broadcasted_iota(jnp.int32, (256, 256), 1)
    keep = lax.rem(token, 16) == lane // 16
    row = lax.broadcasted_iota(jnp.int32, (128, 256), 0)
    lane = lax.broadcasted_iota(jnp.int32, (128, 256), 1)
    for b in range(2):
        part = feature[:, 256 * b:256 * b + 256]
        hi = part.astype(BF16)
        lo = (part - hi.astype(F32)).astype(BF16)
        both = jnp.concatenate([hi, lo], axis=0)
        for i in range(4):
            tile = jnp.where(lax.rem(row, 64) == 16 * i + lax.rem(lane, 16), 1.0, 0.0).astype(BF16)
            wide = lax.dot_general(both, tile, TN, preferred_element_type=F32)
            wide = jnp.where(keep, wide, 0.0).reshape(16, 16, 256)
            wide = jnp.sum(wide, axis=1)
            z_ref[2 * b, pl.ds(i, 16, stride=4), :] = wide[:, :128]
            z_ref[2 * b + 1, pl.ds(i, 16, stride=4), :] = wide[:, 128:]
        o_ref[b] = jnp.concatenate([z_ref[2 * b], z_ref[2 * b + 1]], axis=1)


def attend(tokens, got, r, n):
    return pl.pallas_call(
        attend_kernel,
        out_shape=jax.ShapeDtypeStruct((2, 64, 256), F32),
        scratch_shapes=[pltpu.VMEM((64, 64, 512), BF16), pltpu.VMEM((1344, 512), BF16),
                        pltpu.VMEM((4, 64, 128), F32)],
        name="attend",
        cost_estimate=pl.CostEstimate(flops=1000000000, bytes_accessed=1200000, transcendentals=2800000),
    )(tokens, got, r, n)


def natural(rows):
    return rows.reshape(32, 2, 21, 64).transpose(1, 0, 2, 3).reshape(1344, 64)


def shards(snap_in, snap_qkv, snap_proj, snap_out, coeffs, latent, levels):
    part = contract(
        coeffs,
        snap_qkv.transpose(1, 0, 2).reshape(168, 4032),
        snap_proj.transpose(1, 0, 2).reshape(168, 1344),
        snap_in.transpose(2, 0, 1).reshape(168, 64),
        snap_out.transpose(1, 0, 2).reshape(168, 64),
    )
    part = a2a(part, "core").astype(F32)
    part = (part[0] + part[1]).astype(BF16)
    part = a2a(part.reshape(4, 24, 5632), X).astype(F32)
    part = part.reshape(2, 2, 24, 5632)
    total = (part[0] + part[1])[:, :21].reshape(42, 5632)
    q, p, wi, wo = total[:, :4096], total[:, 4096:5440], total[:, 5504:5568], total[:, 5568:]
    wi = wi / (EPS + jnp.sqrt(jnp.sum(wi * wi, axis=1, keepdims=True)))
    ww = jnp.concatenate([wi, wo], axis=1)
    squares = jnp.pad(jnp.sum(p * p, axis=0), (0, 64)).reshape(11, 128)
    q = q.reshape(42, 32, 128).transpose(1, 0, 2)
    same = jnp.concatenate([ww, squares, jnp.zeros((1, 128), F32)], axis=0)
    send = jnp.concatenate([q, jnp.broadcast_to(same[None], (32, 54, 128))], axis=1).astype(BF16)
    got = a2a(send, ZY)

    q = got[:, :42].reshape(1344, 128)
    wi = got[:, 42:84, :64].reshape(1344, 64)
    wo = got[:, 42:84, 64:].reshape(1344, 64)
    qf = q.astype(F32)
    qn = 1.0 / (EPS + jnp.sqrt(jnp.sum(qf * qf, axis=0)))
    m = lax.dot_general(wi, q, TN, preferred_element_type=F32) * qn
    of = wo.astype(F32)
    on = 1.0 / (EPS + jnp.sqrt(jnp.sum(of * of, axis=0)))
    squares = jnp.sum(got[:, 84:95].astype(F32), axis=0).reshape(1408)[:1344]
    p = (p / (EPS + jnp.sqrt(squares))).astype(BF16)
    r = jnp.dot(p, natural(wo), preferred_element_type=F32) * on
    n = lax.dot_general(wi, wo, TN, preferred_element_type=F32) * on
    r = jnp.pad(r.reshape(2, 21, 64), ((0, 0), (0, 3), (0, 0)))
    r = jnp.concatenate([r[0], r[1]], axis=1)
    send = jnp.concatenate([m, r], axis=0).astype(BF16)
    got = a2a(jnp.broadcast_to(send[None], (32, 88, 128)), ZY)
    r = got[:, 64:85]
    r = jnp.concatenate([r[:, :, :64], r[:, :, 64:]], axis=0).reshape(1344, 64)

    c_in, c_skip, c_out = noise_scales(levels)
    tokens = (c_in[:, None, None] * latent).astype(BF16)
    tokens = tokens.reshape(16, 4, 16, 16).transpose(1, 3, 0, 2).reshape(1, 64, 256)
    tokens = lax.all_gather(tokens, "xl", axis=0, tiled=True)
    feature = a2a(attend(tokens, got, r, n.astype(BF16)), "xl")
    out = c_skip[:, None, None] * latent + c_out[:, None, None] * feature
    return out[:, None]


def solution(mesh):
    fine = Mesh(mesh.devices.reshape(2, 2, 2, 8, 4), ("xh", "core", "xl", "z", "y"))
    in_specs = (
        P(SNAP, None, PARAM),
        P(SNAP, PARAM, None),
        P(SNAP, PARAM, None),
        P(SNAP, PARAM, None),
        P(SNAP, None),
        P(PARAM, None, None),
        P(PARAM),
    )
    out_specs = P(SNAP, PARAM, None, None)
    return jax.shard_map(shards, mesh=fine, in_specs=in_specs, out_specs=out_specs, check_vma=False)
```

time: 166 us -> 123 us (0.74)
  local copies, waits for them, and re-layouts: 38 us -> 4 us
  blocking collectives: 67 us -> 44.5 us
  Pallas kernels: 0 us -> 21.6 us
  matrix products: 19.9 us -> 1.51 us
  waiting for transfers between devices: 14.7 us -> 32.7 us
  other arithmetic: 15.3 us -> 3.74 us
  starting transfers between devices: 8.94 us -> 13.2 us
    all_to_all x3 -> x2, blocking collectives: 62.4 us -> 39.8 us  [a2a(): return lax.all_to_all(x, axis, 0, 0, tiled=True)]
    pallas_call x0 -> x2, Pallas kernels: none -> 21.6 us  [the longest x1 16 us: attend(): pl.pallas_call(attend_kernel, out_shape=jax.ShapeDtypeStruct((2, 64, 256)...]
    dot_general x11 -> x3, matrix products: 19.9 us -> 1.51 us  [the longest x1 1.03 us: shards(): n = lax.dot_general(wi, wo, TN, preferred_element_type=F32) * on]
    all_to_all x2 -> x3, waiting for transfers between devices: 14.7 us -> 32.7 us  [a2a(): return lax.all_to_all(x, axis, 0, 0, tiled=True)]
    mul x5 -> x0, local copies, waits for them, and re-layouts: 12.4 us -> none  [the longest x3 11 us: shards(): out = c_skip[:, None, None] * latent + c_out[:, None, None] * image]
    reshape x7 -> x9, local copies, waits for them, and re-layouts: 11.6 us -> 2.02 us  [the longest x1 0.87 us: shards(): r = jnp.concatenate([r[:, :, :64], r[:, :, 64:]], axis=0).reshape(1344, 64)]
    reduce_sum x2 -> x1, other arithmetic: 7.6 us -> 0.06 us  [shards(): squares = jnp.sum(got[:, 84:95].astype(F32), axis=0).reshape(1408)[:1344]]
    convert_element_type x7 -> x0, local copies, waits for them, and re-layouts: 5.79 us -> none  [the longest x4 3.52 us: shards(): tokens = to_tokens(c_in[:, None, None] * latent).astype(bf16)]
  transfers between devices with their start and end apart: 2 -> 3, of which waited for: 2 -> 3; matrix products, arithmetic and copies ran while one was open for 2% -> 2% of each run, Pallas kernels for 0% -> 0%
where the time goes in v2:
time: 123 us; the launch traced here: 122 us
  blocking collectives  44.5 us (36%)
  waiting for transfers between devices  32.7 us (27%)
  Pallas kernels  21.6 us (18%)
  starting transfers between devices  13.2 us (11%)
  local copies, waits for them, and re-layouts  4 us (3%)
  other arithmetic  3.74 us (3%)
  matrix products  1.51 us (1%)
    all_to_all x2, blocking collectives, a2a(): return lax.all_to_all(x, axis, 0, 0, tiled=True)  39.8 us
    all_to_all x3, waiting for transfers between devices, a2a(): return lax.all_to_all(x, axis, 0, 0, tiled=True)  32.7 us
    pallas_call x1, Pallas kernels, attend(): pl.pallas_call(attend_kernel, out_shape=jax.ShapeDtypeStruct((2, 64, 256)...  16 us
    all_to_all x3, starting transfers between devices, a2a(): return lax.all_to_all(x, axis, 0, 0, tiled=True)  13.2 us
    pallas_call x1, Pallas kernels, contract(): pl.pallas_call(contract_kernel, out_shape=jax.ShapeDtypeStruct((2, 96, 56...  5.69 us
    all_gather x1, blocking collectives, shards(): tokens = lax.all_gather(tokens, 'xl', axis=0, tiled=True)  4.69 us
  transfers between devices with their start and end apart: 3, of which 3 were waited for; matrix products, arithmetic and copies ran while one was open for 2% of the time, Pallas kernels for 0%

profile of v2, /device:TPU:8, one launch (start us, length us, event | category | flops | bytes accessed | tf_op | source)
XLA Modules:
  0.0 122.4 jit_solution(6563997836497834227)
XLA Ops:
  0.0 5.7 %contract.1 = bf16[2,96,5632]{2,1,0:T(8,128)(2,1)} custom-call(f32[8,8]{1,0:T(8,128)} %c_ref.1, f32[168,4032]{1,0:T(8,128)} %bitcast.55, f32[168,1344]{1,0:T(8,128)} %bitcast.61, f32[168,64]{1,0:T(8,128)} %bitcast.62, f32[168,64]{1,0:T(8,128)} %bitcast.63), custom_call_target="tpu_custom_call" | custom-call | flops 1065222144 | bytes 6000000 | tf_op jit(solution)/shard_map/contract/pallas_call | solution.py:72
  5.7 6.7 %all_to_all.25 = bf16[2,96,5632]{2,1,0:T(8,128)(2,1)S(1)} all-to-all(bf16[2,96,5632]{2,1,0:T(8,128)(2,1)} %contract.1), channel_id=1, replica_groups=mesh['xh'=2,'core'=2,'xl'=2,'z'=8,'y'=4] {'core'}, dimensions={0} | all-to-all | bytes 4325376 | tf_op jit(solution)/shard_map/all_to_all | solution.py:31
  12.4 0.5 convert_element_type.48
  12.8 1.2 fusion
  14.0 4.3 %all-to-all-start.1 = ((bf16[4,24,5632]{2,1,0:T(8,128)(2,1)}), bf16[4,24,5632]{2,1,0:T(8,128)(2,1)S(1)}, u32[]{:S(2)}, u32[]{:S(2)}) async-start(bf16[4,24,5632]{2,1,0:T(8,128)(2,1)} %bitcast.13), calls=%async_computation.1 | async-start | bytes 2162688 | tf_op jit(solution)/shard_map/all_to_all | solution.py:31
  18.4 15.7 %all-to-all-done.1 = bf16[4,24,5632]{2,1,0:T(8,128)(2,1)S(1)} async-done(((bf16[4,24,5632]{2,1,0:T(8,128)(2,1)}), bf16[4,24,5632]{2,1,0:T(8,128)(2,1)S(1)}, u32[]{:S(2)}, u32[]{:S(2)}) %all-to-all-start.1) | async-done | bytes 1081376 | tf_op jit(solution)/shard_map/all_to_all | solution.py:31
  34.1 0.2 fusion.11
  34.3 0.1 slice_add_fusion.1
  34.9 0.1 copy.22
  35.2 0.2 pad_maximum_fusion
  35.4 33.1 %all_to_all.26 = bf16[32,96,128]{2,1,0:T(8,128)(2,1)S(1)} all-to-all(bf16[32,96,128]{2,1,0:T(8,128)(2,1)S(1)} %pad_maximum_fusion), channel_id=1, replica_groups=mesh['xh'=2,'core'=2,'xl'=2,'z'=8,'y'=4] {'z','y'}, dimensions={0} | all-to-all | bytes 1572864 | tf_op jit(solution)/shard_map/all_to_all | solution.py:31
  68.5 0.3 multiply_reduce_fusion
  68.8 0.2 slice.94
  69.2 0.1 copy.18
  69.3 0.1 reshape.103
  69.5 0.2 convolution_multiply_fusion
  69.8 0.2 multiply_reduce_fusion.1
  70.0 0.3 fusion.3
  70.4 1.0 broadcast_in_dim.10
  71.3 5.6 %all-to-all-start.3 = ((bf16[32,88,128]{2,1,0:T(8,128)(2,1)}), bf16[32,88,128]{2,1,0:T(8,128)(2,1)S(1)}, u32[]{:S(2)}, u32[]{:S(2)}) async-start(bf16[32,88,128]{2,1,0:T(8,128)(2,1)} %broadcast_in_dim.10), calls=%async_computation.3 | async-start | bytes 1441792 | tf_op jit(solution)/shard_map/all_to_all | solution.py:31
  77.8 0.2 reshape.93
  78.0 0.3 copy.15
  78.3 0.2 reshape.94
  78.5 4.7 %all_gather.3.t_ref = bf16[2,64,256]{2,1,0:T(8,128)(2,1)} all-gather(bf16[1,64,256]{2,1,0:T(8,128)(2,1)S(1)} %reshape.94), channel_id=1, replica_groups=mesh['xh'=2,'core'=2,'xl'=2,'z'=8,'y'=4] {'xl'}, dimensions={0}, use_global_device_ids=true | all-gather | bytes 98304 | tf_op jit(solution)/shard_map/all_gather | solution.py:188
  83.2 1.0 fusion.4.n_ref
  84.2 12.6 %all-to-all-done.3.b_ref = bf16[32,88,128]{2,1,0:T(8,128)(2,1)S(1)} async-done(((bf16[32,88,128]{2,1,0:T(8,128)(2,1)}), bf16[32,88,128]{2,1,0:T(8,128)(2,1)S(1)}, u32[]{:S(2)}, u32[]{:S(2)}) %all-to-all-start.3) | async-done | bytes 720928 | tf_op jit(solution)/shard_map/all_to_all | solution.py:31
  96.8 0.1 fusion.12
  97.1 0.9 reshape.105.r_ref
  97.9 16.0 %attend.1 = f32[2,64,256]{2,1,0:T(8,128)} custom-call(bf16[2,64,256]{2,1,0:T(8,128)(2,1)} %all_gather.3.t_ref, bf16[32,88,128]{2,1,0:T(8,128)(2,1)} %copy-done, bf16[1344,64]{1,0:T(8,128)(2,1)} %reshape.105.r_ref, bf16[64,64]{1,0:T(8,128)(2,1)} %fusion.4.n_ref), custom_call_target="tpu_custom_call" | custom-call | flops 1000000000 | bytes 1200000 | tf_op jit(solution)/shard_map/attend/pallas_call | solution.py:130
  113.9 3.4 %all-to-all-start.4 = ((f32[2,64,256]{2,1,0:T(8,128)}), f32[2,64,256]{2,1,0:T(8,128)S(1)}, u32[]{:S(2)}, u32[]{:S(2)}) async-start(f32[2,64,256]{2,1,0:T(8,128)} %attend.1), calls=%async_computation.4 | async-start | bytes 262144 | tf_op jit(solution)/shard_map/all_to_all | solution.py:31
  117.3 4.4 %all-to-all-done.4 = f32[2,64,256]{2,1,0:T(8,128)S(1)} async-done(((f32[2,64,256]{2,1,0:T(8,128)}), f32[2,64,256]{2,1,0:T(8,128)S(1)}, u32[]{:S(2)}, u32[]{:S(2)}) %all-to-all-start.4) | async-done | bytes 131104 | tf_op jit(solution)/shard_map/all_to_all | solution.py:31
  121.7 0.7 add_bitcast_fusion
  (27 shorter events, 1.1 us)
Async XLA Ops:
  14.0 20.0 %all-to-all-start.1 = ((bf16[4,24,5632]{2,1,0:T(8,128)(2,1)}), bf16[4,24,5632]{2,1,0:T(8,128)(2,1)S(1)}, u32[]{:S(2)}, u32[]{:S(2)}) async-start(bf16[4,24,5632]{2,1,0:T(8,128)(2,1)} %bitcast.13), calls=%async_computation.1 | async-start | bytes 2162688 | tf_op jit(solution)/shard_map/all_to_all | solution.py:31
  70.4 7.3 %copy-start.1 = (f32[1,64,256]{2,1,0:T(8,128)S(1)}, f32[1,64,256]{2,1,0:T(8,128)}, u32[]{:S(2)}) copy-start(f32[1,64,256]{2,1,0:T(8,128)} %param.12) | copy-start | bytes 196612
  71.3 25.5 %all-to-all-start.3 = ((bf16[32,88,128]{2,1,0:T(8,128)(2,1)}), bf16[32,88,128]{2,1,0:T(8,128)(2,1)S(1)}, u32[]{:S(2)}, u32[]{:S(2)}) async-start(bf16[32,88,128]{2,1,0:T(8,128)(2,1)} %broadcast_in_dim.10), calls=%async_computation.3 | async-start | bytes 1441792 | tf_op jit(solution)/shard_map/all_to_all | solution.py:31
  96.8 1.1 copy-start
  113.9 7.8 %all-to-all-start.4 = ((f32[2,64,256]{2,1,0:T(8,128)}), f32[2,64,256]{2,1,0:T(8,128)S(1)}, u32[]{:S(2)}, u32[]{:S(2)}) async-start(f32[2,64,256]{2,1,0:T(8,128)} %attend.1), calls=%async_computation.4 | async-start | bytes 262144 | tf_op jit(solution)/shard_map/all_to_all | solution.py:31

commit v3 on v2

v3 whole, which is shorter than its diff:
```python
import jax
import jax.numpy as jnp
from jax import lax
from jax.experimental import pallas as pl
from jax.experimental.pallas import tpu as pltpu
from jax.sharding import Mesh, PartitionSpec as P

HEAD_DIM = 64
PROF = 8
NLEV = 16
EPS = 0.0001
LOG2E = 1.4426950408889634

SNAP = ("xh", "core")
PARAM = ("xl", "z", "y")
ZY = ("z", "y")
X = ("xh", "xl")
F32 = jnp.float32
BF16 = jnp.bfloat16
TN = (((0,), (0,)), ((), ()))


def noise_scales(levels):
    step = levels.astype(jnp.float32) / (NLEV - 1)
    sigma = jnp.exp(jnp.log(0.2) + step * (jnp.log(5.0) - jnp.log(0.2)))
    square = sigma * sigma + 0.25
    return (1.0 / jnp.sqrt(square), 0.25 / square, 0.5 * sigma / jnp.sqrt(square))


def a2a(x, axis):
    return lax.all_to_all(x, axis, 0, 0, tiled=True)


def contract_kernel(c_ref, q_ref, p_ref, i_ref, o_ref, m_ref, h_ref):
    snap = lax.broadcasted_iota(jnp.int32, (8, 168), 0)
    col = lax.broadcasted_iota(jnp.int32, (8, 168), 1)
    pick = jnp.where(lax.rem(col, 8) == snap, 1.0, 0.0)
    rows = lax.dot_general(c_ref[...], pick, TN, precision=lax.Precision.HIGHEST,
                           preferred_element_type=F32)
    r = lax.broadcasted_iota(jnp.int32, (24, 168), 0)
    col = lax.broadcasted_iota(jnp.int32, (24, 168), 1)
    same = jnp.where(col // 8 == r, 1.0, 0.0)
    mix = jnp.concatenate([rows[p:p + 1] * same for p in range(8)], axis=0)
    mix_hi = mix.astype(BF16)
    mix_lo = (mix - mix_hi.astype(F32)).astype(BF16)

    def piece(x):
        hi = x.astype(BF16)
        lo = (x - hi.astype(F32)).astype(BF16)
        y = jnp.dot(mix_hi, hi, preferred_element_type=F32)
        y = y + jnp.dot(mix_hi, lo, preferred_element_type=F32)
        y = y + jnp.dot(mix_lo, hi, preferred_element_type=F32)
        return y.astype(BF16)

    def store(y, blocks, at):
        width = y.shape[1]
        for p in range(8):
            core, slot = (p // 2) % 2, (p // 4) * 2 + p % 2
            for block in blocks:
                m_ref[core, 4 * slot + block, :, at:at + width] = y[p * 24:p * 24 + 24]

    store(piece(jnp.concatenate([i_ref[...], o_ref[...]], axis=1)), range(4), 1408)
    for start, width in ((0, 512), (512, 512), (1024, 320)):
        h_ref[:, start:start + width] = piece(p_ref[:, start:start + width])
    source = lax.broadcasted_iota(jnp.int32, (1344, 384), 0)
    col = lax.broadcasted_iota(jnp.int32, (1, 384), 1)
    r = lax.rem(col, 24)
    for block in range(4):
        want = jnp.where(r < 21, (col // 24) * 84 + block * 21 + r, -1)
        order = jnp.where(source == want, 1.0, 0.0).astype(BF16)
        y = jnp.dot(h_ref[...], order, preferred_element_type=F32).astype(BF16)
        store(y, (block,), 1024)
    for k in range(8):
        width = 512 if k < 7 else 448
        store(piece(q_ref[:, 512 * k:512 * k + width]), (k // 2,), 512 * (k % 2))
    for slot in range(4):
        m_ref[:, 4 * slot + 3, :, 960:1024] = jnp.zeros((2, 24, 64), BF16)


def contract(coeffs, q, p, w_in, w_out):
    return pl.pallas_call(
        contract_kernel,
        out_shape=jax.ShapeDtypeStruct((2, 16, 24, 1536), BF16),
        scratch_shapes=[pltpu.VMEM((192, 1344), BF16)],
        name="contract",
        compiler_params=pltpu.CompilerParams(vmem_limit_bytes=16 << 20),
        cost_estimate=pl.CostEstimate(flops=3 * 2 * 192 * 168 * 5504, bytes_accessed=6000000,
                                      transcendentals=0),
    )(coeffs, q, p, w_in, w_out)


def lines(values, count, width):
    hi = values.astype(BF16).astype(F32)
    lo = values - hi
    parts = [x[:, width * k:width * k + width] for x in (hi, lo) for k in range(count)]
    row = lax.broadcasted_iota(jnp.int32, (8, width), 0)
    out = jnp.zeros((8, width), F32)
    for k, part in enumerate(parts):
        out = jnp.where(row == k, part, out)
    return out


def unlines(rows, count):
    return jnp.concatenate([rows[k:k + 1] + rows[count + k:count + k + 1] for k in range(count)],
                           axis=1)


def partial_kernel(y_ref, g_ref, o_ref, p_ref):
    total = (g_ref[0:8].astype(F32) + g_ref[8:16].astype(F32)).reshape(192, 1536)
    w_in = total[:, 1408:1472]
    norm = jnp.sqrt(jnp.sum(w_in * w_in, axis=1, keepdims=True))
    w_in = (w_in / (EPS + norm)).astype(BF16)
    w_out = total[:, 1472:1536].astype(BF16)
    n = lax.dot_general(w_in, w_out, TN, preferred_element_type=F32)
    proj = total[:, 1024:1408]
    p_ref[...] = proj
    y = y_ref[0]
    own = [g_ref[4 * x + y].astype(F32) + g_ref[8 + 4 * x + y].astype(F32) for x in range(2)]
    own = jnp.concatenate([x[:, 1472:1536] for x in own], axis=1)
    low = jnp.concatenate([own, lines(jnp.sum(proj * proj, axis=0, keepdims=True), 3, 128)], axis=0)
    for z in range(8):
        q = total[:, 128 * z:128 * z + 128]
        m = lax.dot_general(w_in, q.astype(BF16), TN, preferred_element_type=F32)
        side = lines(jnp.sum(q * q, axis=0, keepdims=True), 2, 64)
        tail = jnp.concatenate([n[8 * z:8 * z + 8], side], axis=1)
        o_ref[z] = jnp.concatenate([m, tail, low], axis=0).astype(BF16)


def partial_products(y, got):
    return pl.pallas_call(
        partial_kernel,
        out_shape=(jax.ShapeDtypeStruct((8, 104, 128), BF16),
                   jax.ShapeDtypeStruct((192, 384), F32)),
        in_specs=[pl.BlockSpec(memory_space=pltpu.SMEM), pl.BlockSpec(memory_space=pltpu.VMEM)],
        name="partial",
        compiler_params=pltpu.CompilerParams(vmem_limit_bytes=8 << 20),
        cost_estimate=pl.CostEstimate(flops=2 * 64 * 192 * 1152, bytes_accessed=1000000,
                                      transcendentals=0),
    )(y, got)


def whole_kernel(g_ref, p_ref, o_ref, r_ref):
    total = g_ref[0].astype(F32)
    for z in range(1, 8):
        total = total + g_ref[z].astype(F32)
    m = total[0:64] / (EPS + jnp.sqrt(unlines(total[64:72, 64:128], 2)))
    out = jnp.concatenate([m, total[64:72]], axis=0).astype(BF16)
    for k in range(32):
        o_ref[k] = out
    w_out = g_ref[:, 72:96, :].astype(F32).reshape(192, 128)
    w_out = jnp.concatenate([w_out[:, :64], w_out[:, 64:]], axis=0)
    norm = jnp.sqrt(unlines(total[96:104], 3))
    proj = (p_ref[...] / (EPS + norm)).astype(BF16)
    r = jnp.dot(proj, w_out.astype(BF16), preferred_element_type=F32)
    square = lines(jnp.sum(w_out * w_out, axis=0, keepdims=True), 1, 64)
    square = jnp.concatenate([square, square], axis=1)
    for y in range(4):
        both = jnp.concatenate([r[24 * y:24 * y + 24], r[96 + 24 * y:120 + 24 * y]], axis=1)
        r_ref[y] = jnp.concatenate([both, square], axis=0).astype(BF16)


def whole_products(got, proj):
    return pl.pallas_call(
        whole_kernel,
        out_shape=(jax.ShapeDtypeStruct((32, 72, 128), BF16),
                   jax.ShapeDtypeStruct((4, 32, 128), BF16)),
        name="whole",
        compiler_params=pltpu.CompilerParams(vmem_limit_bytes=8 << 20),
        cost_estimate=pl.CostEstimate(flops=100000, bytes_accessed=800000, transcendentals=0),
    )(got, proj)


def attend_kernel(t_ref, b_ref, a_ref, s_ref):
    tokens = jnp.concatenate([t_ref[0], t_ref[1]], axis=1)

    def project(c, carry):
        x = lax.dot_general(b_ref[c, 0:64, :], tokens, TN, preferred_element_type=F32)
        x = x.reshape(2, 64, 512)
        scale = jnp.sqrt(jnp.sum(x * x, axis=1, keepdims=True) * (1.0 / 64))
        unit = 2 * (lax.rem(c, 4) * 8 + c // 4)
        s_ref[pl.ds(unit, 2)] = (x * (1.0 / (EPS + scale))).astype(BF16)
        return carry

    lax.fori_loop(0, 32, project, 0, unroll=4)

    def head(h, carry):
        for b in range(2):
            at = slice(256 * b, 256 * b + 256)
            query, keys, values = s_ref[h, :, at], s_ref[21 + h, :, at], s_ref[42 + h, :, at]
            scores = lax.dot_general(keys, query, TN, preferred_element_type=F32)
            expo = jnp.exp2(scores * (0.125 * LOG2E))
            total = jnp.sum(expo, axis=0, keepdims=True)
            out = jnp.dot(values, expo.astype(BF16), preferred_element_type=F32)
            a_ref[pl.ds(pl.multiple_of(h * 64, 64), 64), at] = (out * (1.0 / total)).astype(BF16)
        return carry

    lax.fori_loop(0, 21, head, 0, unroll=3)


def attend(tokens, got):
    return pl.pallas_call(
        attend_kernel,
        out_shape=jax.ShapeDtypeStruct((1344, 512), BF16),
        scratch_shapes=[pltpu.VMEM((64, 64, 512), BF16)],
        name="attend",
        compiler_params=pltpu.CompilerParams(vmem_limit_bytes=16 << 20),
        cost_estimate=pl.CostEstimate(flops=5000000000, bytes_accessed=2400000, transcendentals=2800000),
    )(tokens, got)


def output_kernel(t_ref, b_ref, a_ref, r_ref, s_out_ref, o_ref, z_ref):
    tokens = jnp.concatenate([t_ref[0], t_ref[1]], axis=1)
    feature = 0.3 * lax.dot_general(r_ref[...], a_ref[...], TN, preferred_element_type=F32)
    n = jnp.concatenate([b_ref[4 * z, 64:72, 0:64].astype(F32) for z in range(8)], axis=0)
    feature = feature + 0.7 * lax.dot_general(n.astype(BF16), tokens, TN, preferred_element_type=F32)
    feature = feature * (s_out_ref[...] * (1.0 / (0.58 ** 0.5)))
    token = lax.broadcasted_iota(jnp.int32, (256, 256), 0)
    lane = lax.broadcasted_iota(jnp.int32, (256, 256), 1)
    keep = lax.rem(token, 16) == lane // 16
    row = lax.broadcasted_iota(jnp.int32, (128, 256), 0)
    lane = lax.broadcasted_iota(jnp.int32, (128, 256), 1)
    for b in range(2):
        part = feature[:, 256 * b:256 * b + 256]
        hi = part.astype(BF16)
        lo = (part - hi.astype(F32)).astype(BF16)
        both = jnp.concatenate([hi, lo], axis=0)
        for i in range(4):
            tile = jnp.where(lax.rem(row, 64) == 16 * i + lax.rem(lane, 16), 1.0, 0.0).astype(BF16)
            wide = lax.dot_general(both, tile, TN, preferred_element_type=F32)
            wide = jnp.where(keep, wide, 0.0).reshape(16, 16, 256)
            wide = jnp.sum(wide, axis=1)
            z_ref[2 * b, pl.ds(i, 16, stride=4), :] = wide[:, :128]
            z_ref[2 * b + 1, pl.ds(i, 16, stride=4), :] = wide[:, 128:]
        o_ref[b] = jnp.concatenate([z_ref[2 * b], z_ref[2 * b + 1]], axis=1)


def output(tokens, got, attended, r, scale):
    return pl.pallas_call(
        output_kernel,
        out_shape=jax.ShapeDtypeStruct((2, 64, 256), F32),
        scratch_shapes=[pltpu.VMEM((4, 64, 128), F32)],
        name="output",
        compiler_params=pltpu.CompilerParams(vmem_limit_bytes=12 << 20),
        cost_estimate=pl.CostEstimate(flops=100000000, bytes_accessed=2000000, transcendentals=0),
    )(tokens, got, attended, r, scale)


def shards(snap_in, snap_qkv, snap_proj, snap_out, coeffs, latent, levels):
    y = lax.axis_index("y")
    part = contract(
        coeffs,
        snap_qkv.transpose(1, 0, 2).reshape(168, 4032),
        snap_proj.transpose(1, 0, 2).reshape(168, 1344),
        snap_in.transpose(2, 0, 1).reshape(168, 64),
        snap_out.transpose(1, 0, 2).reshape(168, 64),
    )
    part = a2a(part, "core").astype(F32)
    part = (part[0] + part[1]).astype(BF16)
    part = a2a(part, ("xh", "xl", "y"))
    send, proj = partial_products(y.astype(jnp.int32).reshape(1), part)
    send, side = whole_products(a2a(send, "z"), proj)
    got = a2a(send, ZY)

    total = lax.dynamic_index_in_dim(side, y, 0, False).astype(F32)
    for d in range(1, 4):
        there = lax.dynamic_index_in_dim(side, lax.rem(y + d, 4), 0, False)
        there = lax.ppermute(there, "y", [(k, (k + d) % 4) for k in range(4)])
        total = total + there.astype(F32)
    scale = 1.0 / (EPS + jnp.sqrt(total[24, :64] + total[25, :64]))
    total, _ = lax.optimization_barrier((total, got))
    r = jnp.broadcast_to(total[None, :24].astype(BF16), (32, 24, 128))
    r = a2a(r, ZY)[:, :21]
    r = jnp.concatenate([r[:, :, :64], r[:, :, 64:]], axis=0).reshape(1344, 64)

    c_in, c_skip, c_out = noise_scales(levels)
    tokens = (c_in[:, None, None] * latent).astype(BF16)
    tokens = tokens.reshape(16, 4, 16, 16).transpose(1, 3, 0, 2).reshape(1, 64, 256)
    tokens = lax.all_gather(tokens, "xl", axis=0, tiled=True)
    attended = attend(tokens, got)
    feature = a2a(output(tokens, got, attended, r, scale[:, None]), "xl")
    out = c_skip[:, None, None] * latent + c_out[:, None, None] * feature
    return out[:, None]


def solution(mesh):
    fine = Mesh(mesh.devices.reshape(2, 2, 2, 8, 4), ("xh", "core", "xl", "z", "y"))
    in_specs = (
        P(SNAP, None, PARAM),
        P(SNAP, PARAM, None),
        P(SNAP, PARAM, None),
        P(SNAP, PARAM, None),
        P(SNAP, None),
        P(PARAM, None, None),
        P(PARAM),
    )
    out_specs = P(SNAP, PARAM, None, None)
    return jax.shard_map(shards, mesh=fine, in_specs=in_specs, out_specs=out_specs, check_vma=False)
```

time: 123 us -> 112 us (0.911)
  blocking collectives: 44.5 us -> 28.4 us
  starting transfers between devices: 13.2 us -> 26.3 us
  waiting for transfers between devices: 32.7 us -> 26.2 us
  local copies, waits for them, and re-layouts: 4 us -> 7.21 us
  Pallas kernels: 21.6 us -> 19.7 us
  matrix products: 1.51 us -> 0 us
    all_to_all x2, blocking collectives: 39.8 us -> 23.8 us  [a2a(): return lax.all_to_all(x, axis, 0, 0, tiled=True)]
    all_to_all x3 -> x4, starting transfers between devices: 13.2 us -> 21.5 us  [a2a(): return lax.all_to_all(x, axis, 0, 0, tiled=True)]
    all_to_all x3 -> x4, waiting for transfers between devices: 32.7 us -> 26.2 us  [a2a(): return lax.all_to_all(x, axis, 0, 0, tiled=True)]
    unnamed x5 -> x12, local copies, waits for them, and re-layouts: 0.07 us -> 5.43 us
    ppermute x0 -> x3, starting transfers between devices: none -> 4.79 us  [shards(): there = lax.ppermute(there, 'y', [(k, (k + d) % 4) for k in range(4)])]
    pallas_call x2 -> x5, Pallas kernels: 21.6 us -> 19.7 us  [the longest x1 13.1 us: attend(): pl.pallas_call(attend_kernel, out_shape=jax.ShapeDtypeStruct((1344, 512),...]
    dot_general x3 -> x0, matrix products: 1.51 us -> none  [the longest x1 1.03 us: shards(): n = lax.dot_general(wi, wo, TN, preferred_element_type=F32) * on]
  transfers between devices with their start and end apart: 3 -> 7, of which waited for: 3 -> 3; matrix products, arithmetic and copies ran while one was open for 2% -> 1% of each run, Pallas kernels for 0% -> 12%
where the time goes in v3:
time: 112 us
  blocking collectives  28.4 us (25%)
  starting transfers between devices  26.3 us (23%)
  waiting for transfers between devices  26.2 us (23%)
  Pallas kernels  19.7 us (18%)
  local copies, waits for them, and re-layouts  7.21 us (6%)
  other arithmetic  2.77 us (2%)
    all_to_all x4, waiting for transfers between devices, a2a(): return lax.all_to_all(x, axis, 0, 0, tiled=True)  26.2 us
    all_to_all x2, blocking collectives, a2a(): return lax.all_to_all(x, axis, 0, 0, tiled=True)  23.8 us
    all_to_all x4, starting transfers between devices, a2a(): return lax.all_to_all(x, axis, 0, 0, tiled=True)  21.5 us
    pallas_call x1, Pallas kernels, attend(): pl.pallas_call(attend_kernel, out_shape=jax.ShapeDtypeStruct((1344, 512),...  13.1 us
    unnamed x12, local copies, waits for them, and re-layouts  5.43 us
    ppermute x3, starting transfers between devices, shards(): there = lax.ppermute(there, 'y', [(k, (k + d) % 4) for k in range(4)])  4.79 us
    all_gather x1, blocking collectives, shards(): tokens = lax.all_gather(tokens, 'xl', axis=0, tiled=True)  4.57 us
    pallas_call x1, Pallas kernels, contract(): pl.pallas_call(contract_kernel, out_shape=jax.ShapeDtypeStruct((2, 16, 24...  3.35 us
  transfers between devices with their start and end apart: 7, of which 3 were waited for; matrix products, arithmetic and copies ran while one was open for 1% of the time, Pallas kernels for 12%

profile of v3, /device:TPU:8, one launch (start us, length us, event | category | flops | bytes accessed | tf_op | source)
XLA Modules:
  0.0 111.6 jit_solution(10670366826589716708)
XLA Ops:
  0.0 1.8 %copy-done = f32[8,21,4032]{2,0,1:T(8,128)S(1)} copy-done((f32[8,21,4032]{2,0,1:T(8,128)S(1)}, f32[8,21,4032]{2,0,1:T(8,128)}, u32[]{:S(2)}) %copy-start) | copy-done | bytes 2709528
  1.8 1.2 %copy-done.1 = f32[8,21,1344]{2,0,1:T(8,128)S(1)} copy-done((f32[8,21,1344]{2,0,1:T(8,128)S(1)}, f32[8,21,1344]{2,0,1:T(8,128)}, u32[]{:S(2)}) %copy-start.1) | copy-done | bytes 903192
  3.0 0.9 copy-done.2
  3.9 0.9 copy-done.3
  4.7 0.7 copy-done.4
  5.4 3.4 %contract.1 = bf16[2,16,24,1536]{3,2,1,0:T(8,128)(2,1)S(1)} custom-call(f32[8,8]{1,0:T(8,128)S(1)} %copy-done.4, f32[168,4032]{1,0:T(8,128)S(1)} %bitcast.38, f32[168,1344]{1,0:T(8,128)S(1)} %bitcast.39, f32[168,64]{1,0:T(8,128)S(1)} %bitcast.40, f32[168,64]{1,0:T(8,128)S(1)} %bitcast.41), custom_call_target="tpu_custom_call" | custom-call | flops 1065222144 | bytes 6000000 | tf_op jit(solution)/shard_map/contract/pallas_call | solution.py:81
  8.8 5.6 %all_to_all.30 = bf16[2,16,24,1536]{3,2,1,0:T(8,128)(2,1)S(1)} all-to-all(bf16[2,16,24,1536]{3,2,1,0:T(8,128)(2,1)S(1)} %contract.1), channel_id=1, replica_groups=mesh['xh'=2,'core'=2,'xl'=2,'z'=8,'y'=4] {'core'}, dimensions={0} | all-to-all | bytes 4718592 | tf_op jit(solution)/shard_map/all_to_all | solution.py:31
  14.4 0.6 convert_element_type.34
  15.1 1.3 %fusion.1 = bf16[16,24,1536]{2,1,0:T(8,128)(2,1)} fusion(f32[2,16,24,1536]{3,2,1,0:T(8,128)S(1)} %convert_element_type.34), kind=kLoop, calls=%fused_computation.2 | loop fusion | flops 1179648 | bytes 5898240 | tf_op jit(solution)/shard_map/convert_element_type | solution.py:258
  16.4 7.5 %all-to-all-start.1 = ((bf16[16,24,1536]{2,1,0:T(8,128)(2,1)}), bf16[16,24,1536]{2,1,0:T(8,128)(2,1)S(1)}, u32[]{:S(2)}, u32[]{:S(2)}) async-start(bf16[16,24,1536]{2,1,0:T(8,128)(2,1)} %fusion.1), calls=%async_computation.1 | async-start | bytes 2359296 | tf_op jit(solution)/shard_map/all_to_all | solution.py:31
  23.9 18.2 %all-to-all-done.1.g_ref = bf16[16,24,1536]{2,1,0:T(8,128)(2,1)S(1)} async-done(((bf16[16,24,1536]{2,1,0:T(8,128)(2,1)}), bf16[16,24,1536]{2,1,0:T(8,128)(2,1)S(1)}, u32[]{:S(2)}, u32[]{:S(2)}) %all-to-all-start.1) | async-done | bytes 1179680 | tf_op jit(solution)/shard_map/all_to_all | solution.py:31
  42.2 0.5 partial.1
  42.7 18.2 %all_to_all.31.g_ref = bf16[8,104,128]{2,1,0:T(8,128)(2,1)S(1)} all-to-all(bf16[8,104,128]{2,1,0:T(8,128)(2,1)S(1)} %get-tuple-element.10), channel_id=1, replica_groups=mesh['xh'=2,'core'=2,'xl'=2,'z'=8,'y'=4] {'z'}, dimensions={0} | all-to-all | bytes 425984 | tf_op jit(solution)/shard_map/all_to_all | solution.py:31
  60.9 1.1 whole.1
  62.0 5.0 %all-to-all-start.3 = ((bf16[32,72,128]{2,1,0:T(8,128)(2,1)}), bf16[32,72,128]{2,1,0:T(8,128)(2,1)S(1)}, u32[]{:S(2)}, u32[]{:S(2)}) async-start(bf16[32,72,128]{2,1,0:T(8,128)(2,1)} %get-tuple-element.12), calls=%async_computation.3 | async-start | bytes 1179648 | tf_op jit(solution)/shard_map/all_to_all | solution.py:31
  67.9 0.2 reshape.69
  68.1 0.3 copy.14
  68.4 0.2 reshape.70
  68.7 1.5 %collective-permute-start = (bf16[32,128]{1,0:T(8,128)(2,1)S(1)}, bf16[32,128]{1,0:T(8,128)(2,1)S(1)}, u32[]{:S(2)}, u32[]{:S(2)}) collective-permute-start(bf16[32,128]{1,0:T(8,128)(2,1)S(1)} %get-tuple-element.19), channel_id=1, source_target_pairs={{0,1},{1,2},{2,3},{3,0},{4,5},{5,6},{6,7},{7,4},{8,9},{9,10},{10,1... | collective-permute-start | bytes 24584 | tf_op jit(solution)/shard_map/ppermute | solution.py:267
  70.2 0.9 collective-permute-start.1
  71.2 2.3 %collective-permute-start.2 = (bf16[32,128]{1,0:T(8,128)(2,1)S(1)}, bf16[32,128]{1,0:T(8,128)(2,1)S(1)}, u32[]{:S(2)}, u32[]{:S(2)}) collective-permute-start(bf16[32,128]{1,0:T(8,128)(2,1)S(1)} %get-tuple-element.20), channel_id=1, source_target_pairs={{0,3},{1,0},{2,1},{3,2},{4,7},{5,4},{6,5},{7,6},{8,11},{9,8},{10,9... | collective-permute-start | bytes 24584 | tf_op jit(solution)/shard_map/ppermute | solution.py:267
  73.4 4.6 %all_gather.3.t_ref = bf16[2,64,256]{2,1,0:T(8,128)(2,1)S(1)} all-gather(bf16[1,64,256]{2,1,0:T(8,128)(2,1)S(1)} %reshape.70), channel_id=1, replica_groups=mesh['xh'=2,'core'=2,'xl'=2,'z'=8,'y'=4] {'xl'}, dimensions={0}, use_global_device_ids=true | all-gather | bytes 98304 | tf_op jit(solution)/shard_map/all_gather | solution.py:278
  78.2 3.5 %all-to-all-done.3.b_ref = bf16[32,72,128]{2,1,0:T(8,128)(2,1)S(1)} async-done(((bf16[32,72,128]{2,1,0:T(8,128)(2,1)}), bf16[32,72,128]{2,1,0:T(8,128)(2,1)S(1)}, u32[]{:S(2)}, u32[]{:S(2)}) %all-to-all-start.3) | async-done | bytes 589856 | tf_op jit(solution)/shard_map/all_to_all | solution.py:31
  81.7 0.7 broadcast_in_dim.4
  82.4 5.6 %all-to-all-start.4 = ((bf16[32,24,128]{2,1,0:T(8,128)(2,1)}), bf16[32,24,128]{2,1,0:T(8,128)(2,1)S(1)}, u32[]{:S(2)}, u32[]{:S(2)}) async-start(bf16[32,24,128]{2,1,0:T(8,128)(2,1)} %broadcast_in_dim.4), calls=%async_computation.4 | async-start | bytes 393216 | tf_op jit(solution)/shard_map/all_to_all | solution.py:31
  87.9 13.1 %attend.1.a_ref = bf16[1344,512]{1,0:T(8,128)(2,1)S(1)} custom-call(bf16[2,64,256]{2,1,0:T(8,128)(2,1)S(1)} %all_gather.3.t_ref, bf16[32,72,128]{2,1,0:T(8,128)(2,1)S(1)} %all-to-all-done.3.b_ref), custom_call_target="tpu_custom_call" | custom-call | flops 5000000000 | bytes 2400000 | tf_op jit(solution)/shard_map/attend/pallas_call | solution.py:201
  101.1 0.1 fusion.5
  101.3 0.1 reshape.76.r_ref
  101.5 1.6 %output.1 = f32[2,64,256]{2,1,0:T(8,128)} custom-call(bf16[2,64,256]{2,1,0:T(8,128)(2,1)S(1)} %all_gather.3.t_ref, bf16[32,72,128]{2,1,0:T(8,128)(2,1)S(1)} %all-to-all-done.3.b_ref, bf16[1344,512]{1,0:T(8,128)(2,1)S(1)} %attend.1.a_ref, bf16[1344,64]{1,0:T(8,128)(2,1)S(1)} %reshape.76.r_ref, f32[64,1]{1,0:T(8,128)S(1)} %copy.15.s_out_ref), custom_call_target="tpu_custom_call" | custom-call | flops 100000000 | bytes 2000000 | tf_op jit(solution)/shard_map/output/pallas_call | solution.py:238
  103.1 3.4 %all-to-all-start.5 = ((f32[2,64,256]{2,1,0:T(8,128)}), f32[2,64,256]{2,1,0:T(8,128)S(1)}, u32[]{:S(2)}, u32[]{:S(2)}) async-start(f32[2,64,256]{2,1,0:T(8,128)} %output.1), calls=%async_computation.5 | async-start | bytes 262144 | tf_op jit(solution)/shard_map/all_to_all | solution.py:31
  106.5 4.4 %all-to-all-done.5 = f32[2,64,256]{2,1,0:T(8,128)S(1)} async-done(((f32[2,64,256]{2,1,0:T(8,128)}), f32[2,64,256]{2,1,0:T(8,128)S(1)}, u32[]{:S(2)}, u32[]{:S(2)}) %all-to-all-start.5) | async-done | bytes 131104 | tf_op jit(solution)/shard_map/all_to_all | solution.py:31
  110.9 0.7 add_bitcast_fusion
  (18 shorter events, 0.3 us)
Async XLA Ops:
  0.0 1.8 %copy-start = (f32[8,21,4032]{2,0,1:T(8,128)S(1)}, f32[8,21,4032]{2,0,1:T(8,128)}, u32[]{:S(2)}) copy-start(f32[8,21,4032]{2,0,1:T(8,128)} %param.8) | copy-start | bytes 8128516
  1.8 1.2 %copy-start.1 = (f32[8,21,1344]{2,0,1:T(8,128)S(1)}, f32[8,21,1344]{2,0,1:T(8,128)}, u32[]{:S(2)}) copy-start(f32[8,21,1344]{2,0,1:T(8,128)} %param.9) | copy-start | bytes 2709508
  3.0 0.9 copy-start.2
  3.9 0.9 copy-start.3
  4.7 0.7 copy-start.4
  16.4 51.5 %copy-start.5 = (f32[1,64,256]{2,1,0:T(8,128)S(1)}, f32[1,64,256]{2,1,0:T(8,128)}, u32[]{:S(2)}) copy-start(f32[1,64,256]{2,1,0:T(8,128)} %param.12) | copy-start | bytes 196612
  16.4 25.8 %all-to-all-start.1 = ((bf16[16,24,1536]{2,1,0:T(8,128)(2,1)}), bf16[16,24,1536]{2,1,0:T(8,128)(2,1)S(1)}, u32[]{:S(2)}, u32[]{:S(2)}) async-start(bf16[16,24,1536]{2,1,0:T(8,128)(2,1)} %fusion.1), calls=%async_computation.1 | async-start | bytes 2359296 | tf_op jit(solution)/shard_map/all_to_all | solution.py:31
  62.0 19.7 %all-to-all-start.3 = ((bf16[32,72,128]{2,1,0:T(8,128)(2,1)}), bf16[32,72,128]{2,1,0:T(8,128)(2,1)S(1)}, u32[]{:S(2)}, u32[]{:S(2)}) async-start(bf16[32,72,128]{2,1,0:T(8,128)(2,1)} %get-tuple-element.12), calls=%async_computation.3 | async-start | bytes 1179648 | tf_op jit(solution)/shard_map/all_to_all | solution.py:31
  68.7 9.4 %collective-permute-start = (bf16[32,128]{1,0:T(8,128)(2,1)S(1)}, bf16[32,128]{1,0:T(8,128)(2,1)S(1)}, u32[]{:S(2)}, u32[]{:S(2)}) collective-permute-start(bf16[32,128]{1,0:T(8,128)(2,1)S(1)} %get-tuple-element.19), channel_id=1, source_target_pairs={{0,1},{1,2},{2,3},{3,0},{4,5},{5,6},{6,7},{7,4},{8,9},{9,10},{10,1... | collective-permute-start | bytes 24584 | tf_op jit(solution)/shard_map/ppermute | solution.py:267
  70.2 7.8 %collective-permute-start.1 = (bf16[32,128]{1,0:T(8,128)(2,1)S(1)}, bf16[32,128]{1,0:T(8,128)(2,1)S(1)}, u32[]{:S(2)}, u32[]{:S(2)}) collective-permute-start(bf16[32,128]{1,0:T(8,128)(2,1)S(1)} %get-tuple-element.21), channel_id=1, source_target_pairs={{0,2},{1,3},{2,0},{3,1},{4,6},{5,7},{6,4},{7,5},{8,10},{9,11},{10,... | collective-permute-start | bytes 24584 | tf_op jit(solution)/shard_map/ppermute | solution.py:267
  71.2 6.9 %collective-permute-start.2 = (bf16[32,128]{1,0:T(8,128)(2,1)S(1)}, bf16[32,128]{1,0:T(8,128)(2,1)S(1)}, u32[]{:S(2)}, u32[]{:S(2)}) collective-permute-start(bf16[32,128]{1,0:T(8,128)(2,1)S(1)} %get-tuple-element.20), channel_id=1, source_target_pairs={{0,3},{1,0},{2,1},{3,2},{4,7},{5,4},{6,5},{7,6},{8,11},{9,8},{10,9... | collective-permute-start | bytes 24584 | tf_op jit(solution)/shard_map/ppermute | solution.py:267
  82.4 18.7 %all-to-all-start.4 = ((bf16[32,24,128]{2,1,0:T(8,128)(2,1)}), bf16[32,24,128]{2,1,0:T(8,128)(2,1)S(1)}, u32[]{:S(2)}, u32[]{:S(2)}) async-start(bf16[32,24,128]{2,1,0:T(8,128)(2,1)} %broadcast_in_dim.4), calls=%async_computation.4 | async-start | bytes 393216 | tf_op jit(solution)/shard_map/all_to_all | solution.py:31
  103.1 7.8 %all-to-all-start.5 = ((f32[2,64,256]{2,1,0:T(8,128)}), f32[2,64,256]{2,1,0:T(8,128)S(1)}, u32[]{:S(2)}, u32[]{:S(2)}) async-start(f32[2,64,256]{2,1,0:T(8,128)} %output.1), calls=%async_computation.5 | async-start | bytes 262144 | tf_op jit(solution)/shard_map/all_to_all | solution.py:31

commit v4 on v3

--- a/solution.py
+++ b/solution.py
@@ -31,7 +31,13 @@
     return lax.all_to_all(x, axis, 0, 0, tiled=True)
 
 
-def contract_kernel(c_ref, q_ref, p_ref, i_ref, o_ref, m_ref, h_ref):
+def contract_kernel(c_hbm, q_hbm, p_hbm, i_hbm, o_hbm, keep_ref, give_ref, q_ref, p_ref, i_ref,
+                    o_ref, h_ref, c_ref, sems):
+    copies = [pltpu.make_async_copy(a, b, sems.at[k]) for k, (a, b) in enumerate(
+        ((i_hbm, i_ref), (o_hbm, o_ref), (p_hbm, p_ref), (q_hbm, q_ref), (c_hbm, c_ref)))]
+    for k in (4, 0, 1, 2, 3):
+        copies[k].start()
+    copies[4].wait()
     snap = lax.broadcasted_iota(jnp.int32, (8, 168), 0)
     col = lax.broadcasted_iota(jnp.int32, (8, 168), 1)
     pick = jnp.where(lax.rem(col, 8) == snap, 1.0, 0.0)
@@ -40,7 +46,13 @@
     r = lax.broadcasted_iota(jnp.int32, (24, 168), 0)
     col = lax.broadcasted_iota(jnp.int32, (24, 168), 1)
     same = jnp.where(col // 8 == r, 1.0, 0.0)
-    mix = jnp.concatenate([rows[p:p + 1] * same for p in range(8)], axis=0)
+    mine = lax.axis_index("core")
+    picked = []
+    for k in range(2):
+        for slot in range(4):
+            p = (slot // 2) * 4 + slot % 2
+            picked.append(jnp.where(mine == k, rows[p:p + 1], rows[p + 2:p + 3]))
+    mix = jnp.concatenate([row * same for row in picked], axis=0)
     mix_hi = mix.astype(BF16)
     mix_lo = (mix - mix_hi.astype(F32)).astype(BF16)
 
@@ -54,12 +66,16 @@
 
     def store(y, blocks, at):
         width = y.shape[1]
-        for p in range(8):
-            core, slot = (p // 2) % 2, (p // 4) * 2 + p % 2
-            for block in blocks:
-                m_ref[core, 4 * slot + block, :, at:at + width] = y[p * 24:p * 24 + 24]
-
+        for k, ref in enumerate((keep_ref, give_ref)):
+            for slot in range(4):
+                row = 96 * k + 24 * slot
+                for block in blocks:
+                    ref[4 * slot + block, :, at:at + width] = y[row:row + 24]
+
+    copies[0].wait()
+    copies[1].wait()
     store(piece(jnp.concatenate([i_ref[...], o_ref[...]], axis=1)), range(4), 1408)
+    copies[2].wait()
     for start, width in ((0, 512), (512, 512), (1024, 320)):
         h_ref[:, start:start + width] = piece(p_ref[:, start:start + width])
     source = lax.broadcasted_iota(jnp.int32, (1344, 384), 0)
@@ -70,23 +86,50 @@
         order = jnp.where(source == want, 1.0, 0.0).astype(BF16)
         y = jnp.dot(h_ref[...], order, preferred_element_type=F32).astype(BF16)
         store(y, (block,), 1024)
+    copies[3].wait()
     for k in range(8):
         width = 512 if k < 7 else 448
         store(piece(q_ref[:, 512 * k:512 * k + width]), (k // 2,), 512 * (k % 2))
     for slot in range(4):
-        m_ref[:, 4 * slot + 3, :, 960:1024] = jnp.zeros((2, 24, 64), BF16)
+        for ref in (keep_ref, give_ref):
+            ref[4 * slot + 3, :, 960:1024] = jnp.zeros((24, 64), BF16)
+
+
+VMEM = pl.BlockSpec(memory_space=pltpu.VMEM)
+HBM = pl.BlockSpec(memory_space=pltpu.HBM)
 
 
 def contract(coeffs, q, p, w_in, w_out):
+    shape = jax.ShapeDtypeStruct((16, 24, 1536), BF16)
     return pl.pallas_call(
         contract_kernel,
-        out_shape=jax.ShapeDtypeStruct((2, 16, 24, 1536), BF16),
-        scratch_shapes=[pltpu.VMEM((192, 1344), BF16)],
+        out_shape=(shape, shape),
+        in_specs=[HBM] * 5,
+        out_specs=(VMEM, VMEM),
+        scratch_shapes=[pltpu.VMEM((168, 4032), F32), pltpu.VMEM((168, 1344), F32),
+                        pltpu.VMEM((168, 64), F32), pltpu.VMEM((168, 64), F32),
+                        pltpu.VMEM((192, 1344), BF16), pltpu.VMEM((8, 8), F32),
+                        pltpu.SemaphoreType.DMA((5,))],
         name="contract",
         compiler_params=pltpu.CompilerParams(vmem_limit_bytes=16 << 20),
         cost_estimate=pl.CostEstimate(flops=3 * 2 * 192 * 168 * 5504, bytes_accessed=6000000,
                                       transcendentals=0),
-    )(coeffs, q, p, w_in, w_out)
+    )(*[pltpu.with_memory_space_constraint(x, pltpu.HBM) for x in (coeffs, q, p, w_in, w_out)])
+
+
+def pair_kernel(a_ref, b_ref, o_ref):
+    for k in range(16):
+        o_ref[k] = (a_ref[k].astype(F32) + b_ref[k].astype(F32)).astype(BF16)
+
+
+def pair_sum(a, b):
+    return pl.pallas_call(
+        pair_kernel,
+        out_shape=jax.ShapeDtypeStruct((16, 24, 1536), BF16),
+        name="pair",
+        compiler_params=pltpu.CompilerParams(vmem_limit_bytes=8 << 20),
+        cost_estimate=pl.CostEstimate(flops=600000, bytes_accessed=3600000, transcendentals=0),
+    )(a, b)
 
 
 def lines(values, count, width):
@@ -105,7 +148,7 @@
                            axis=1)
 
 
-def partial_kernel(y_ref, g_ref, o_ref, p_ref):
+def partial_kernel(g_ref, o_ref, p_ref):
     total = (g_ref[0:8].astype(F32) + g_ref[8:16].astype(F32)).reshape(192, 1536)
     w_in = total[:, 1408:1472]
     norm = jnp.sqrt(jnp.sum(w_in * w_in, axis=1, keepdims=True))
@@ -114,7 +157,7 @@
     n = lax.dot_general(w_in, w_out, TN, preferred_element_type=F32)
     proj = total[:, 1024:1408]
     p_ref[...] = proj
-    y = y_ref[0]
+    y = lax.axis_index("y")
     own = [g_ref[4 * x + y].astype(F32) + g_ref[8 + 4 * x + y].astype(F32) for x in range(2)]
     own = jnp.concatenate([x[:, 1472:1536] for x in own], axis=1)
     low = jnp.concatenate([own, lines(jnp.sum(proj * proj, axis=0, keepdims=True), 3, 128)], axis=0)
@@ -126,17 +169,16 @@
         o_ref[z] = jnp.concatenate([m, tail, low], axis=0).astype(BF16)
 
 
-def partial_products(y, got):
+def partial_products(got):
     return pl.pallas_call(
         partial_kernel,
         out_shape=(jax.ShapeDtypeStruct((8, 104, 128), BF16),
                    jax.ShapeDtypeStruct((192, 384), F32)),
-        in_specs=[pl.BlockSpec(memory_space=pltpu.SMEM), pl.BlockSpec(memory_space=pltpu.VMEM)],
         name="partial",
         compiler_params=pltpu.CompilerParams(vmem_limit_bytes=8 << 20),
         cost_estimate=pl.CostEstimate(flops=2 * 64 * 192 * 1152, bytes_accessed=1000000,
                                       transcendentals=0),
-    )(y, got)
+    )(got)
 
 
 def whole_kernel(g_ref, p_ref, o_ref, r_ref):
@@ -154,9 +196,10 @@
     r = jnp.dot(proj, w_out.astype(BF16), preferred_element_type=F32)
     square = lines(jnp.sum(w_out * w_out, axis=0, keepdims=True), 1, 64)
     square = jnp.concatenate([square, square], axis=1)
+    mine = lax.axis_index("y")
     for y in range(4):
         both = jnp.concatenate([r[24 * y:24 * y + 24], r[96 + 24 * y:120 + 24 * y]], axis=1)
-        r_ref[y] = jnp.concatenate([both, square], axis=0).astype(BF16)
+        r_ref[lax.rem(y + 4 - mine, 4)] = jnp.concatenate([both, square], axis=0).astype(BF16)
 
 
 def whole_products(got, proj):
@@ -170,45 +213,64 @@
     )(got, proj)
 
 
-def attend_kernel(t_ref, b_ref, a_ref, s_ref):
+def attend_kernel(t_ref, b_ref, a_ref, s_ref, e_ref, d_ref):
     tokens = jnp.concatenate([t_ref[0], t_ref[1]], axis=1)
 
-    def project(c, carry):
-        x = lax.dot_general(b_ref[c, 0:64, :], tokens, TN, preferred_element_type=F32)
-        x = x.reshape(2, 64, 512)
-        scale = jnp.sqrt(jnp.sum(x * x, axis=1, keepdims=True) * (1.0 / 64))
-        unit = 2 * (lax.rem(c, 4) * 8 + c // 4)
-        s_ref[pl.ds(unit, 2)] = (x * (1.0 / (EPS + scale))).astype(BF16)
+    def project(g, carry):
+        xs = []
+        for k in range(4):
+            x = lax.dot_general(b_ref[4 * g + k, 0:64, :], tokens, TN, preferred_element_type=F32)
+            xs.append(x.reshape(2, 64, 512))
+        squares = [jnp.sum(x * x, axis=1) for x in xs]
+        scale = jnp.sqrt(jnp.concatenate(squares, axis=0) * (1.0 / 64))
+        scale = 1.0 / (EPS + scale)
+        for k in range(4):
+            for half in range(2):
+                unit = 16 * k + 2 * g + half
+                s_ref[unit] = (xs[k][half] * scale[2 * k + half:2 * k + half + 1]).astype(BF16)
         return carry
 
-    lax.fori_loop(0, 32, project, 0, unroll=4)
+    lax.fori_loop(0, 8, project, 0)
+
+    def weigh(h, b, slot):
+        at = slice(256 * b, 256 * b + 256)
+        scores = lax.dot_general(s_ref[21 + h, :, at], s_ref[h, :, at], TN,
+                                 preferred_element_type=F32)
+        expo = jnp.exp2(scores * (0.125 * LOG2E))
+        e_ref[slot] = expo.astype(BF16)
+        d_ref[slot] = jnp.sum(expo.reshape(32, 8, 256), axis=0)
+
+    def gather(h, b, slot):
+        at = slice(256 * b, 256 * b + 256)
+        out = jnp.dot(s_ref[42 + h, :, at], e_ref[slot], preferred_element_type=F32)
+        total = jnp.sum(d_ref[slot], axis=0, keepdims=True)
+        a_ref[pl.ds(pl.multiple_of(h * 64, 64), 64), at] = (out * (1.0 / total)).astype(BF16)
+
+    weigh(0, 0, 0)
 
     def head(h, carry):
-        for b in range(2):
-            at = slice(256 * b, 256 * b + 256)
-            query, keys, values = s_ref[h, :, at], s_ref[21 + h, :, at], s_ref[42 + h, :, at]
-            scores = lax.dot_general(keys, query, TN, preferred_element_type=F32)
-            expo = jnp.exp2(scores * (0.125 * LOG2E))
-            total = jnp.sum(expo, axis=0, keepdims=True)
-            out = jnp.dot(values, expo.astype(BF16), preferred_element_type=F32)
-            a_ref[pl.ds(pl.multiple_of(h * 64, 64), 64), at] = (out * (1.0 / total)).astype(BF16)
+        weigh(h, 1, 1)
+        gather(h, 0, 0)
+        weigh(jnp.minimum(h + 1, 20), 0, 0)
+        gather(h, 1, 1)
         return carry
 
-    lax.fori_loop(0, 21, head, 0, unroll=3)
+    lax.fori_loop(0, 21, head, 0, unroll=1)
 
 
 def attend(tokens, got):
     return pl.pallas_call(
         attend_kernel,
         out_shape=jax.ShapeDtypeStruct((1344, 512), BF16),
-        scratch_shapes=[pltpu.VMEM((64, 64, 512), BF16)],
+        scratch_shapes=[pltpu.VMEM((64, 64, 512), BF16), pltpu.VMEM((2, 256, 256), BF16),
+                        pltpu.VMEM((2, 8, 256), F32)],
         name="attend",
         compiler_params=pltpu.CompilerParams(vmem_limit_bytes=16 << 20),
         cost_estimate=pl.CostEstimate(flops=5000000000, bytes_accessed=2400000, transcendentals=2800000),
     )(tokens, got)
 
 
-def output_kernel(t_ref, b_ref, a_ref, r_ref, s_out_ref, o_ref, z_ref):
+def output_kernel(t_ref, b_ref, a_ref, r_ref, s_out_ref, own_ref, other_ref, z_ref):
     tokens = jnp.concatenate([t_ref[0], t_ref[1]], axis=1)
     feature = 0.3 * lax.dot_general(r_ref[...], a_ref[...], TN, preferred_element_type=F32)
     n = jnp.concatenate([b_ref[4 * z, 64:72, 0:64].astype(F32) for z in range(8)], axis=0)
@@ -231,13 +293,15 @@
             wide = jnp.sum(wide, axis=1)
             z_ref[2 * b, pl.ds(i, 16, stride=4), :] = wide[:, :128]
             z_ref[2 * b + 1, pl.ds(i, 16, stride=4), :] = wide[:, 128:]
-        o_ref[b] = jnp.concatenate([z_ref[2 * b], z_ref[2 * b + 1]], axis=1)
+    mine = lax.axis_index("xl")
+    for ref, b in ((own_ref, mine), (other_ref, 1 - mine)):
+        ref[...] = jnp.concatenate([z_ref[2 * b], z_ref[2 * b + 1]], axis=1)
 
 
 def output(tokens, got, attended, r, scale):
     return pl.pallas_call(
         output_kernel,
-        out_shape=jax.ShapeDtypeStruct((2, 64, 256), F32),
+        out_shape=(jax.ShapeDtypeStruct((64, 256), F32),) * 2,
         scratch_shapes=[pltpu.VMEM((4, 64, 128), F32)],
         name="output",
         compiler_params=pltpu.CompilerParams(vmem_limit_bytes=12 << 20),
@@ -246,29 +310,27 @@
 
 
 def shards(snap_in, snap_qkv, snap_proj, snap_out, coeffs, latent, levels):
-    y = lax.axis_index("y")
-    part = contract(
+    swap = [(0, 1), (1, 0)]
+    keep, give = contract(
         coeffs,
         snap_qkv.transpose(1, 0, 2).reshape(168, 4032),
         snap_proj.transpose(1, 0, 2).reshape(168, 1344),
         snap_in.transpose(2, 0, 1).reshape(168, 64),
         snap_out.transpose(1, 0, 2).reshape(168, 64),
     )
-    part = a2a(part, "core").astype(F32)
-    part = (part[0] + part[1]).astype(BF16)
+    part = pair_sum(keep, lax.ppermute(give, "core", swap))
     part = a2a(part, ("xh", "xl", "y"))
-    send, proj = partial_products(y.astype(jnp.int32).reshape(1), part)
+    send, proj = partial_products(part)
     send, side = whole_products(a2a(send, "z"), proj)
+    send, latent, levels = lax.optimization_barrier((send, latent, levels))
     got = a2a(send, ZY)
 
-    total = lax.dynamic_index_in_dim(side, y, 0, False).astype(F32)
+    total = side[0].astype(F32)
     for d in range(1, 4):
-        there = lax.dynamic_index_in_dim(side, lax.rem(y + d, 4), 0, False)
-        there = lax.ppermute(there, "y", [(k, (k + d) % 4) for k in range(4)])
-        total = total + there.astype(F32)
+        total = total + lax.ppermute(side[d], "y", [(k, (k + d) % 4) for k in range(4)]).astype(F32)
     scale = 1.0 / (EPS + jnp.sqrt(total[24, :64] + total[25, :64]))
-    total, _ = lax.optimization_barrier((total, got))
     r = jnp.broadcast_to(total[None, :24].astype(BF16), (32, 24, 128))
+    r, _ = lax.optimization_barrier((r, got))
     r = a2a(r, ZY)[:, :21]
     r = jnp.concatenate([r[:, :, :64], r[:, :, 64:]], axis=0).reshape(1344, 64)
 
@@ -277,7 +339,10 @@
     tokens = tokens.reshape(16, 4, 16, 16).transpose(1, 3, 0, 2).reshape(1, 64, 256)
     tokens = lax.all_gather(tokens, "xl", axis=0, tiled=True)
     attended = attend(tokens, got)
-    feature = a2a(output(tokens, got, attended, r, scale[:, None]), "xl")
+    own, other = output(tokens, got, attended, r, scale[:, None])
+    other = lax.ppermute(other, "xl", swap)
+    first = lax.axis_index("xl") == 0
+    feature = jnp.stack([jnp.where(first, own, other), jnp.where(first, other, own)])
     out = c_skip[:, None, None] * latent + c_out[:, None, None] * feature
     return out[:, None]
 

time: 112 us -> 98.5 us (0.88)
  blocking collectives: 28.4 us -> 47.3 us
  waiting for transfers between devices: 26.2 us -> 12.1 us
  starting transfers between devices: 26.3 us -> 15.7 us
  local copies, waits for them, and re-layouts: 7.21 us -> 1.79 us
  other arithmetic: 2.77 us -> 0.8 us
    all_to_all x4 -> x2, waiting for transfers between devices: 26.2 us -> 5.12 us  [a2a(): return lax.all_to_all(x, axis, 0, 0, tiled=True)]
    all_to_all x2, blocking collectives: 23.8 us -> 42.8 us  [a2a(): return lax.all_to_all(x, axis, 0, 0, tiled=True)]
    all_to_all x4 -> x2, starting transfers between devices: 21.5 us -> 10.7 us  [a2a(): return lax.all_to_all(x, axis, 0, 0, tiled=True)]
    ppermute x3 -> x5, waiting for transfers between devices: 0.01 us -> 6.96 us  [the longest x1 4.12 us: shards(): other = lax.ppermute(other, 'xl', swap)]
    unnamed x12 -> x2, local copies, waits for them, and re-layouts: 5.43 us -> 0.01 us
    convert_element_type x2 -> x0, other arithmetic: 1.97 us -> none  [the longest x1 1.34 us: shards(): part = (part[0] + part[1]).astype(BF16)]
    pallas_call x1, Pallas kernels: 13.1 us -> 11.9 us  [attend(): pl.pallas_call(attend_kernel, out_shape=jax.ShapeDtypeStruct((1344, 512),...]
    pallas_call x2 -> x3, Pallas kernels: 4.98 us -> 5.92 us  [the longest x1 4.7 us: contract(): pl.pallas_call(contract_kernel, out_shape=(shape, shape), in_specs=[HBM]...]
where the time goes in v4:
time: 98.5 us; the launch traced here: 98.2 us
  blocking collectives  47.3 us (48%)
  Pallas kernels  19.4 us (20%)
  starting transfers between devices  15.7 us (16%)
  waiting for transfers between devices  12.1 us (12%)
  local copies, waits for them, and re-layouts  1.79 us (2%)
  between operations  1.03 us (1%)
    all_to_all x2, blocking collectives, a2a(): return lax.all_to_all(x, axis, 0, 0, tiled=True)  42.8 us
    pallas_call x1, Pallas kernels, attend(): pl.pallas_call(attend_kernel, out_shape=jax.ShapeDtypeStruct((1344, 512),...  11.9 us
    all_to_all x2, starting transfers between devices, a2a(): return lax.all_to_all(x, axis, 0, 0, tiled=True)  10.7 us
    all_to_all x2, waiting for transfers between devices, a2a(): return lax.all_to_all(x, axis, 0, 0, tiled=True)  5.12 us
    ppermute x3, starting transfers between devices, shards(): lax.ppermute(side[d], 'y', [(k, (k + d) % 4) for k in range(4)]).astype(F32)  4.79 us
    pallas_call x1, Pallas kernels, contract(): pl.pallas_call(contract_kernel, out_shape=(shape, shape), in_specs=[HBM]...  4.7 us
    all_gather x1, blocking collectives, shards(): tokens = lax.all_gather(tokens, 'xl', axis=0, tiled=True)  4.57 us
    ppermute x1, waiting for transfers between devices, shards(): other = lax.ppermute(other, 'xl', swap)  4.12 us
  transfers between devices with their start and end apart: 7, of which 3 were waited for; matrix products, arithmetic and copies ran while one was open for 1% of the time, Pallas kernels for 12%

profile of v4, /device:TPU:8, one launch (start us, length us, event | category | flops | bytes accessed | tf_op | source)
XLA Modules:
  0.0 98.2 jit_solution(17767306554747775313)
XLA Ops:
  0.0 4.7 %contract.1 = (bf16[16,24,1536]{2,1,0:T(8,128)(2,1)S(1)}, bf16[16,24,1536]{2,1,0:T(8,128)(2,1)S(1)}) custom-call(f32[8,8]{1,0:T(8,128)} %c_hbm.1, f32[168,4032]{1,0:T(8,128)} %bitcast.36, f32[168,1344]{1,0:T(8,128)} %bitcast.37, f32[168,64]{1,0:T(8,128)} %bitcast.38, f32[168,64]{1,0:T(8,128)} %bitcast.39), custom_call_target="tpu_custom_call" | custom-call | flops 1065222144 | bytes 6000000 | tf_op jit(solution)/shard_map/contract/pallas_call | solution.py:104
  4.7 0.1 collective-permute-start
  4.8 2.8 %collective-permute-done.b_ref = bf16[16,24,1536]{2,1,0:T(8,128)(2,1)S(1)} collective-permute-done((bf16[16,24,1536]{2,1,0:T(8,128)(2,1)S(1)}, bf16[16,24,1536]{2,1,0:T(8,128)(2,1)S(1)}, u32[]{:S(2)}, u32[]{:S(2)}) %collective-permute-start) | collective-permute-done | bytes 1179680 | tf_op jit(solution)/shard_map/ppermute | solution.py:321
  7.6 0.3 pair.1
  7.9 24.4 %all_to_all.20.g_ref = bf16[16,24,1536]{2,1,0:T(8,128)(2,1)S(1)} all-to-all(bf16[16,24,1536]{2,1,0:T(8,128)(2,1)S(1)} %pair.1), channel_id=1, replica_groups=mesh['xh'=2,'core'=2,'xl'=2,'z'=8,'y'=4] {'xh','xl','y'}, dimensions={0} | all-to-all | bytes 2359296 | tf_op jit(solution)/shard_map/all_to_all | solution.py:31
  32.3 0.5 partial.1
  32.8 0.0 copy-start
  32.8 18.4 %all_to_all.21.g_ref = bf16[8,104,128]{2,1,0:T(8,128)(2,1)S(1)} all-to-all(bf16[8,104,128]{2,1,0:T(8,128)(2,1)S(1)} %get-tuple-element.19), channel_id=1, replica_groups=mesh['xh'=2,'core'=2,'xl'=2,'z'=8,'y'=4] {'z'}, dimensions={0} | all-to-all | bytes 425984 | tf_op jit(solution)/shard_map/all_to_all | solution.py:31
  51.2 1.1 %whole.1 = (bf16[32,72,128]{2,1,0:T(8,128)(2,1)}, bf16[4,32,128]{2,1,0:T(8,128)(2,1)S(1)}) custom-call(bf16[8,104,128]{2,1,0:T(8,128)(2,1)S(1)} %all_to_all.21.g_ref, f32[192,384]{1,0:T(8,128)S(1)} %get-tuple-element.20.p_ref), custom_call_target="tpu_custom_call" | custom-call | flops 100000 | bytes 800000 | tf_op jit(solution)/shard_map/whole/pallas_call | solution.py:206
  52.3 5.1 %all-to-all-start.2 = ((bf16[32,72,128]{2,1,0:T(8,128)(2,1)}), bf16[32,72,128]{2,1,0:T(8,128)(2,1)S(1)}, u32[]{:S(2)}, u32[]{:S(2)}) async-start(bf16[32,72,128]{2,1,0:T(8,128)(2,1)} %get-tuple-element.24), calls=%async_computation.2 | async-start | bytes 1179648 | tf_op jit(solution)/shard_map/all_to_all | solution.py:31
  58.2 0.2 reshape.102
  58.5 0.3 copy.12
  58.7 0.2 reshape.103
  59.0 0.4 collective-permute-start.3
  59.4 2.6 %collective-permute-start.2 = (bf16[32,128]{1,0:T(8,128)(2,1)S(1)}, bf16[32,128]{1,0:T(8,128)(2,1)S(1)}, u32[]{:S(2)}, u32[]{:S(2)}) collective-permute-start(bf16[32,128]{1,0:T(8,128)(2,1)S(1)} %get-tuple-element.37), channel_id=1, source_target_pairs={{0,2},{1,3},{2,0},{3,1},{4,6},{5,7},{6,4},{7,5},{8,10},{9,11},{10,... | collective-permute-start | bytes 24584 | tf_op jit(solution)/shard_map/ppermute | solution.py:330
  62.0 1.8 %collective-permute-start.1 = (bf16[32,128]{1,0:T(8,128)(2,1)S(1)}, bf16[32,128]{1,0:T(8,128)(2,1)S(1)}, u32[]{:S(2)}, u32[]{:S(2)}) collective-permute-start(bf16[32,128]{1,0:T(8,128)(2,1)S(1)} %get-tuple-element.35), channel_id=1, source_target_pairs={{0,1},{1,2},{2,3},{3,0},{4,5},{5,6},{6,7},{7,4},{8,9},{9,10},{10,1... | collective-permute-start | bytes 24584 | tf_op jit(solution)/shard_map/ppermute | solution.py:330
  63.8 4.6 %all_gather.3.t_ref = bf16[2,64,256]{2,1,0:T(8,128)(2,1)S(1)} all-gather(bf16[1,64,256]{2,1,0:T(8,128)(2,1)S(1)} %reshape.103), channel_id=1, replica_groups=mesh['xh'=2,'core'=2,'xl'=2,'z'=8,'y'=4] {'xl'}, dimensions={0}, use_global_device_ids=true | all-gather | bytes 98304 | tf_op jit(solution)/shard_map/all_gather | solution.py:340
  68.4 0.0 collective-permute-done.3
  68.4 0.0 collective-permute-done.2
  68.4 0.0 collective-permute-done.1
  68.4 0.1 copy.13.s_out_ref
  68.5 5.1 %all-to-all-done.2.b_ref = bf16[32,72,128]{2,1,0:T(8,128)(2,1)S(1)} async-done(((bf16[32,72,128]{2,1,0:T(8,128)(2,1)}), bf16[32,72,128]{2,1,0:T(8,128)(2,1)S(1)}, u32[]{:S(2)}, u32[]{:S(2)}) %all-to-all-start.2) | async-done | bytes 589856 | tf_op jit(solution)/shard_map/all_to_all | solution.py:31
  73.6 0.7 broadcast_in_dim.2
  74.3 5.6 %all-to-all-start.3 = ((bf16[32,24,128]{2,1,0:T(8,128)(2,1)}), bf16[32,24,128]{2,1,0:T(8,128)(2,1)S(1)}, u32[]{:S(2)}, u32[]{:S(2)}) async-start(bf16[32,24,128]{2,1,0:T(8,128)(2,1)} %broadcast_in_dim.2), calls=%async_computation.3 | async-start | bytes 393216 | tf_op jit(solution)/shard_map/all_to_all | solution.py:31
  79.9 11.9 %attend.1.a_ref = bf16[1344,512]{1,0:T(8,128)(2,1)S(1)} custom-call(bf16[2,64,256]{2,1,0:T(8,128)(2,1)S(1)} %all_gather.3.t_ref, bf16[32,72,128]{2,1,0:T(8,128)(2,1)S(1)} %all-to-all-done.2.b_ref), custom_call_target="tpu_custom_call" | custom-call | flops 5000000000 | bytes 2400000 | tf_op jit(solution)/shard_map/attend/pallas_call | solution.py:262
  91.8 0.1 fusion.4
  91.9 0.1 pad_maximum_fusion
  92.0 0.1 reshape.104.r_ref
  92.2 1.0 output.1
  93.1 0.2 collective-permute-start.4
  93.4 4.1 %collective-permute-done.4 = f32[64,256]{1,0:T(8,128)S(1)} collective-permute-done((f32[64,256]{1,0:T(8,128)S(1)}, f32[64,256]{1,0:T(8,128)S(1)}, u32[]{:S(2)}, u32[]{:S(2)}) %collective-permute-start.4) | collective-permute-done | bytes 65568 | tf_op jit(solution)/shard_map/ppermute | solution.py:343
  97.5 0.7 fusion
  (8 shorter events, 0.1 us)
Async XLA Ops:
  4.7 2.9 %collective-permute-start = (bf16[16,24,1536]{2,1,0:T(8,128)(2,1)S(1)}, bf16[16,24,1536]{2,1,0:T(8,128)(2,1)S(1)}, u32[]{:S(2)}, u32[]{:S(2)}) collective-permute-start(bf16[16,24,1536]{2,1,0:T(8,128)(2,1)S(1)} %get-tuple-element.18), channel_id=1, source_target_pairs={{0,64},{64,0},{1,65},{65,1},{2,66},{66,2},{3,67},{67,3},{4,68},{68... | collective-permute-start | bytes 3538952 | tf_op jit(solution)/shard_map/ppermute | solution.py:321
  32.8 25.4 %copy-start = (f32[1,64,256]{2,1,0:T(8,128)S(1)}, f32[1,64,256]{2,1,0:T(8,128)}, u32[]{:S(2)}) copy-start(f32[1,64,256]{2,1,0:T(8,128)} %param.12) | copy-start | bytes 196612
  52.3 21.3 %all-to-all-start.2 = ((bf16[32,72,128]{2,1,0:T(8,128)(2,1)}), bf16[32,72,128]{2,1,0:T(8,128)(2,1)S(1)}, u32[]{:S(2)}, u32[]{:S(2)}) async-start(bf16[32,72,128]{2,1,0:T(8,128)(2,1)} %get-tuple-element.24), calls=%async_computation.2 | async-start | bytes 1179648 | tf_op jit(solution)/shard_map/all_to_all | solution.py:31
  59.0 9.4 %collective-permute-start.3 = (bf16[32,128]{1,0:T(8,128)(2,1)S(1)}, bf16[32,128]{1,0:T(8,128)(2,1)S(1)}, u32[]{:S(2)}, u32[]{:S(2)}) collective-permute-start(bf16[32,128]{1,0:T(8,128)(2,1)S(1)} %get-tuple-element.36), channel_id=1, source_target_pairs={{0,3},{1,0},{2,1},{3,2},{4,7},{5,4},{6,5},{7,6},{8,11},{9,8},{10,9... | collective-permute-start | bytes 24584 | tf_op jit(solution)/shard_map/ppermute | solution.py:330
  59.4 8.9 %collective-permute-start.2 = (bf16[32,128]{1,0:T(8,128)(2,1)S(1)}, bf16[32,128]{1,0:T(8,128)(2,1)S(1)}, u32[]{:S(2)}, u32[]{:S(2)}) collective-permute-start(bf16[32,128]{1,0:T(8,128)(2,1)S(1)} %get-tuple-element.37), channel_id=1, source_target_pairs={{0,2},{1,3},{2,0},{3,1},{4,6},{5,7},{6,4},{7,5},{8,10},{9,11},{10,... | collective-permute-start | bytes 24584 | tf_op jit(solution)/shard_map/ppermute | solution.py:330
  62.0 6.4 %collective-permute-start.1 = (bf16[32,128]{1,0:T(8,128)(2,1)S(1)}, bf16[32,128]{1,0:T(8,128)(2,1)S(1)}, u32[]{:S(2)}, u32[]{:S(2)}) collective-permute-start(bf16[32,128]{1,0:T(8,128)(2,1)S(1)} %get-tuple-element.35), channel_id=1, source_target_pairs={{0,1},{1,2},{2,3},{3,0},{4,5},{5,6},{6,7},{7,4},{8,9},{9,10},{10,1... | collective-permute-start | bytes 24584 | tf_op jit(solution)/shard_map/ppermute | solution.py:330
  74.3 17.5 %all-to-all-start.3 = ((bf16[32,24,128]{2,1,0:T(8,128)(2,1)}), bf16[32,24,128]{2,1,0:T(8,128)(2,1)S(1)}, u32[]{:S(2)}, u32[]{:S(2)}) async-start(bf16[32,24,128]{2,1,0:T(8,128)(2,1)} %broadcast_in_dim.2), calls=%async_computation.3 | async-start | bytes 393216 | tf_op jit(solution)/shard_map/all_to_all | solution.py:31
  93.1 4.4 %collective-permute-start.4 = (f32[64,256]{1,0:T(8,128)S(1)}, f32[64,256]{1,0:T(8,128)S(1)}, u32[]{:S(2)}, u32[]{:S(2)}) collective-permute-start(f32[64,256]{1,0:T(8,128)S(1)} %get-tuple-element.28), channel_id=1, source_target_pairs={{0,32},{32,0},{1,33},{33,1},{2,34},{34,2},{3,35},{35,3},{4,36},{36... | collective-permute-start | bytes 196616 | tf_op jit(solution)/shard_map/ppermute | solution.py:343

commit v5 on v4

--- a/solution.py
+++ b/solution.py
@@ -33,11 +33,11 @@
 
 def contract_kernel(c_hbm, q_hbm, p_hbm, i_hbm, o_hbm, keep_ref, give_ref, q_ref, p_ref, i_ref,
                     o_ref, h_ref, c_ref, sems):
-    copies = [pltpu.make_async_copy(a, b, sems.at[k]) for k, (a, b) in enumerate(
-        ((i_hbm, i_ref), (o_hbm, o_ref), (p_hbm, p_ref), (q_hbm, q_ref), (c_hbm, c_ref)))]
-    for k in (4, 0, 1, 2, 3):
-        copies[k].start()
-    copies[4].wait()
+    pairs = [(c_hbm, c_ref), (i_hbm, i_ref), (o_hbm, o_ref), (p_hbm, p_ref), (q_hbm, q_ref)]
+    copies = [pltpu.make_async_copy(a, b, sems.at[k]) for k, (a, b) in enumerate(pairs)]
+    for copy in copies:
+        copy.start()
+    copies[0].wait()
     snap = lax.broadcasted_iota(jnp.int32, (8, 168), 0)
     col = lax.broadcasted_iota(jnp.int32, (8, 168), 1)
     pick = jnp.where(lax.rem(col, 8) == snap, 1.0, 0.0)
@@ -72,10 +72,10 @@
                 for block in blocks:
                     ref[4 * slot + block, :, at:at + width] = y[row:row + 24]
 
-    copies[0].wait()
     copies[1].wait()
+    copies[2].wait()
     store(piece(jnp.concatenate([i_ref[...], o_ref[...]], axis=1)), range(4), 1408)
-    copies[2].wait()
+    copies[3].wait()
     for start, width in ((0, 512), (512, 512), (1024, 320)):
         h_ref[:, start:start + width] = piece(p_ref[:, start:start + width])
     source = lax.broadcasted_iota(jnp.int32, (1344, 384), 0)
@@ -86,8 +86,9 @@
         order = jnp.where(source == want, 1.0, 0.0).astype(BF16)
         y = jnp.dot(h_ref[...], order, preferred_element_type=F32).astype(BF16)
         store(y, (block,), 1024)
-    copies[3].wait()
     for k in range(8):
+        if k == 0:
+            copies[4].wait()
         width = 512 if k < 7 else 448
         store(piece(q_ref[:, 512 * k:512 * k + width]), (k // 2,), 512 * (k % 2))
     for slot in range(4):
@@ -181,12 +182,13 @@
     )(got)
 
 
-def whole_kernel(g_ref, p_ref, o_ref, r_ref):
+def whole_kernel(g_ref, p_ref, o_ref, r_ref, n_ref):
     total = g_ref[0].astype(F32)
     for z in range(1, 8):
         total = total + g_ref[z].astype(F32)
     m = total[0:64] / (EPS + jnp.sqrt(unlines(total[64:72, 64:128], 2)))
-    out = jnp.concatenate([m, total[64:72]], axis=0).astype(BF16)
+    n_ref[...] = total[64:72]
+    out = m.astype(BF16)
     for k in range(32):
         o_ref[k] = out
     w_out = g_ref[:, 72:96, :].astype(F32).reshape(192, 128)
@@ -205,16 +207,37 @@
 def whole_products(got, proj):
     return pl.pallas_call(
         whole_kernel,
-        out_shape=(jax.ShapeDtypeStruct((32, 72, 128), BF16),
-                   jax.ShapeDtypeStruct((4, 32, 128), BF16)),
+        out_shape=(jax.ShapeDtypeStruct((32, 64, 128), BF16),
+                   jax.ShapeDtypeStruct((4, 32, 128), BF16),
+                   jax.ShapeDtypeStruct((8, 128), F32)),
         name="whole",
         compiler_params=pltpu.CompilerParams(vmem_limit_bytes=8 << 20),
         cost_estimate=pl.CostEstimate(flops=100000, bytes_accessed=800000, transcendentals=0),
     )(got, proj)
 
 
-def attend_kernel(t_ref, b_ref, a_ref, s_ref, e_ref, d_ref):
-    tokens = jnp.concatenate([t_ref[0], t_ref[1]], axis=1)
+def spread_kernel(a_ref, b_ref, c_ref, d_ref, n_ref, o_ref):
+    total = a_ref[0].astype(F32)
+    for ref in (b_ref, c_ref, d_ref):
+        total = total + ref[...].astype(F32)
+    scale = 1.0 / (EPS + jnp.sqrt(total[24:25] + total[25:26]))
+    out = jnp.concatenate([total[:24] * scale, n_ref[...] * scale], axis=0).astype(BF16)
+    for k in range(32):
+        o_ref[k] = out
+
+
+def spread(side, parts, n):
+    return pl.pallas_call(
+        spread_kernel,
+        out_shape=jax.ShapeDtypeStruct((32, 32, 128), BF16),
+        name="spread",
+        compiler_params=pltpu.CompilerParams(vmem_limit_bytes=4 << 20),
+        cost_estimate=pl.CostEstimate(flops=20000, bytes_accessed=300000, transcendentals=0),
+    )(side, *parts, n)
+
+
+def attend_kernel(t_ref, u_ref, b_ref, a_ref, s_ref, e_ref, d_ref):
+    tokens = jnp.concatenate([t_ref[...], u_ref[...]], axis=1)
 
     def project(g, carry):
         xs = []
@@ -258,7 +281,7 @@
     lax.fori_loop(0, 21, head, 0, unroll=1)
 
 
-def attend(tokens, got):
+def attend(tokens, others, got):
     return pl.pallas_call(
         attend_kernel,
         out_shape=jax.ShapeDtypeStruct((1344, 512), BF16),
@@ -267,15 +290,14 @@
         name="attend",
         compiler_params=pltpu.CompilerParams(vmem_limit_bytes=16 << 20),
         cost_estimate=pl.CostEstimate(flops=5000000000, bytes_accessed=2400000, transcendentals=2800000),
-    )(tokens, got)
-
-
-def output_kernel(t_ref, b_ref, a_ref, r_ref, s_out_ref, own_ref, other_ref, z_ref):
-    tokens = jnp.concatenate([t_ref[0], t_ref[1]], axis=1)
+    )(tokens, others, got)
+
+
+def output_kernel(t_ref, u_ref, a_ref, r_ref, n_ref, own_ref, other_ref, z_ref):
+    tokens = jnp.concatenate([t_ref[...], u_ref[...]], axis=1)
     feature = 0.3 * lax.dot_general(r_ref[...], a_ref[...], TN, preferred_element_type=F32)
-    n = jnp.concatenate([b_ref[4 * z, 64:72, 0:64].astype(F32) for z in range(8)], axis=0)
-    feature = feature + 0.7 * lax.dot_general(n.astype(BF16), tokens, TN, preferred_element_type=F32)
-    feature = feature * (s_out_ref[...] * (1.0 / (0.58 ** 0.5)))
+    feature = feature + 0.7 * lax.dot_general(n_ref[...], tokens, TN, preferred_element_type=F32)
+    feature = feature * (1.0 / (0.58 ** 0.5))
     token = lax.broadcasted_iota(jnp.int32, (256, 256), 0)
     lane = lax.broadcasted_iota(jnp.int32, (256, 256), 1)
     keep = lax.rem(token, 16) == lane // 16
@@ -293,20 +315,19 @@
             wide = jnp.sum(wide, axis=1)
             z_ref[2 * b, pl.ds(i, 16, stride=4), :] = wide[:, :128]
             z_ref[2 * b + 1, pl.ds(i, 16, stride=4), :] = wide[:, 128:]
-    mine = lax.axis_index("xl")
-    for ref, b in ((own_ref, mine), (other_ref, 1 - mine)):
-        ref[...] = jnp.concatenate([z_ref[2 * b], z_ref[2 * b + 1]], axis=1)
-
-
-def output(tokens, got, attended, r, scale):
+    own_ref[...] = jnp.concatenate([z_ref[0], z_ref[1]], axis=1)
+    other_ref[...] = jnp.concatenate([z_ref[2], z_ref[3]], axis=1).astype(BF16)
+
+
+def output(tokens, others, attended, r, n):
     return pl.pallas_call(
         output_kernel,
-        out_shape=(jax.ShapeDtypeStruct((64, 256), F32),) * 2,
+        out_shape=(jax.ShapeDtypeStruct((64, 256), F32), jax.ShapeDtypeStruct((64, 256), BF16)),
         scratch_shapes=[pltpu.VMEM((4, 64, 128), F32)],
         name="output",
         compiler_params=pltpu.CompilerParams(vmem_limit_bytes=12 << 20),
         cost_estimate=pl.CostEstimate(flops=100000000, bytes_accessed=2000000, transcendentals=0),
-    )(tokens, got, attended, r, scale)
+    )(tokens, others, attended, r, n)
 
 
 def shards(snap_in, snap_qkv, snap_proj, snap_out, coeffs, latent, levels):
@@ -321,26 +342,24 @@
     part = pair_sum(keep, lax.ppermute(give, "core", swap))
     part = a2a(part, ("xh", "xl", "y"))
     send, proj = partial_products(part)
-    send, side = whole_products(a2a(send, "z"), proj)
+    send, side, n = whole_products(a2a(send, "z"), proj)
     send, latent, levels = lax.optimization_barrier((send, latent, levels))
     got = a2a(send, ZY)
 
-    total = side[0].astype(F32)
-    for d in range(1, 4):
-        total = total + lax.ppermute(side[d], "y", [(k, (k + d) % 4) for k in range(4)]).astype(F32)
-    scale = 1.0 / (EPS + jnp.sqrt(total[24, :64] + total[25, :64]))
-    r = jnp.broadcast_to(total[None, :24].astype(BF16), (32, 24, 128))
-    r, _ = lax.optimization_barrier((r, got))
-    r = a2a(r, ZY)[:, :21]
-    r = jnp.concatenate([r[:, :, :64], r[:, :, 64:]], axis=0).reshape(1344, 64)
-
     c_in, c_skip, c_out = noise_scales(levels)
     tokens = (c_in[:, None, None] * latent).astype(BF16)
-    tokens = tokens.reshape(16, 4, 16, 16).transpose(1, 3, 0, 2).reshape(1, 64, 256)
-    tokens = lax.all_gather(tokens, "xl", axis=0, tiled=True)
-    attended = attend(tokens, got)
-    own, other = output(tokens, got, attended, r, scale[:, None])
-    other = lax.ppermute(other, "xl", swap)
+    tokens = tokens.reshape(16, 4, 16, 16).transpose(1, 3, 0, 2).reshape(64, 256)
+    others = lax.ppermute(tokens, "xl", swap)
+    parts = [lax.ppermute(side[d], "y", [(k, (k + d) % 4) for k in range(4)]) for d in range(1, 4)]
+    r = spread(side, parts, n)
+    r, others, _ = lax.optimization_barrier((r, others, got))
+    r = a2a(r, ZY)
+    n = r.reshape(8, 4, 32, 128)[:, 0, 24:, :64].reshape(64, 64)
+    r = jnp.concatenate([r[:, :21, :64], r[:, :21, 64:]], axis=0).reshape(1344, 64)
+
+    attended = attend(tokens, others, got)
+    own, other = output(tokens, others, attended, r, n)
+    other = lax.ppermute(other, "xl", swap).astype(F32)
     first = lax.axis_index("xl") == 0
     feature = jnp.stack([jnp.where(first, own, other), jnp.where(first, other, own)])
     out = c_skip[:, None, None] * latent + c_out[:, None, None] * feature

time: 98.5 us -> 96.1 us (0.976)
  blocking collectives: 47.3 us -> 42.8 us
  starting transfers between devices: 15.7 us -> 17.6 us
    all_gather x1 -> x0, blocking collectives: 4.57 us -> none  [shards(): tokens = lax.all_gather(tokens, 'xl', axis=0, tiled=True)]
    ppermute x4 -> x5, starting transfers between devices: 4.98 us -> 6.81 us  [the longest x3 4.71 us: shards(): lax.ppermute(side[d], 'y', [(k, (k + d) % 4) for k in range(4)])]
    ppermute x4 -> x5, waiting for transfers between devices: 4.12 us -> 4.42 us  [the longest x1 2.42 us: shards(): other = lax.ppermute(other, 'xl', swap).astype(F32)]
  transfers between devices with their start and end apart: 7 -> 8, of which waited for: 3 -> 4; matrix products, arithmetic and copies ran while one was open for 1% -> 1% of each run, Pallas kernels for 12% -> 13%
where the time goes in v5:
time: 96.1 us; the launch traced here: 95.7 us
  blocking collectives  42.8 us (45%)
  Pallas kernels  20.1 us (21%)
  starting transfers between devices  17.6 us (18%)
  waiting for transfers between devices  12.5 us (13%)
  local copies, waits for them, and re-layouts  1.01 us (1%)
  between operations  1 us (1%)
    all_to_all x2, blocking collectives, a2a(): return lax.all_to_all(x, axis, 0, 0, tiled=True)  42.8 us
    pallas_call x1, Pallas kernels, attend(): pl.pallas_call(attend_kernel, out_shape=jax.ShapeDtypeStruct((1344, 512),...  11.9 us
    all_to_all x2, starting transfers between devices, a2a(): return lax.all_to_all(x, axis, 0, 0, tiled=True)  10.7 us
    all_to_all x2, waiting for transfers between devices, a2a(): return lax.all_to_all(x, axis, 0, 0, tiled=True)  5.2 us
    ppermute x3, starting transfers between devices, shards(): lax.ppermute(side[d], 'y', [(k, (k + d) % 4) for k in range(4)])  4.71 us
    pallas_call x1, Pallas kernels, contract(): pl.pallas_call(contract_kernel, out_shape=(shape, shape), in_specs=[HBM]...  4.7 us
    ppermute x1, waiting for transfers between devices, shards(): part = pair_sum(keep, lax.ppermute(give, 'core', swap))  2.83 us
    ppermute x1, waiting for transfers between devices, shards(): other = lax.ppermute(other, 'xl', swap).astype(F32)  2.42 us
  transfers between devices with their start and end apart: 8, of which 4 were waited for; matrix products, arithmetic and copies ran while one was open for 1% of the time, Pallas kernels for 13%

profile of v5, /device:TPU:8, one launch (start us, length us, event | category | flops | bytes accessed | tf_op | source)
XLA Modules:
  0.0 95.7 jit_solution(8782909350330610188)
XLA Ops:
  0.0 4.7 %contract.1 = (bf16[16,24,1536]{2,1,0:T(8,128)(2,1)S(1)}, bf16[16,24,1536]{2,1,0:T(8,128)(2,1)S(1)}) custom-call(f32[8,8]{1,0:T(8,128)} %c_hbm.1, f32[168,4032]{1,0:T(8,128)} %bitcast.37, f32[168,1344]{1,0:T(8,128)} %bitcast.38, f32[168,64]{1,0:T(8,128)} %bitcast.39, f32[168,64]{1,0:T(8,128)} %bitcast.40), custom_call_target="tpu_custom_call" | custom-call | flops 1065222144 | bytes 6000000 | tf_op jit(solution)/shard_map/contract/pallas_call | solution.py:105
  4.7 0.1 collective-permute-start
  4.8 2.8 %collective-permute-done.b_ref = bf16[16,24,1536]{2,1,0:T(8,128)(2,1)S(1)} collective-permute-done((bf16[16,24,1536]{2,1,0:T(8,128)(2,1)S(1)}, bf16[16,24,1536]{2,1,0:T(8,128)(2,1)S(1)}, u32[]{:S(2)}, u32[]{:S(2)}) %collective-permute-start) | collective-permute-done | bytes 1179680 | tf_op jit(solution)/shard_map/ppermute | solution.py:342
  7.6 0.3 pair.1
  7.9 24.4 %all_to_all.20.g_ref = bf16[16,24,1536]{2,1,0:T(8,128)(2,1)S(1)} all-to-all(bf16[16,24,1536]{2,1,0:T(8,128)(2,1)S(1)} %pair.1), channel_id=1, replica_groups=mesh['xh'=2,'core'=2,'xl'=2,'z'=8,'y'=4] {'xh','xl','y'}, dimensions={0} | all-to-all | bytes 2359296 | tf_op jit(solution)/shard_map/all_to_all | solution.py:31
  32.3 0.5 partial.1
  32.8 0.0 copy-start
  32.8 18.4 %all_to_all.21.g_ref = bf16[8,104,128]{2,1,0:T(8,128)(2,1)S(1)} all-to-all(bf16[8,104,128]{2,1,0:T(8,128)(2,1)S(1)} %get-tuple-element.21), channel_id=1, replica_groups=mesh['xh'=2,'core'=2,'xl'=2,'z'=8,'y'=4] {'z'}, dimensions={0} | all-to-all | bytes 425984 | tf_op jit(solution)/shard_map/all_to_all | solution.py:31
  51.2 1.1 %whole.1 = (bf16[32,64,128]{2,1,0:T(8,128)(2,1)}, bf16[4,32,128]{2,1,0:T(8,128)(2,1)S(1)}, f32[8,128]{1,0:T(8,128)S(1)}) custom-call(bf16[8,104,128]{2,1,0:T(8,128)(2,1)S(1)} %all_to_all.21.g_ref, f32[192,384]{1,0:T(8,128)S(1)} %get-tuple-element.22.p_ref), custom_call_target="tpu_custom_call" | custom-call | flops 100000 | bytes 800000 | tf_op jit(solution)/shard_map/whole/pallas_call | solution.py:208
  52.3 5.1 %all-to-all-start.2 = ((bf16[32,64,128]{2,1,0:T(8,128)(2,1)}), bf16[32,64,128]{2,1,0:T(8,128)(2,1)S(1)}, u32[]{:S(2)}, u32[]{:S(2)}) async-start(bf16[32,64,128]{2,1,0:T(8,128)(2,1)} %get-tuple-element.28), calls=%async_computation.2 | async-start | bytes 1048576 | tf_op jit(solution)/shard_map/all_to_all | solution.py:31
  58.2 0.2 reshape.69
  58.4 0.3 copy.10
  58.7 0.2 reshape.70.t_ref
  59.0 0.6 collective-permute-start.4
  59.5 1.5 %collective-permute-start.1 = (bf16[32,128]{1,0:T(8,128)(2,1)S(1)}, bf16[32,128]{1,0:T(8,128)(2,1)S(1)}, u32[]{:S(2)}, u32[]{:S(2)}) collective-permute-start(bf16[32,128]{1,0:T(8,128)(2,1)S(1)} %get-tuple-element.41), channel_id=1, source_target_pairs={{0,1},{1,2},{2,3},{3,0},{4,5},{5,6},{6,7},{7,4},{8,9},{9,10},{10,1... | collective-permute-start | bytes 24584 | tf_op jit(solution)/shard_map/ppermute | solution.py:353
  61.0 0.9 collective-permute-start.2
  62.0 2.3 %collective-permute-start.3 = (bf16[32,128]{1,0:T(8,128)(2,1)S(1)}, bf16[32,128]{1,0:T(8,128)(2,1)S(1)}, u32[]{:S(2)}, u32[]{:S(2)}) collective-permute-start(bf16[32,128]{1,0:T(8,128)(2,1)S(1)} %get-tuple-element.39), channel_id=1, source_target_pairs={{0,3},{1,0},{2,1},{3,2},{4,7},{5,4},{6,5},{7,6},{8,11},{9,8},{10,9... | collective-permute-start | bytes 24584 | tf_op jit(solution)/shard_map/ppermute | solution.py:353
  64.3 0.0 collective-permute-done.1.b_ref
  64.3 2.0 %collective-permute-done.2.c_ref = bf16[32,128]{1,0:T(8,128)(2,1)S(1)} collective-permute-done((bf16[32,128]{1,0:T(8,128)(2,1)S(1)}, bf16[32,128]{1,0:T(8,128)(2,1)S(1)}, u32[]{:S(2)}, u32[]{:S(2)}) %collective-permute-start.2) | collective-permute-done | bytes 8224 | tf_op jit(solution)/shard_map/ppermute | solution.py:353
  66.3 0.0 collective-permute-done.3.d_ref
  66.3 0.7 spread.1
  67.0 0.0 collective-permute-done.4.u_ref
  67.0 5.2 %all-to-all-done.2.b_ref = bf16[32,64,128]{2,1,0:T(8,128)(2,1)S(1)} async-done(((bf16[32,64,128]{2,1,0:T(8,128)(2,1)}), bf16[32,64,128]{2,1,0:T(8,128)(2,1)S(1)}, u32[]{:S(2)}, u32[]{:S(2)}) %all-to-all-start.2) | async-done | bytes 524320 | tf_op jit(solution)/shard_map/all_to_all | solution.py:31
  72.2 5.6 %all-to-all-start.3 = ((bf16[32,32,128]{2,1,0:T(8,128)(2,1)}), bf16[32,32,128]{2,1,0:T(8,128)(2,1)S(1)}, u32[]{:S(2)}, u32[]{:S(2)}) async-start(bf16[32,32,128]{2,1,0:T(8,128)(2,1)} %spread.1), calls=%async_computation.3 | async-start | bytes 524288 | tf_op jit(solution)/shard_map/all_to_all | solution.py:31
  77.8 11.9 %attend.1.a_ref = bf16[1344,512]{1,0:T(8,128)(2,1)S(1)} custom-call(bf16[64,256]{1,0:T(8,128)(2,1)S(1)} %reshape.70.t_ref, bf16[64,256]{1,0:T(8,128)(2,1)S(1)} %collective-permute-done.4.u_ref, bf16[32,64,128]{2,1,0:T(8,128)(2,1)S(1)} %all-to-all-done.2.b_ref), custom_call_target="tpu_custom_call" | custom-call | flops 5000000000 | bytes 2400000 | tf_op jit(solution)/shard_map/attend/pallas_call | solution.py:285
  89.7 0.1 fusion.3
  89.8 0.1 pad_maximum_fusion
  89.9 0.1 reshape.71.r_ref
  90.0 1.0 output.1
  91.0 1.5 %collective-permute-start.5 = (bf16[64,256]{1,0:T(8,128)(2,1)S(1)}, bf16[64,256]{1,0:T(8,128)(2,1)S(1)}, u32[]{:S(2)}, u32[]{:S(2)}) collective-permute-start(bf16[64,256]{1,0:T(8,128)(2,1)S(1)} %get-tuple-element.32), channel_id=1, source_target_pairs={{0,32},{32,0},{1,33},{33,1},{2,34},{34,2},{3,35},{35,3},{4,36},{36... | collective-permute-start | bytes 98312 | tf_op jit(solution)/shard_map/ppermute | solution.py:362
  92.6 2.4 %collective-permute-done.5 = bf16[64,256]{1,0:T(8,128)(2,1)S(1)} collective-permute-done((bf16[64,256]{1,0:T(8,128)(2,1)S(1)}, bf16[64,256]{1,0:T(8,128)(2,1)S(1)}, u32[]{:S(2)}, u32[]{:S(2)}) %collective-permute-start.5) | collective-permute-done | bytes 32800 | tf_op jit(solution)/shard_map/ppermute | solution.py:362
  95.0 0.7 fusion
  (6 shorter events, 0.0 us)
Async XLA Ops:
  4.7 2.9 %collective-permute-start = (bf16[16,24,1536]{2,1,0:T(8,128)(2,1)S(1)}, bf16[16,24,1536]{2,1,0:T(8,128)(2,1)S(1)}, u32[]{:S(2)}, u32[]{:S(2)}) collective-permute-start(bf16[16,24,1536]{2,1,0:T(8,128)(2,1)S(1)} %get-tuple-element.20), channel_id=1, source_target_pairs={{0,64},{64,0},{1,65},{65,1},{2,66},{66,2},{3,67},{67,3},{4,68},{68... | collective-permute-start | bytes 3538952 | tf_op jit(solution)/shard_map/ppermute | solution.py:342
  32.8 25.4 %copy-start = (f32[1,64,256]{2,1,0:T(8,128)S(1)}, f32[1,64,256]{2,1,0:T(8,128)}, u32[]{:S(2)}) copy-start(f32[1,64,256]{2,1,0:T(8,128)} %param.12) | copy-start | bytes 196612
  52.3 19.9 %all-to-all-start.2 = ((bf16[32,64,128]{2,1,0:T(8,128)(2,1)}), bf16[32,64,128]{2,1,0:T(8,128)(2,1)S(1)}, u32[]{:S(2)}, u32[]{:S(2)}) async-start(bf16[32,64,128]{2,1,0:T(8,128)(2,1)} %get-tuple-element.28), calls=%async_computation.2 | async-start | bytes 1048576 | tf_op jit(solution)/shard_map/all_to_all | solution.py:31
  59.0 8.0 %collective-permute-start.4 = (bf16[64,256]{1,0:T(8,128)(2,1)S(1)}, bf16[64,256]{1,0:T(8,128)(2,1)S(1)}, u32[]{:S(2)}, u32[]{:S(2)}) collective-permute-start(bf16[64,256]{1,0:T(8,128)(2,1)S(1)} %reshape.70.t_ref), channel_id=1, source_target_pairs={{0,32},{32,0},{1,33},{33,1},{2,34},{34,2},{3,35},{35,3},{4,36},{36... | collective-permute-start | bytes 98312 | tf_op jit(solution)/shard_map/ppermute | solution.py:352
  59.5 4.7 %collective-permute-start.1 = (bf16[32,128]{1,0:T(8,128)(2,1)S(1)}, bf16[32,128]{1,0:T(8,128)(2,1)S(1)}, u32[]{:S(2)}, u32[]{:S(2)}) collective-permute-start(bf16[32,128]{1,0:T(8,128)(2,1)S(1)} %get-tuple-element.41), channel_id=1, source_target_pairs={{0,1},{1,2},{2,3},{3,0},{4,5},{5,6},{6,7},{7,4},{8,9},{9,10},{10,1... | collective-permute-start | bytes 24584 | tf_op jit(solution)/shard_map/ppermute | solution.py:353
  61.0 5.2 %collective-permute-start.2 = (bf16[32,128]{1,0:T(8,128)(2,1)S(1)}, bf16[32,128]{1,0:T(8,128)(2,1)S(1)}, u32[]{:S(2)}, u32[]{:S(2)}) collective-permute-start(bf16[32,128]{1,0:T(8,128)(2,1)S(1)} %get-tuple-element.40), channel_id=1, source_target_pairs={{0,2},{1,3},{2,0},{3,1},{4,6},{5,7},{6,4},{7,5},{8,10},{9,11},{10,... | collective-permute-start | bytes 24584 | tf_op jit(solution)/shard_map/ppermute | solution.py:353
  62.0 4.3 %collective-permute-start.3 = (bf16[32,128]{1,0:T(8,128)(2,1)S(1)}, bf16[32,128]{1,0:T(8,128)(2,1)S(1)}, u32[]{:S(2)}, u32[]{:S(2)}) collective-permute-start(bf16[32,128]{1,0:T(8,128)(2,1)S(1)} %get-tuple-element.39), channel_id=1, source_target_pairs={{0,3},{1,0},{2,1},{3,2},{4,7},{5,4},{6,5},{7,6},{8,11},{9,8},{10,9... | collective-permute-start | bytes 24584 | tf_op jit(solution)/shard_map/ppermute | solution.py:353
  72.2 17.5 %all-to-all-start.3 = ((bf16[32,32,128]{2,1,0:T(8,128)(2,1)}), bf16[32,32,128]{2,1,0:T(8,128)(2,1)S(1)}, u32[]{:S(2)}, u32[]{:S(2)}) async-start(bf16[32,32,128]{2,1,0:T(8,128)(2,1)} %spread.1), calls=%async_computation.3 | async-start | bytes 524288 | tf_op jit(solution)/shard_map/all_to_all | solution.py:31
  91.0 4.0 %collective-permute-start.5 = (bf16[64,256]{1,0:T(8,128)(2,1)S(1)}, bf16[64,256]{1,0:T(8,128)(2,1)S(1)}, u32[]{:S(2)}, u32[]{:S(2)}) collective-permute-start(bf16[64,256]{1,0:T(8,128)(2,1)S(1)} %get-tuple-element.32), channel_id=1, source_target_pairs={{0,32},{32,0},{1,33},{33,1},{2,34},{34,2},{3,35},{35,3},{4,36},{36... | collective-permute-start | bytes 98312 | tf_op jit(solution)/shard_map/ppermute | solution.py:362

commit v6 on v5

--- a/solution.py
+++ b/solution.py
@@ -188,9 +188,7 @@
         total = total + g_ref[z].astype(F32)
     m = total[0:64] / (EPS + jnp.sqrt(unlines(total[64:72, 64:128], 2)))
     n_ref[...] = total[64:72]
-    out = m.astype(BF16)
-    for k in range(32):
-        o_ref[k] = out
+    o_ref[...] = m
     w_out = g_ref[:, 72:96, :].astype(F32).reshape(192, 128)
     w_out = jnp.concatenate([w_out[:, :64], w_out[:, 64:]], axis=0)
     norm = jnp.sqrt(unlines(total[96:104], 3))
@@ -207,7 +205,7 @@
 def whole_products(got, proj):
     return pl.pallas_call(
         whole_kernel,
-        out_shape=(jax.ShapeDtypeStruct((32, 64, 128), BF16),
+        out_shape=(jax.ShapeDtypeStruct((64, 128), F32),
                    jax.ShapeDtypeStruct((4, 32, 128), BF16),
                    jax.ShapeDtypeStruct((8, 128), F32)),
         name="whole",
@@ -216,77 +214,109 @@
     )(got, proj)
 
 
-def spread_kernel(a_ref, b_ref, c_ref, d_ref, n_ref, o_ref):
+def spread_kernel(a_ref, b_ref, c_ref, d_ref, n_ref, m_ref, o_ref):
     total = a_ref[0].astype(F32)
     for ref in (b_ref, c_ref, d_ref):
         total = total + ref[...].astype(F32)
     scale = 1.0 / (EPS + jnp.sqrt(total[24:25] + total[25:26]))
-    out = jnp.concatenate([total[:24] * scale, n_ref[...] * scale], axis=0).astype(BF16)
+    n = n_ref[...]
+    mine = lax.axis_index("y")
+    line = jnp.zeros((1, 128), F32)
+    for y in range(4):
+        pair = jnp.concatenate([n[2 * y:2 * y + 1, :64], n[2 * y + 1:2 * y + 2, :64]], axis=1)
+        line = jnp.where(mine == y, pair, line)
+    row = lax.broadcasted_iota(jnp.int32, (24, 128), 0)
+    r = jnp.where(row == 21, line, total[:24]) * scale
+    out = jnp.concatenate([m_ref[...], r], axis=0).astype(BF16)
     for k in range(32):
         o_ref[k] = out
 
 
-def spread(side, parts, n):
+def spread(side, parts, n, m):
     return pl.pallas_call(
         spread_kernel,
-        out_shape=jax.ShapeDtypeStruct((32, 32, 128), BF16),
+        out_shape=jax.ShapeDtypeStruct((32, 88, 128), BF16),
         name="spread",
         compiler_params=pltpu.CompilerParams(vmem_limit_bytes=4 << 20),
-        cost_estimate=pl.CostEstimate(flops=20000, bytes_accessed=300000, transcendentals=0),
-    )(side, *parts, n)
-
-
-def attend_kernel(t_ref, u_ref, b_ref, a_ref, s_ref, e_ref, d_ref):
+        cost_estimate=pl.CostEstimate(flops=20000, bytes_accessed=800000, transcendentals=0),
+    )(side, *parts, n, m)
+
+
+def attend_kernel(t_ref, u_ref, b_ref, a_ref, s_ref, x0_ref, x1_ref, c0_ref, c1_ref, e0_ref, e1_ref,
+                  d0_ref, d1_ref):
     tokens = jnp.concatenate([t_ref[...], u_ref[...]], axis=1)
-
-    def project(g, carry):
-        xs = []
+    blocks, scores, expos, sums = (x0_ref, x1_ref), (c0_ref, c1_ref), (e0_ref, e1_ref), (d0_ref, d1_ref)
+
+    def columns(g, x_ref):
         for k in range(4):
             x = lax.dot_general(b_ref[4 * g + k, 0:64, :], tokens, TN, preferred_element_type=F32)
-            xs.append(x.reshape(2, 64, 512))
-        squares = [jnp.sum(x * x, axis=1) for x in xs]
+            x_ref[k] = x.reshape(2, 64, 512)
+
+    def unit(g, x_ref):
+        squares = []
+        for k in range(4):
+            x = x_ref[k]
+            squares.append(jnp.sum(x * x, axis=1))
         scale = jnp.sqrt(jnp.concatenate(squares, axis=0) * (1.0 / 64))
         scale = 1.0 / (EPS + scale)
         for k in range(4):
             for half in range(2):
-                unit = 16 * k + 2 * g + half
-                s_ref[unit] = (xs[k][half] * scale[2 * k + half:2 * k + half + 1]).astype(BF16)
+                row = scale[2 * k + half:2 * k + half + 1]
+                s_ref[16 * k + 2 * g + half] = (x_ref[k, half] * row).astype(BF16)
+
+    columns(0, x0_ref)
+    columns(1, x1_ref)
+
+    def project(i, carry):
+        for k in range(2):
+            unit(2 * i + k, blocks[k])
+            columns(jnp.minimum(2 * i + k + 2, 7), blocks[k])
         return carry
 
-    lax.fori_loop(0, 8, project, 0)
-
-    def weigh(h, b, slot):
+    lax.fori_loop(0, 4, project, 0, unroll=4)
+
+    def score(h, b):
         at = slice(256 * b, 256 * b + 256)
-        scores = lax.dot_general(s_ref[21 + h, :, at], s_ref[h, :, at], TN,
-                                 preferred_element_type=F32)
-        expo = jnp.exp2(scores * (0.125 * LOG2E))
-        e_ref[slot] = expo.astype(BF16)
-        d_ref[slot] = jnp.sum(expo.reshape(32, 8, 256), axis=0)
-
-    def gather(h, b, slot):
+        scores[b][...] = lax.dot_general(s_ref[21 + h, :, at], s_ref[h, :, at], TN,
+                                         preferred_element_type=F32)
+
+    def weigh(b):
+        expo = jnp.exp2(scores[b][...] * (0.125 * LOG2E))
+        expos[b][...] = expo.astype(BF16)
+        sums[b][...] = jnp.sum(expo.reshape(32, 8, 256), axis=0)
+
+    def gather(h, b):
         at = slice(256 * b, 256 * b + 256)
-        out = jnp.dot(s_ref[42 + h, :, at], e_ref[slot], preferred_element_type=F32)
-        total = jnp.sum(d_ref[slot], axis=0, keepdims=True)
+        out = jnp.dot(s_ref[42 + h, :, at], expos[b][...], preferred_element_type=F32)
+        total = jnp.sum(sums[b][...], axis=0, keepdims=True)
         a_ref[pl.ds(pl.multiple_of(h * 64, 64), 64), at] = (out * (1.0 / total)).astype(BF16)
 
-    weigh(0, 0, 0)
+    score(0, 0)
+    score(0, 1)
+    e1_ref[...] = jnp.zeros((256, 256), BF16)
+    d1_ref[...] = jnp.ones((8, 256), F32)
 
     def head(h, carry):
-        weigh(h, 1, 1)
-        gather(h, 0, 0)
-        weigh(jnp.minimum(h + 1, 20), 0, 0)
-        gather(h, 1, 1)
+        later = jnp.minimum(h + 1, 20)
+        weigh(0)
+        gather(jnp.maximum(h - 1, 0), 1)
+        score(later, 0)
+        weigh(1)
+        gather(h, 0)
+        score(later, 1)
         return carry
 
-    lax.fori_loop(0, 21, head, 0, unroll=1)
+    lax.fori_loop(0, 21, head, 0, unroll=21)
+    gather(20, 1)
 
 
 def attend(tokens, others, got):
     return pl.pallas_call(
         attend_kernel,
         out_shape=jax.ShapeDtypeStruct((1344, 512), BF16),
-        scratch_shapes=[pltpu.VMEM((64, 64, 512), BF16), pltpu.VMEM((2, 256, 256), BF16),
-                        pltpu.VMEM((2, 8, 256), F32)],
+        scratch_shapes=[pltpu.VMEM((64, 64, 512), BF16)]
+        + [pltpu.VMEM((4, 2, 64, 512), F32)] * 2 + [pltpu.VMEM((256, 256), F32)] * 2
+        + [pltpu.VMEM((256, 256), BF16)] * 2 + [pltpu.VMEM((8, 256), F32)] * 2,
         name="attend",
         compiler_params=pltpu.CompilerParams(vmem_limit_bytes=16 << 20),
         cost_estimate=pl.CostEstimate(flops=5000000000, bytes_accessed=2400000, transcendentals=2800000),
@@ -342,21 +372,17 @@
     part = pair_sum(keep, lax.ppermute(give, "core", swap))
     part = a2a(part, ("xh", "xl", "y"))
     send, proj = partial_products(part)
-    send, side, n = whole_products(a2a(send, "z"), proj)
-    send, latent, levels = lax.optimization_barrier((send, latent, levels))
+    m, side, n = whole_products(a2a(send, "z"), proj)
+    parts = [lax.ppermute(side[d], "y", [(k, (k + d) % 4) for k in range(4)]) for d in range(1, 4)]
+    send, latent, levels = lax.optimization_barrier((spread(side, parts, n, m), latent, levels))
     got = a2a(send, ZY)
 
     c_in, c_skip, c_out = noise_scales(levels)
     tokens = (c_in[:, None, None] * latent).astype(BF16)
     tokens = tokens.reshape(16, 4, 16, 16).transpose(1, 3, 0, 2).reshape(64, 256)
     others = lax.ppermute(tokens, "xl", swap)
-    parts = [lax.ppermute(side[d], "y", [(k, (k + d) % 4) for k in range(4)]) for d in range(1, 4)]
-    r = spread(side, parts, n)
-    r, others, _ = lax.optimization_barrier((r, others, got))
-    r = a2a(r, ZY)
-    n = r.reshape(8, 4, 32, 128)[:, 0, 24:, :64].reshape(64, 64)
-    r = jnp.concatenate([r[:, :21, :64], r[:, :21, 64:]], axis=0).reshape(1344, 64)
-
+    n = got[:, 85].reshape(64, 64)
+    r = jnp.concatenate([got[:, 64:85, :64], got[:, 64:85, 64:]], axis=0).reshape(1344, 64)
     attended = attend(tokens, others, got)
     own, other = output(tokens, others, attended, r, n)
     other = lax.ppermute(other, "xl", swap).astype(F32)

time: 96.1 us -> 92.8 us (0.966)
  waiting for transfers between devices: 12.5 us -> 24 us
  Pallas kernels: 20.1 us -> 12.5 us
  starting transfers between devices: 17.6 us -> 10.5 us
    all_to_all x2 -> x1, waiting for transfers between devices: 5.2 us -> 14.8 us  [a2a(): return lax.all_to_all(x, axis, 0, 0, tiled=True)]
    pallas_call x1, Pallas kernels: 11.9 us -> 4.83 us  [attend(): pl.pallas_call(attend_kernel, out_shape=jax.ShapeDtypeStruct((1344, 512),...]
    all_to_all x2 -> x1, starting transfers between devices: 10.7 us -> 4.86 us  [a2a(): return lax.all_to_all(x, axis, 0, 0, tiled=True)]
    ppermute x3, waiting for transfers between devices: 2 us -> 3 us  [shards(): lax.ppermute(side[d], 'y', [(k, (k + d) % 4) for k in range(4)])]
    ppermute x1, starting transfers between devices: 1.53 us -> 0.57 us  [shards(): other = lax.ppermute(other, 'xl', swap).astype(F32)]
    ppermute x1, waiting for transfers between devices: 2.42 us -> 3.39 us  [shards(): other = lax.ppermute(other, 'xl', swap).astype(F32)]
  transfers between devices with their start and end apart: 8 -> 7, of which waited for: 4 -> 5; matrix products, arithmetic and copies ran while one was open for 1% -> 1% of each run, Pallas kernels for 13% -> 0%
where the time goes in v6:
time: 92.8 us; the launch traced here: 92.6 us
  blocking collectives  42.6 us (46%)
  waiting for transfers between devices  24 us (26%)
  Pallas kernels  12.5 us (13%)
  starting transfers between devices  10.5 us (11%)
  local copies, waits for them, and re-layouts  1.13 us (1%)
  between operations  0.99 us (1%)
    all_to_all x2, blocking collectives, a2a(): return lax.all_to_all(x, axis, 0, 0, tiled=True)  42.6 us
    all_to_all x1, waiting for transfers between devices, a2a(): return lax.all_to_all(x, axis, 0, 0, tiled=True)  14.8 us
    all_to_all x1, starting transfers between devices, a2a(): return lax.all_to_all(x, axis, 0, 0, tiled=True)  4.86 us
    pallas_call x1, Pallas kernels, attend(): pl.pallas_call(attend_kernel, out_shape=jax.ShapeDtypeStruct((1344, 512),...  4.83 us
    pallas_call x1, Pallas kernels, contract(): pl.pallas_call(contract_kernel, out_shape=(shape, shape), in_specs=[HBM]...  4.7 us
    ppermute x3, starting transfers between devices, shards(): lax.ppermute(side[d], 'y', [(k, (k + d) % 4) for k in range(4)])  4.35 us
    ppermute x1, waiting for transfers between devices, shards(): other = lax.ppermute(other, 'xl', swap).astype(F32)  3.39 us
    ppermute x3, waiting for transfers between devices, shards(): lax.ppermute(side[d], 'y', [(k, (k + d) % 4) for k in range(4)])  3 us
  transfers between devices with their start and end apart: 7, of which 5 were waited for; matrix products, arithmetic and copies ran while one was open for 1% of the time, Pallas kernels for 0%

profile of v6, /device:TPU:8, one launch (start us, length us, event | category | flops | bytes accessed | tf_op | source)
XLA Modules:
  0.0 92.6 jit_solution(12743813988868430439)
XLA Ops:
  0.0 4.7 %contract.1 = (bf16[16,24,1536]{2,1,0:T(8,128)(2,1)S(1)}, bf16[16,24,1536]{2,1,0:T(8,128)(2,1)S(1)}) custom-call(f32[8,8]{1,0:T(8,128)} %c_hbm.1, f32[168,4032]{1,0:T(8,128)} %bitcast.31, f32[168,1344]{1,0:T(8,128)} %bitcast.32, f32[168,64]{1,0:T(8,128)} %bitcast.33, f32[168,64]{1,0:T(8,128)} %bitcast.34), custom_call_target="tpu_custom_call" | custom-call | flops 1065222144 | bytes 6000000 | tf_op jit(solution)/shard_map/contract/pallas_call | solution.py:105
  4.7 0.1 collective-permute-start
  4.8 2.8 %collective-permute-done.b_ref = bf16[16,24,1536]{2,1,0:T(8,128)(2,1)S(1)} collective-permute-done((bf16[16,24,1536]{2,1,0:T(8,128)(2,1)S(1)}, bf16[16,24,1536]{2,1,0:T(8,128)(2,1)S(1)}, u32[]{:S(2)}, u32[]{:S(2)}) %collective-permute-start) | collective-permute-done | bytes 1179680 | tf_op jit(solution)/shard_map/ppermute | solution.py:372
  7.6 0.3 pair.1
  7.9 24.4 %all_to_all.15.g_ref = bf16[16,24,1536]{2,1,0:T(8,128)(2,1)S(1)} all-to-all(bf16[16,24,1536]{2,1,0:T(8,128)(2,1)S(1)} %pair.1), channel_id=1, replica_groups=mesh['xh'=2,'core'=2,'xl'=2,'z'=8,'y'=4] {'xh','xl','y'}, dimensions={0} | all-to-all | bytes 2359296 | tf_op jit(solution)/shard_map/all_to_all | solution.py:31
  32.3 0.5 partial.1
  32.8 18.2 %all_to_all.16.g_ref = bf16[8,104,128]{2,1,0:T(8,128)(2,1)S(1)} all-to-all(bf16[8,104,128]{2,1,0:T(8,128)(2,1)S(1)} %get-tuple-element.19), channel_id=1, replica_groups=mesh['xh'=2,'core'=2,'xl'=2,'z'=8,'y'=4] {'z'}, dimensions={0} | all-to-all | bytes 425984 | tf_op jit(solution)/shard_map/all_to_all | solution.py:31
  51.0 0.3 whole.1
  51.4 0.0 copy-start
  51.4 1.1 %collective-permute-start.1 = (bf16[32,128]{1,0:T(8,128)(2,1)S(1)}, bf16[32,128]{1,0:T(8,128)(2,1)S(1)}, u32[]{:S(2)}, u32[]{:S(2)}) collective-permute-start(bf16[32,128]{1,0:T(8,128)(2,1)S(1)} %get-tuple-element.37), channel_id=1, source_target_pairs={{0,1},{1,2},{2,3},{3,0},{4,5},{5,6},{6,7},{7,4},{8,9},{9,10},{10,1... | collective-permute-start | bytes 24584 | tf_op jit(solution)/shard_map/ppermute | solution.py:376
  52.5 2.6 %collective-permute-start.2 = (bf16[32,128]{1,0:T(8,128)(2,1)S(1)}, bf16[32,128]{1,0:T(8,128)(2,1)S(1)}, u32[]{:S(2)}, u32[]{:S(2)}) collective-permute-start(bf16[32,128]{1,0:T(8,128)(2,1)S(1)} %get-tuple-element.36), channel_id=1, source_target_pairs={{0,2},{1,3},{2,0},{3,1},{4,6},{5,7},{6,4},{7,5},{8,10},{9,11},{10,... | collective-permute-start | bytes 24584 | tf_op jit(solution)/shard_map/ppermute | solution.py:376
  55.1 0.7 collective-permute-start.3
  55.7 0.0 collective-permute-done.1.b_ref
  55.7 1.9 %collective-permute-done.2.c_ref = bf16[32,128]{1,0:T(8,128)(2,1)S(1)} collective-permute-done((bf16[32,128]{1,0:T(8,128)(2,1)S(1)}, bf16[32,128]{1,0:T(8,128)(2,1)S(1)}, u32[]{:S(2)}, u32[]{:S(2)}) %collective-permute-start.2) | collective-permute-done | bytes 8224 | tf_op jit(solution)/shard_map/ppermute | solution.py:376
  57.6 1.1 %collective-permute-done.3.d_ref = bf16[32,128]{1,0:T(8,128)(2,1)S(1)} collective-permute-done((bf16[32,128]{1,0:T(8,128)(2,1)S(1)}, bf16[32,128]{1,0:T(8,128)(2,1)S(1)}, u32[]{:S(2)}, u32[]{:S(2)}) %collective-permute-start.3) | collective-permute-done | bytes 8224 | tf_op jit(solution)/shard_map/ppermute | solution.py:376
  58.7 0.9 %spread.1 = bf16[32,88,128]{2,1,0:T(8,128)(2,1)} custom-call(bf16[4,32,128]{2,1,0:T(8,128)(2,1)S(1)} %get-tuple-element.21.a_ref, bf16[32,128]{1,0:T(8,128)(2,1)S(1)} %collective-permute-done.1.b_ref, bf16[32,128]{1,0:T(8,128)(2,1)S(1)} %collective-permute-done.2.c_ref, bf16[32,128]{1,0:T(8,128)(2,1)S(1)} %collective-permute-done.3.d_ref, ...), custom_call_target="tpu_custom_call" | custom-call | flops 20000 | bytes 800000 | tf_op jit(solution)/shard_map/spread/pallas_call | solution.py:236
  59.7 4.9 %all-to-all-start.2 = ((bf16[32,88,128]{2,1,0:T(8,128)(2,1)}), bf16[32,88,128]{2,1,0:T(8,128)(2,1)S(1)}, u32[]{:S(2)}, u32[]{:S(2)}) async-start(bf16[32,88,128]{2,1,0:T(8,128)(2,1)} %spread.1), calls=%async_computation.2 | async-start | bytes 1441792 | tf_op jit(solution)/shard_map/all_to_all | solution.py:31
  65.4 0.2 reshape.66
  65.6 0.3 copy.9
  65.9 0.2 reshape.67.t_ref
  66.1 0.6 collective-permute-start.4
  66.7 14.8 %all-to-all-done.2.b_ref = bf16[32,88,128]{2,1,0:T(8,128)(2,1)S(1)} async-done(((bf16[32,88,128]{2,1,0:T(8,128)(2,1)}), bf16[32,88,128]{2,1,0:T(8,128)(2,1)S(1)}, u32[]{:S(2)}, u32[]{:S(2)}) %all-to-all-start.2) | async-done | bytes 720928 | tf_op jit(solution)/shard_map/all_to_all | solution.py:31
  81.6 0.1 fusion.3
  81.7 0.1 pad_maximum_fusion
  81.8 0.1 slice_reduce_fusion
  81.9 0.1 reshape.68.r_ref
  82.0 0.1 reshape_squeeze.3.n_ref
  82.1 4.8 %attend.1.a_ref = bf16[1344,512]{1,0:T(8,128)(2,1)S(1)} custom-call(bf16[64,256]{1,0:T(8,128)(2,1)S(1)} %reshape.67.t_ref, bf16[64,256]{1,0:T(8,128)(2,1)S(1)} %collective-permute-done.4.u_ref, bf16[32,88,128]{2,1,0:T(8,128)(2,1)S(1)} %all-to-all-done.2.b_ref), custom_call_target="tpu_custom_call" | custom-call | flops 5000000000 | bytes 2400000 | tf_op jit(solution)/shard_map/attend/pallas_call | solution.py:314
  86.9 1.0 %output.1 = (f32[64,256]{1,0:T(8,128)S(1)}, bf16[64,256]{1,0:T(8,128)(2,1)S(1)}) custom-call(bf16[64,256]{1,0:T(8,128)(2,1)S(1)} %reshape.67.t_ref, bf16[64,256]{1,0:T(8,128)(2,1)S(1)} %collective-permute-done.4.u_ref, bf16[1344,512]{1,0:T(8,128)(2,1)S(1)} %attend.1.a_ref, bf16[1344,64]{1,0:T(8,128)(2,1)S(1)} %reshape.68.r_ref, ...), custom_call_target="tpu_custom_call" | custom-call | flops 100000000 | bytes 2000000 | tf_op jit(solution)/shard_map/output/pallas_call | solution.py:353
  87.9 0.6 collective-permute-start.5
  88.5 3.4 %collective-permute-done.5 = bf16[64,256]{1,0:T(8,128)(2,1)S(1)} collective-permute-done((bf16[64,256]{1,0:T(8,128)(2,1)S(1)}, bf16[64,256]{1,0:T(8,128)(2,1)S(1)}, u32[]{:S(2)}, u32[]{:S(2)}) %collective-permute-start.5) | collective-permute-done | bytes 32800 | tf_op jit(solution)/shard_map/ppermute | solution.py:388
  91.9 0.7 fusion
  (5 shorter events, 0.0 us)
Async XLA Ops:
  4.7 2.9 %collective-permute-start = (bf16[16,24,1536]{2,1,0:T(8,128)(2,1)S(1)}, bf16[16,24,1536]{2,1,0:T(8,128)(2,1)S(1)}, u32[]{:S(2)}, u32[]{:S(2)}) collective-permute-start(bf16[16,24,1536]{2,1,0:T(8,128)(2,1)S(1)} %get-tuple-element.18), channel_id=1, source_target_pairs={{0,64},{64,0},{1,65},{65,1},{2,66},{66,2},{3,67},{67,3},{4,68},{68... | collective-permute-start | bytes 3538952 | tf_op jit(solution)/shard_map/ppermute | solution.py:372
  51.4 14.0 %copy-start = (f32[1,64,256]{2,1,0:T(8,128)S(1)}, f32[1,64,256]{2,1,0:T(8,128)}, u32[]{:S(2)}) copy-start(f32[1,64,256]{2,1,0:T(8,128)} %param.12) | copy-start | bytes 196612
  51.4 4.3 %collective-permute-start.1 = (bf16[32,128]{1,0:T(8,128)(2,1)S(1)}, bf16[32,128]{1,0:T(8,128)(2,1)S(1)}, u32[]{:S(2)}, u32[]{:S(2)}) collective-permute-start(bf16[32,128]{1,0:T(8,128)(2,1)S(1)} %get-tuple-element.37), channel_id=1, source_target_pairs={{0,1},{1,2},{2,3},{3,0},{4,5},{5,6},{6,7},{7,4},{8,9},{9,10},{10,1... | collective-permute-start | bytes 24584 | tf_op jit(solution)/shard_map/ppermute | solution.py:376
  52.5 5.2 %collective-permute-start.2 = (bf16[32,128]{1,0:T(8,128)(2,1)S(1)}, bf16[32,128]{1,0:T(8,128)(2,1)S(1)}, u32[]{:S(2)}, u32[]{:S(2)}) collective-permute-start(bf16[32,128]{1,0:T(8,128)(2,1)S(1)} %get-tuple-element.36), channel_id=1, source_target_pairs={{0,2},{1,3},{2,0},{3,1},{4,6},{5,7},{6,4},{7,5},{8,10},{9,11},{10,... | collective-permute-start | bytes 24584 | tf_op jit(solution)/shard_map/ppermute | solution.py:376
  55.1 3.7 %collective-permute-start.3 = (bf16[32,128]{1,0:T(8,128)(2,1)S(1)}, bf16[32,128]{1,0:T(8,128)(2,1)S(1)}, u32[]{:S(2)}, u32[]{:S(2)}) collective-permute-start(bf16[32,128]{1,0:T(8,128)(2,1)S(1)} %get-tuple-element.35), channel_id=1, source_target_pairs={{0,3},{1,0},{2,1},{3,2},{4,7},{5,4},{6,5},{7,6},{8,11},{9,8},{10,9... | collective-permute-start | bytes 24584 | tf_op jit(solution)/shard_map/ppermute | solution.py:376
  59.7 21.9 %all-to-all-start.2 = ((bf16[32,88,128]{2,1,0:T(8,128)(2,1)}), bf16[32,88,128]{2,1,0:T(8,128)(2,1)S(1)}, u32[]{:S(2)}, u32[]{:S(2)}) async-start(bf16[32,88,128]{2,1,0:T(8,128)(2,1)} %spread.1), calls=%async_computation.2 | async-start | bytes 1441792 | tf_op jit(solution)/shard_map/all_to_all | solution.py:31
  66.1 15.9 %collective-permute-start.4 = (bf16[64,256]{1,0:T(8,128)(2,1)S(1)}, bf16[64,256]{1,0:T(8,128)(2,1)S(1)}, u32[]{:S(2)}, u32[]{:S(2)}) collective-permute-start(bf16[64,256]{1,0:T(8,128)(2,1)S(1)} %reshape.67.t_ref), channel_id=1, source_target_pairs={{0,32},{32,0},{1,33},{33,1},{2,34},{34,2},{3,35},{35,3},{4,36},{36... | collective-permute-start | bytes 98312 | tf_op jit(solution)/shard_map/ppermute | solution.py:383
  87.9 4.0 %collective-permute-start.5 = (bf16[64,256]{1,0:T(8,128)(2,1)S(1)}, bf16[64,256]{1,0:T(8,128)(2,1)S(1)}, u32[]{:S(2)}, u32[]{:S(2)}) collective-permute-start(bf16[64,256]{1,0:T(8,128)(2,1)S(1)} %get-tuple-element.28), channel_id=1, source_target_pairs={{0,32},{32,0},{1,33},{33,1},{2,34},{34,2},{3,35},{35,3},{4,36},{36... | collective-permute-start | bytes 98312 | tf_op jit(solution)/shard_map/ppermute | solution.py:388

commit v7 on v6

--- a/solution.py
+++ b/solution.py
@@ -182,16 +182,14 @@
     )(got)
 
 
-def whole_kernel(g_ref, p_ref, o_ref, r_ref, n_ref):
-    total = g_ref[0].astype(F32)
+def rows_kernel(g_ref, p_ref, r_ref, n_ref):
+    total = g_ref[0, 64:104].astype(F32)
     for z in range(1, 8):
-        total = total + g_ref[z].astype(F32)
-    m = total[0:64] / (EPS + jnp.sqrt(unlines(total[64:72, 64:128], 2)))
-    n_ref[...] = total[64:72]
-    o_ref[...] = m
+        total = total + g_ref[z, 64:104].astype(F32)
+    n_ref[...] = total[0:8]
     w_out = g_ref[:, 72:96, :].astype(F32).reshape(192, 128)
     w_out = jnp.concatenate([w_out[:, :64], w_out[:, 64:]], axis=0)
-    norm = jnp.sqrt(unlines(total[96:104], 3))
+    norm = jnp.sqrt(unlines(total[32:40], 3))
     proj = (p_ref[...] / (EPS + norm)).astype(BF16)
     r = jnp.dot(proj, w_out.astype(BF16), preferred_element_type=F32)
     square = lines(jnp.sum(w_out * w_out, axis=0, keepdims=True), 1, 64)
@@ -202,16 +200,32 @@
         r_ref[lax.rem(y + 4 - mine, 4)] = jnp.concatenate([both, square], axis=0).astype(BF16)
 
 
-def whole_products(got, proj):
-    return pl.pallas_call(
-        whole_kernel,
-        out_shape=(jax.ShapeDtypeStruct((64, 128), F32),
-                   jax.ShapeDtypeStruct((4, 32, 128), BF16),
+def row_products(got, proj):
+    return pl.pallas_call(
+        rows_kernel,
+        out_shape=(jax.ShapeDtypeStruct((4, 32, 128), BF16),
                    jax.ShapeDtypeStruct((8, 128), F32)),
-        name="whole",
+        name="rows",
         compiler_params=pltpu.CompilerParams(vmem_limit_bytes=8 << 20),
         cost_estimate=pl.CostEstimate(flops=100000, bytes_accessed=800000, transcendentals=0),
     )(got, proj)
+
+
+def units_kernel(g_ref, o_ref):
+    total = g_ref[0, 0:72].astype(F32)
+    for z in range(1, 8):
+        total = total + g_ref[z, 0:72].astype(F32)
+    o_ref[...] = total[0:64] / (EPS + jnp.sqrt(unlines(total[64:72, 64:128], 2)))
+
+
+def unit_products(got):
+    return pl.pallas_call(
+        units_kernel,
+        out_shape=jax.ShapeDtypeStruct((64, 128), F32),
+        name="units",
+        compiler_params=pltpu.CompilerParams(vmem_limit_bytes=4 << 20),
+        cost_estimate=pl.CostEstimate(flops=100000, bytes_accessed=200000, transcendentals=0),
+    )(got)
 
 
 def spread_kernel(a_ref, b_ref, c_ref, d_ref, n_ref, m_ref, o_ref):
@@ -242,89 +256,58 @@
     )(side, *parts, n, m)
 
 
-def attend_kernel(t_ref, u_ref, b_ref, a_ref, s_ref, x0_ref, x1_ref, c0_ref, c1_ref, e0_ref, e1_ref,
-                  d0_ref, d1_ref):
-    tokens = jnp.concatenate([t_ref[...], u_ref[...]], axis=1)
+def attend_kernel(t_ref, b_ref, r_ref, n_ref, o_ref, a_ref, z_ref, s_ref, x0_ref, x1_ref, c0_ref,
+                  c1_ref, e0_ref, e1_ref, d0_ref, d1_ref):
+    tokens = t_ref[...]
     blocks, scores, expos, sums = (x0_ref, x1_ref), (c0_ref, c1_ref), (e0_ref, e1_ref), (d0_ref, d1_ref)
 
-    def columns(g, x_ref):
+    def columns(g):
         for k in range(4):
             x = lax.dot_general(b_ref[4 * g + k, 0:64, :], tokens, TN, preferred_element_type=F32)
-            x_ref[k] = x.reshape(2, 64, 512)
-
-    def unit(g, x_ref):
+            blocks[g % 2][k] = x.reshape(2, 64, 256)
+
+    def unit(g):
         squares = []
         for k in range(4):
-            x = x_ref[k]
+            x = blocks[g % 2][k]
             squares.append(jnp.sum(x * x, axis=1))
         scale = jnp.sqrt(jnp.concatenate(squares, axis=0) * (1.0 / 64))
         scale = 1.0 / (EPS + scale)
         for k in range(4):
             for half in range(2):
                 row = scale[2 * k + half:2 * k + half + 1]
-                s_ref[16 * k + 2 * g + half] = (x_ref[k, half] * row).astype(BF16)
-
-    columns(0, x0_ref)
-    columns(1, x1_ref)
-
-    def project(i, carry):
-        for k in range(2):
-            unit(2 * i + k, blocks[k])
-            columns(jnp.minimum(2 * i + k + 2, 7), blocks[k])
-        return carry
-
-    lax.fori_loop(0, 4, project, 0, unroll=4)
-
-    def score(h, b):
-        at = slice(256 * b, 256 * b + 256)
-        scores[b][...] = lax.dot_general(s_ref[21 + h, :, at], s_ref[h, :, at], TN,
-                                         preferred_element_type=F32)
-
-    def weigh(b):
-        expo = jnp.exp2(scores[b][...] * (0.125 * LOG2E))
-        expos[b][...] = expo.astype(BF16)
-        sums[b][...] = jnp.sum(expo.reshape(32, 8, 256), axis=0)
-
-    def gather(h, b):
-        at = slice(256 * b, 256 * b + 256)
-        out = jnp.dot(s_ref[42 + h, :, at], expos[b][...], preferred_element_type=F32)
-        total = jnp.sum(sums[b][...], axis=0, keepdims=True)
-        a_ref[pl.ds(pl.multiple_of(h * 64, 64), 64), at] = (out * (1.0 / total)).astype(BF16)
-
-    score(0, 0)
-    score(0, 1)
-    e1_ref[...] = jnp.zeros((256, 256), BF16)
-    d1_ref[...] = jnp.ones((8, 256), F32)
-
-    def head(h, carry):
-        later = jnp.minimum(h + 1, 20)
-        weigh(0)
-        gather(jnp.maximum(h - 1, 0), 1)
-        score(later, 0)
-        weigh(1)
-        gather(h, 0)
-        score(later, 1)
-        return carry
-
-    lax.fori_loop(0, 21, head, 0, unroll=21)
-    gather(20, 1)
-
-
-def attend(tokens, others, got):
-    return pl.pallas_call(
-        attend_kernel,
-        out_shape=jax.ShapeDtypeStruct((1344, 512), BF16),
-        scratch_shapes=[pltpu.VMEM((64, 64, 512), BF16)]
-        + [pltpu.VMEM((4, 2, 64, 512), F32)] * 2 + [pltpu.VMEM((256, 256), F32)] * 2
-        + [pltpu.VMEM((256, 256), BF16)] * 2 + [pltpu.VMEM((8, 256), F32)] * 2,
-        name="attend",
-        compiler_params=pltpu.CompilerParams(vmem_limit_bytes=16 << 20),
-        cost_estimate=pl.CostEstimate(flops=5000000000, bytes_accessed=2400000, transcendentals=2800000),
-    )(tokens, others, got)
-
-
-def output_kernel(t_ref, u_ref, a_ref, r_ref, n_ref, own_ref, other_ref, z_ref):
-    tokens = jnp.concatenate([t_ref[...], u_ref[...]], axis=1)
+                s_ref[16 * k + 2 * g + half] = (blocks[g % 2][k, half] * row).astype(BF16)
+
+    columns(0)
+    columns(1)
+    for g in range(8):
+        unit(g)
+        if g + 2 < 8:
+            columns(g + 2)
+
+    def score(h):
+        scores[h % 2][...] = lax.dot_general(s_ref[21 + h], s_ref[h], TN, preferred_element_type=F32)
+
+    def weigh(h):
+        expo = jnp.exp2(scores[h % 2][...] * (0.125 * LOG2E))
+        expos[h % 2][...] = expo.astype(BF16)
+        sums[h % 2][...] = jnp.sum(expo.reshape(32, 8, 256), axis=0)
+
+    def gather(h):
+        out = jnp.dot(s_ref[42 + h], expos[h % 2][...], preferred_element_type=F32)
+        total = jnp.sum(sums[h % 2][...], axis=0, keepdims=True)
+        a_ref[64 * h:64 * h + 64, :] = (out * (1.0 / total)).astype(BF16)
+
+    score(0)
+    score(1)
+    for h in range(21):
+        weigh(h)
+        if h > 0:
+            gather(h - 1)
+        if h + 2 < 21:
+            score(h + 2)
+    gather(20)
+
     feature = 0.3 * lax.dot_general(r_ref[...], a_ref[...], TN, preferred_element_type=F32)
     feature = feature + 0.7 * lax.dot_general(n_ref[...], tokens, TN, preferred_element_type=F32)
     feature = feature * (1.0 / (0.58 ** 0.5))
@@ -333,31 +316,31 @@
     keep = lax.rem(token, 16) == lane // 16
     row = lax.broadcasted_iota(jnp.int32, (128, 256), 0)
     lane = lax.broadcasted_iota(jnp.int32, (128, 256), 1)
-    for b in range(2):
-        part = feature[:, 256 * b:256 * b + 256]
-        hi = part.astype(BF16)
-        lo = (part - hi.astype(F32)).astype(BF16)
-        both = jnp.concatenate([hi, lo], axis=0)
-        for i in range(4):
-            tile = jnp.where(lax.rem(row, 64) == 16 * i + lax.rem(lane, 16), 1.0, 0.0).astype(BF16)
-            wide = lax.dot_general(both, tile, TN, preferred_element_type=F32)
-            wide = jnp.where(keep, wide, 0.0).reshape(16, 16, 256)
-            wide = jnp.sum(wide, axis=1)
-            z_ref[2 * b, pl.ds(i, 16, stride=4), :] = wide[:, :128]
-            z_ref[2 * b + 1, pl.ds(i, 16, stride=4), :] = wide[:, 128:]
-    own_ref[...] = jnp.concatenate([z_ref[0], z_ref[1]], axis=1)
-    other_ref[...] = jnp.concatenate([z_ref[2], z_ref[3]], axis=1).astype(BF16)
-
-
-def output(tokens, others, attended, r, n):
-    return pl.pallas_call(
-        output_kernel,
-        out_shape=(jax.ShapeDtypeStruct((64, 256), F32), jax.ShapeDtypeStruct((64, 256), BF16)),
-        scratch_shapes=[pltpu.VMEM((4, 64, 128), F32)],
-        name="output",
+    hi = feature.astype(BF16)
+    lo = (feature - hi.astype(F32)).astype(BF16)
+    both = jnp.concatenate([hi, lo], axis=0)
+    for i in range(4):
+        tile = jnp.where(lax.rem(row, 64) == 16 * i + lax.rem(lane, 16), 1.0, 0.0).astype(BF16)
+        wide = lax.dot_general(both, tile, TN, preferred_element_type=F32)
+        wide = jnp.where(keep, wide, 0.0).reshape(16, 16, 256)
+        wide = jnp.sum(wide, axis=1)
+        z_ref[0, pl.ds(i, 16, stride=4), :] = wide[:, :128]
+        z_ref[1, pl.ds(i, 16, stride=4), :] = wide[:, 128:]
+    o_ref[...] = jnp.concatenate([z_ref[0], z_ref[1]], axis=1).astype(o_ref.dtype)
+
+
+def attend(tokens, got, r, n, dtype):
+    return pl.pallas_call(
+        attend_kernel,
+        out_shape=jax.ShapeDtypeStruct((64, 256), dtype),
+        scratch_shapes=[pltpu.VMEM((1344, 256), BF16), pltpu.VMEM((2, 64, 128), F32),
+                        pltpu.VMEM((64, 64, 256), BF16)]
+        + [pltpu.VMEM((4, 2, 64, 256), F32)] * 2 + [pltpu.VMEM((256, 256), F32)] * 2
+        + [pltpu.VMEM((256, 256), BF16)] * 2 + [pltpu.VMEM((8, 256), F32)] * 2,
+        name="attend",
         compiler_params=pltpu.CompilerParams(vmem_limit_bytes=12 << 20),
-        cost_estimate=pl.CostEstimate(flops=100000000, bytes_accessed=2000000, transcendentals=0),
-    )(tokens, others, attended, r, n)
+        cost_estimate=pl.CostEstimate(flops=2500000000, bytes_accessed=1200000, transcendentals=1400000),
+    )(tokens, got, r, n)
 
 
 def shards(snap_in, snap_qkv, snap_proj, snap_out, coeffs, latent, levels):
@@ -372,9 +355,11 @@
     part = pair_sum(keep, lax.ppermute(give, "core", swap))
     part = a2a(part, ("xh", "xl", "y"))
     send, proj = partial_products(part)
-    m, side, n = whole_products(a2a(send, "z"), proj)
+    got = a2a(send, "z")
+    side, n = row_products(got, proj)
     parts = [lax.ppermute(side[d], "y", [(k, (k + d) % 4) for k in range(4)]) for d in range(1, 4)]
-    send, latent, levels = lax.optimization_barrier((spread(side, parts, n, m), latent, levels))
+    send = spread(side, parts, n, unit_products(got))
+    send, latent, levels = lax.optimization_barrier((send, latent, levels))
     got = a2a(send, ZY)
 
     c_in, c_skip, c_out = noise_scales(levels)
@@ -383,9 +368,10 @@
     others = lax.ppermute(tokens, "xl", swap)
     n = got[:, 85].reshape(64, 64)
     r = jnp.concatenate([got[:, 64:85, :64], got[:, 64:85, 64:]], axis=0).reshape(1344, 64)
-    attended = attend(tokens, others, got)
-    own, other = output(tokens, others, attended, r, n)
+    other = attend(others, got, r, n, BF16)
+    tokens, other = lax.optimization_barrier((tokens, other))
     other = lax.ppermute(other, "xl", swap).astype(F32)
+    own = attend(tokens, got, r, n, F32)
     first = lax.axis_index("xl") == 0
     feature = jnp.stack([jnp.where(first, own, other), jnp.where(first, other, own)])
     out = c_skip[:, None, None] * latent + c_out[:, None, None] * feature

time: 92.8 us -> 90.5 us (0.975)
  waiting for transfers between devices: 24 us -> 21.1 us
    ppermute x1, waiting for transfers between devices: 3.39 us -> 0.38 us  [shards(): other = lax.ppermute(other, 'xl', swap).astype(F32)]
    pallas_call x3 -> x4, Pallas kernels: 6.11 us -> 6.51 us  [the longest x2 6.1 us: attend(): pl.pallas_call(attend_kernel, out_shape=jax.ShapeDtypeStruct((64, 256), d...]
  transfers between devices with their start and end apart: 7 -> 7, of which waited for: 5 -> 5; matrix products, arithmetic and copies ran while one was open for 1% -> 1% of each run, Pallas kernels for 0% -> 3%
where the time goes in v7:
time: 90.5 us; the launch traced here: 90 us
  blocking collectives  42.6 us (47%)
  waiting for transfers between devices  21.1 us (23%)
  Pallas kernels  12.9 us (14%)
  starting transfers between devices  10.5 us (12%)
  local copies, waits for them, and re-layouts  1.13 us (1%)
  between operations  1 us (1%)
    all_to_all x2, blocking collectives, a2a(): return lax.all_to_all(x, axis, 0, 0, tiled=True)  42.6 us
    all_to_all x1, waiting for transfers between devices, a2a(): return lax.all_to_all(x, axis, 0, 0, tiled=True)  15 us
    pallas_call x2, Pallas kernels, attend(): pl.pallas_call(attend_kernel, out_shape=jax.ShapeDtypeStruct((64, 256), d...  6.1 us
    all_to_all x1, starting transfers between devices, a2a(): return lax.all_to_all(x, axis, 0, 0, tiled=True)  4.86 us
    pallas_call x1, Pallas kernels, contract(): pl.pallas_call(contract_kernel, out_shape=(shape, shape), in_specs=[HBM]...  4.7 us
    ppermute x3, starting transfers between devices, shards(): lax.ppermute(side[d], 'y', [(k, (k + d) % 4) for k in range(4)])  4.35 us
    ppermute x3, waiting for transfers between devices, shards(): lax.ppermute(side[d], 'y', [(k, (k + d) % 4) for k in range(4)])  2.88 us
    ppermute x1, waiting for transfers between devices, shards(): part = pair_sum(keep, lax.ppermute(give, 'core', swap))  2.83 us
  transfers between devices with their start and end apart: 7, of which 5 were waited for; matrix products, arithmetic and copies ran while one was open for 1% of the time, Pallas kernels for 3%

profile of v7, /device:TPU:8, one launch (start us, length us, event | category | flops | bytes accessed | tf_op | source)
XLA Modules:
  0.0 90.0 jit_solution(3458264168761214976)
XLA Ops:
  0.0 4.7 %contract.1 = (bf16[16,24,1536]{2,1,0:T(8,128)(2,1)S(1)}, bf16[16,24,1536]{2,1,0:T(8,128)(2,1)S(1)}) custom-call(f32[8,8]{1,0:T(8,128)} %c_hbm.1, f32[168,4032]{1,0:T(8,128)} %bitcast.31, f32[168,1344]{1,0:T(8,128)} %bitcast.32, f32[168,64]{1,0:T(8,128)} %bitcast.33, f32[168,64]{1,0:T(8,128)} %bitcast.34), custom_call_target="tpu_custom_call" | custom-call | flops 1065222144 | bytes 6000000 | tf_op jit(solution)/shard_map/contract/pallas_call | solution.py:105
  4.7 0.1 collective-permute-start
  4.8 2.8 %collective-permute-done.b_ref = bf16[16,24,1536]{2,1,0:T(8,128)(2,1)S(1)} collective-permute-done((bf16[16,24,1536]{2,1,0:T(8,128)(2,1)S(1)}, bf16[16,24,1536]{2,1,0:T(8,128)(2,1)S(1)}, u32[]{:S(2)}, u32[]{:S(2)}) %collective-permute-start) | collective-permute-done | bytes 1179680 | tf_op jit(solution)/shard_map/ppermute | solution.py:355
  7.6 0.3 pair.1
  7.9 24.4 %all_to_all.15.g_ref = bf16[16,24,1536]{2,1,0:T(8,128)(2,1)S(1)} all-to-all(bf16[16,24,1536]{2,1,0:T(8,128)(2,1)S(1)} %pair.1), channel_id=1, replica_groups=mesh['xh'=2,'core'=2,'xl'=2,'z'=8,'y'=4] {'xh','xl','y'}, dimensions={0} | all-to-all | bytes 2359296 | tf_op jit(solution)/shard_map/all_to_all | solution.py:31
  32.3 0.5 partial.1
  32.8 18.2 %all_to_all.16.g_ref = bf16[8,104,128]{2,1,0:T(8,128)(2,1)S(1)} all-to-all(bf16[8,104,128]{2,1,0:T(8,128)(2,1)S(1)} %get-tuple-element.18), channel_id=1, replica_groups=mesh['xh'=2,'core'=2,'xl'=2,'z'=8,'y'=4] {'z'}, dimensions={0} | all-to-all | bytes 425984 | tf_op jit(solution)/shard_map/all_to_all | solution.py:31
  51.0 0.3 rows.1
  51.4 1.1 %collective-permute-start.1 = (bf16[32,128]{1,0:T(8,128)(2,1)S(1)}, bf16[32,128]{1,0:T(8,128)(2,1)S(1)}, u32[]{:S(2)}, u32[]{:S(2)}) collective-permute-start(bf16[32,128]{1,0:T(8,128)(2,1)S(1)} %get-tuple-element.35), channel_id=1, source_target_pairs={{0,1},{1,2},{2,3},{3,0},{4,5},{5,6},{6,7},{7,4},{8,9},{9,10},{10,1... | collective-permute-start | bytes 24584 | tf_op jit(solution)/shard_map/ppermute | solution.py:360
  52.5 2.6 %collective-permute-start.2 = (bf16[32,128]{1,0:T(8,128)(2,1)S(1)}, bf16[32,128]{1,0:T(8,128)(2,1)S(1)}, u32[]{:S(2)}, u32[]{:S(2)}) collective-permute-start(bf16[32,128]{1,0:T(8,128)(2,1)S(1)} %get-tuple-element.34), channel_id=1, source_target_pairs={{0,2},{1,3},{2,0},{3,1},{4,6},{5,7},{6,4},{7,5},{8,10},{9,11},{10,... | collective-permute-start | bytes 24584 | tf_op jit(solution)/shard_map/ppermute | solution.py:360
  55.1 0.7 collective-permute-start.3
  55.7 0.1 units.1.m_ref
  55.8 0.0 copy-start
  55.8 1.8 %collective-permute-done.2.c_ref = bf16[32,128]{1,0:T(8,128)(2,1)S(1)} collective-permute-done((bf16[32,128]{1,0:T(8,128)(2,1)S(1)}, bf16[32,128]{1,0:T(8,128)(2,1)S(1)}, u32[]{:S(2)}, u32[]{:S(2)}) %collective-permute-start.2) | collective-permute-done | bytes 8224 | tf_op jit(solution)/shard_map/ppermute | solution.py:360
  57.6 1.1 %collective-permute-done.3.d_ref = bf16[32,128]{1,0:T(8,128)(2,1)S(1)} collective-permute-done((bf16[32,128]{1,0:T(8,128)(2,1)S(1)}, bf16[32,128]{1,0:T(8,128)(2,1)S(1)}, u32[]{:S(2)}, u32[]{:S(2)}) %collective-permute-start.3) | collective-permute-done | bytes 8224 | tf_op jit(solution)/shard_map/ppermute | solution.py:360
  58.7 0.9 %spread.1 = bf16[32,88,128]{2,1,0:T(8,128)(2,1)} custom-call(bf16[4,32,128]{2,1,0:T(8,128)(2,1)S(1)} %get-tuple-element.20.a_ref, bf16[32,128]{1,0:T(8,128)(2,1)S(1)} %collective-permute-done.1.b_ref, bf16[32,128]{1,0:T(8,128)(2,1)S(1)} %collective-permute-done.2.c_ref, bf16[32,128]{1,0:T(8,128)(2,1)S(1)} %collective-permute-done.3.d_ref, ...), custom_call_target="tpu_custom_call" | custom-call | flops 20000 | bytes 800000 | tf_op jit(solution)/shard_map/spread/pallas_call | solution.py:250
  59.7 4.9 %all-to-all-start.2 = ((bf16[32,88,128]{2,1,0:T(8,128)(2,1)}), bf16[32,88,128]{2,1,0:T(8,128)(2,1)S(1)}, u32[]{:S(2)}, u32[]{:S(2)}) async-start(bf16[32,88,128]{2,1,0:T(8,128)(2,1)} %spread.1), calls=%async_computation.2 | async-start | bytes 1441792 | tf_op jit(solution)/shard_map/all_to_all | solution.py:31
  65.4 0.2 reshape.66
  65.7 0.3 copy.9
  65.9 0.2 reshape.67.t_ref
  66.2 0.4 collective-permute-start.4
  66.6 15.0 %all-to-all-done.2.b_ref = bf16[32,88,128]{2,1,0:T(8,128)(2,1)S(1)} async-done(((bf16[32,88,128]{2,1,0:T(8,128)(2,1)}), bf16[32,88,128]{2,1,0:T(8,128)(2,1)S(1)}, u32[]{:S(2)}, u32[]{:S(2)}) %all-to-all-start.2) | async-done | bytes 720928 | tf_op jit(solution)/shard_map/all_to_all | solution.py:31
  81.6 0.1 fusion.3
  81.7 0.1 pad_maximum_fusion
  81.8 0.1 slice_reduce_fusion
  81.8 0.1 reshape.68.r_ref
  82.0 0.1 reshape_squeeze.3.n_ref
  82.1 3.1 %attend.2 = bf16[64,256]{1,0:T(8,128)(2,1)S(1)} custom-call(bf16[64,256]{1,0:T(8,128)(2,1)S(1)} %collective-permute-done.4.t_ref, bf16[32,88,128]{2,1,0:T(8,128)(2,1)S(1)} %all-to-all-done.2.b_ref, bf16[1344,64]{1,0:T(8,128)(2,1)S(1)} %reshape.68.r_ref, bf16[64,64]{1,0:T(8,128)(2,1)S(1)} %reshape_squeeze.3.n_ref), custom_call_target="tpu_custom_call" | custom-call | flops 2500000000 | bytes 1200000 | tf_op jit(solution)/shard_map/attend/pallas_call | solution.py:333
  85.1 0.7 collective-permute-start.5
  85.9 3.0 %attend.3 = f32[64,256]{1,0:T(8,128)S(1)} custom-call(bf16[64,256]{1,0:T(8,128)(2,1)S(1)} %reshape.67.t_ref, bf16[32,88,128]{2,1,0:T(8,128)(2,1)S(1)} %all-to-all-done.2.b_ref, bf16[1344,64]{1,0:T(8,128)(2,1)S(1)} %reshape.68.r_ref, bf16[64,64]{1,0:T(8,128)(2,1)S(1)} %reshape_squeeze.3.n_ref), custom_call_target="tpu_custom_call" | custom-call | flops 2500000000 | bytes 1200000 | tf_op jit(solution)/shard_map/attend/pallas_call | solution.py:333
  88.9 0.4 collective-permute-done.5
  89.3 0.7 fusion
  (6 shorter events, 0.0 us)
Async XLA Ops:
  4.7 2.9 %collective-permute-start = (bf16[16,24,1536]{2,1,0:T(8,128)(2,1)S(1)}, bf16[16,24,1536]{2,1,0:T(8,128)(2,1)S(1)}, u32[]{:S(2)}, u32[]{:S(2)}) collective-permute-start(bf16[16,24,1536]{2,1,0:T(8,128)(2,1)S(1)} %get-tuple-element.17), channel_id=1, source_target_pairs={{0,64},{64,0},{1,65},{65,1},{2,66},{66,2},{3,67},{67,3},{4,68},{68... | collective-permute-start | bytes 3538952 | tf_op jit(solution)/shard_map/ppermute | solution.py:355
  51.4 4.5 %collective-permute-start.1 = (bf16[32,128]{1,0:T(8,128)(2,1)S(1)}, bf16[32,128]{1,0:T(8,128)(2,1)S(1)}, u32[]{:S(2)}, u32[]{:S(2)}) collective-permute-start(bf16[32,128]{1,0:T(8,128)(2,1)S(1)} %get-tuple-element.35), channel_id=1, source_target_pairs={{0,1},{1,2},{2,3},{3,0},{4,5},{5,6},{6,7},{7,4},{8,9},{9,10},{10,1... | collective-permute-start | bytes 24584 | tf_op jit(solution)/shard_map/ppermute | solution.py:360
  52.5 5.2 %collective-permute-start.2 = (bf16[32,128]{1,0:T(8,128)(2,1)S(1)}, bf16[32,128]{1,0:T(8,128)(2,1)S(1)}, u32[]{:S(2)}, u32[]{:S(2)}) collective-permute-start(bf16[32,128]{1,0:T(8,128)(2,1)S(1)} %get-tuple-element.34), channel_id=1, source_target_pairs={{0,2},{1,3},{2,0},{3,1},{4,6},{5,7},{6,4},{7,5},{8,10},{9,11},{10,... | collective-permute-start | bytes 24584 | tf_op jit(solution)/shard_map/ppermute | solution.py:360
  55.1 3.7 %collective-permute-start.3 = (bf16[32,128]{1,0:T(8,128)(2,1)S(1)}, bf16[32,128]{1,0:T(8,128)(2,1)S(1)}, u32[]{:S(2)}, u32[]{:S(2)}) collective-permute-start(bf16[32,128]{1,0:T(8,128)(2,1)S(1)} %get-tuple-element.33), channel_id=1, source_target_pairs={{0,3},{1,0},{2,1},{3,2},{4,7},{5,4},{6,5},{7,6},{8,11},{9,8},{10,9... | collective-permute-start | bytes 24584 | tf_op jit(solution)/shard_map/ppermute | solution.py:360
  55.8 9.6 %copy-start = (f32[1,64,256]{2,1,0:T(8,128)S(1)}, f32[1,64,256]{2,1,0:T(8,128)}, u32[]{:S(2)}) copy-start(f32[1,64,256]{2,1,0:T(8,128)} %param.12) | copy-start | bytes 196612
  59.7 21.9 %all-to-all-start.2 = ((bf16[32,88,128]{2,1,0:T(8,128)(2,1)}), bf16[32,88,128]{2,1,0:T(8,128)(2,1)S(1)}, u32[]{:S(2)}, u32[]{:S(2)}) async-start(bf16[32,88,128]{2,1,0:T(8,128)(2,1)} %spread.1), calls=%async_computation.2 | async-start | bytes 1441792 | tf_op jit(solution)/shard_map/all_to_all | solution.py:31
  66.2 15.9 %collective-permute-start.4 = (bf16[64,256]{1,0:T(8,128)(2,1)S(1)}, bf16[64,256]{1,0:T(8,128)(2,1)S(1)}, u32[]{:S(2)}, u32[]{:S(2)}) collective-permute-start(bf16[64,256]{1,0:T(8,128)(2,1)S(1)} %reshape.67.t_ref), channel_id=1, source_target_pairs={{0,32},{32,0},{1,33},{33,1},{2,34},{34,2},{3,35},{35,3},{4,36},{36... | collective-permute-start | bytes 98312 | tf_op jit(solution)/shard_map/ppermute | solution.py:368
  85.1 4.2 %collective-permute-start.5 = (bf16[64,256]{1,0:T(8,128)(2,1)S(1)}, bf16[64,256]{1,0:T(8,128)(2,1)S(1)}, u32[]{:S(2)}, u32[]{:S(2)}) collective-permute-start(bf16[64,256]{1,0:T(8,128)(2,1)S(1)} %attend.2), channel_id=1, source_target_pairs={{0,32},{32,0},{1,33},{33,1},{2,34},{34,2},{3,35},{35,3},{4,36},{36... | collective-permute-start | bytes 98312 | tf_op jit(solution)/shard_map/ppermute | solution.py:373
